TPU v7x, 32 devices: a whole 2x2x4 slice. The times are simulated.
32 devices in a mesh: seg: 8 (over z, y), blk: 4 (over x, core).
Axes of the slice: x: 2, y: 2, z: 4, core: 2. Of those that a mesh axis runs over, the one named last changes fastest.
Arguments:
- strain_rate: bfloat16 [2048, 16384], P('blk', 'seg'), may hold values from -1000 to 1000
- fir_taps: float32 [64], replicated, may hold values from -0.75 to 0.75
Outputs:
- correlation: float32 [2048, 2048, 128], P('blk', 'seg')
All inputs are finite; a program needn't handle non-finite values.
Results may differ from a plain program's by a relative error of at most 0.0023.
Values may be sent and summed in bfloat16 or wider, within the bound.
No kernel may reach another device: no remote copies, remote signals or barrier semaphores. Data moves between devices by JAX's collectives and lax.ppermute only.
A program may use at most 256 MiB of HBM per device.

v0:
```python
import math

import jax
import jax.numpy as jnp
from jax import lax
from jax.sharding import PartitionSpec as P

NFFT = 1024
NBIN = 128
FLO = 8
LAGS = 128
TAPS = 64
RAMW = 32
S_DEV = 2


epsilon = 1e-06


def with_halo(cells, sides, width):
    for axis, dim in sides:
        count = lax.axis_size(axis)
        ends = count - 1
        head = lax.slice_in_dim(cells, 0, width, axis=dim)
        tail = lax.slice_in_dim(cells, cells.shape[dim] - width, cells.shape[dim], axis=dim)
        cells = jnp.concatenate(
            [
                lax.ppermute(tail, axis, [(i, (i + 1) % count) for i in range(ends)]),
                cells,
                lax.ppermute(head, axis, [((i + 1) % count, i) for i in range(ends)]),
            ],
            axis=dim,
        )
    return cells


def broadcast(shard, axis, root):
    mine = lax.axis_index(axis) == root
    return lax.psum(jnp.where(mine, shard, jnp.zeros_like(shard)), axis)


def normalize(extended):
    window_len = 2 * RAMW + 1
    magnitude = jnp.abs(extended)
    running = lax.reduce_window(
        magnitude, jnp.zeros((), extended.dtype), lax.add, (1, window_len), (1, 1), "VALID"
    )
    return extended[:, RAMW : extended.shape[1] - RAMW] / (running / window_len + epsilon)


def band_matrix(fir_taps):
    rows_len = NFFT + TAPS
    padded = jnp.concatenate([fir_taps, jnp.zeros((rows_len + 2 - TAPS,), fir_taps.dtype)])
    tiled = jnp.tile(padded, NFFT // 2)[: NFFT // 2 * rows_len]
    return tiled.reshape(NFFT // 2, rows_len).T


def filter_blocks(normed, fir_taps):
    channels = normed.shape[0]
    groups = (normed.shape[1] - TAPS) // NFFT
    leading = normed[:, : groups * NFFT].reshape(channels, groups, NFFT)
    trailing = jnp.concatenate([leading[:, 1:, :TAPS], normed[:, None, groups * NFFT :]], axis=1)
    framed = jnp.concatenate([leading, trailing], axis=2)
    return jnp.einsum("cgw,wu->cgu", framed, band_matrix(fir_taps), precision=lax.Precision.HIGHEST)


def dft_table():
    sample_index = jnp.arange(NFFT, dtype=jnp.int32)[:, None]
    freq_index = jnp.arange(NBIN, dtype=jnp.int32)[None, :] + FLO
    phase_arg = (sample_index * freq_index % NFFT).astype(jnp.float32) * (2 * math.pi / NFFT)
    norm_scale = 1.0 / math.sqrt(NFFT)
    stacked = jnp.stack([jnp.cos(phase_arg) * norm_scale, -jnp.sin(phase_arg) * norm_scale], axis=2)
    return stacked.reshape(NFFT, 2 * NBIN)


def lag_table():
    freq_index = jnp.arange(NBIN, dtype=jnp.int32)[:, None] + FLO
    lag_index = jnp.arange(LAGS, dtype=jnp.int32)[None, :]
    phase_arg = (freq_index * lag_index % NFFT).astype(jnp.float32) * (2 * math.pi / NFFT)
    return jnp.cos(phase_arg)


def shards(strain_rate, fir_taps):
    channels, own_time = strain_rate.shape
    margin = RAMW + TAPS // 2
    reach_len = NFFT + margin
    widened = with_halo(strain_rate, (("seg", 1),), reach_len)
    extended = widened[:, reach_len - margin :].astype(jnp.float32)
    halves = filter_blocks(normalize(extended), fir_taps)
    dft_cols = dft_table()
    early_half = jnp.einsum(
        "csh,hk->ksc", halves[:, :-1], dft_cols[: NFFT // 2], precision=lax.Precision.HIGHEST
    )
    late_half = jnp.einsum(
        "csh,hk->ksc", halves[:, 1:], dft_cols[NFFT // 2 :], precision=lax.Precision.HIGHEST
    )
    spectra = (early_half + late_half).astype(jnp.bfloat16).reshape(NBIN, 2, S_DEV, channels)
    segs_total = S_DEV * lax.axis_size("seg")
    lag_cos = lag_table()
    gathered = lax.all_gather(spectra, "seg", axis=2, tiled=True)
    part_width = channels * lax.axis_size("blk") // lax.axis_size("seg")
    first_col = lax.axis_index("seg") * part_width
    source_block = broadcast(gathered, "blk", first_col // channels)
    partner = lax.dynamic_slice_in_dim(source_block, first_col % channels, part_width, 3)
    cross_spec = (
        jnp.einsum("fpsi,fpsj->fij", gathered, partner, preferred_element_type=jnp.float32)
        / segs_total
    )
    correlation = (
        jnp.einsum("fij,fl->ijl", cross_spec, lag_cos, precision=lax.Precision.HIGHEST) / NBIN
    )
    return correlation


def solution(mesh):
    return jax.shard_map(
        shards,
        mesh=mesh,
        in_specs=(P("blk", "seg"), P()),
        out_specs=P("blk", "seg", None),
        check_vma=False,
    )
```

profile of v0, /device:TPU:3, one launch (start us, length us, event | category | flops | bytes accessed | tf_op | source)
XLA Modules:
  0.0 575.9 jit_solution(5507240948475038173)
XLA Ops:
  6.5 2.9 copy.27
  10.9 3.3 collective-permute-start
  15.6 2.1 cosine_multiply_fusion
  18.7 2.0 copy.26
  20.7 2.2 reshape.133
  22.9 2.0 copy.31
  24.9 2.2 reshape.134
  28.7 4.5 tile.10
  33.2 3.1 slice.64
  36.3 3.4 reshape.130
  39.7 21.9 %collective-permute-done = bf16[512,1088]{0,1:T(8,128)(2,1)S(1)} collective-permute-done((bf16[512,1088]{0,1:T(8,128)(2,1)}, bf16[512,1088]{0,1:T(8,128)(2,1)S(1)}, u32[]{:S(2)}, u32[]{:S(2)}) %collective-permute-start) | collective-permute-done | bytes 1114144 | tf_op jit(solution)/shard_map/ppermute | solution.py:28
  61.6 5.0 fusion.56
  66.6 120.4 %reduce_window.7 = f32[512,3136]{0,1:T(8,128)} reduce-window(f32[512,3200]{0,1:T(8,128)} %fusion.56, f32[]{:T(128)} %constant.69.clone.1), window={size=1x65}, to_apply=%region_0.0 | reduce-window | flops 102760448 | bytes 12976132 | tf_op jit(solution)/shard_map/reduce_window | solution.py:45
  187.0 2.3 fusion.11
  190.2 4.4 slice_divide_fusion
  195.5 3.6 slice.61
  199.2 24.3 %fusion.4 = f32[512,3,512]{2,0,1:T(8,128)S(1)} fusion(f32[512,1,64]{0,2,1:T(8,128)S(1)} %slice_bitcast_fusion, f32[512,2,64]{0,2,1:T(8,128)S(1)} %slice.62, f32[512,3,1024]{0,2,1:T(8,128)S(1)} %bitcast.25, f32[512,1088]{1,0:T(8,128)S(1)} %copy-done.1), kind=kOutput, calls=%fused_computation.4 | convolution fusion | flops 10270998528 | bytes 12058624 | tf_op jit(solution)/shard_map/cgw,wu->cgu/dot_general | solution.py:64
  223.5 1.9 fusion.13
  225.5 1.9 fusion.24
  228.6 75.3 %all-gather.2.cloned.1.call-done = bf16[128,2,16,512]{3,0,1,2:T(8,128)(2,1)} async-done(((bf16[128,2,2,512]{3,0,1,2:T(8,128)(2,1)}), bf16[128,2,16,512]{3,0,1,2:T(8,128)(2,1)}) %all-gather.2.cloned.1.call-update) | async-done | bytes 4194320 | tf_op jit(solution)/shard_map/all_gather | solution.py:100
  303.9 6.6 %broadcast_select_fusion = bf16[128,2,16,512]{3,2,1,0:T(8,128)(2,1)} fusion(pred[]{:T(512)S(6)} %eq.9, bf16[128,2,16,512]{3,0,1,2:T(8,128)(2,1)} %all-gather.2.cloned.1.call-done), kind=kLoop, calls=%fused_computation.11 | loop fusion | flops 2097152 | bytes 8388609 | tf_op jit(solution)/shard_map/jit(_where)/select_n | solution.py:39
  310.6 84.3 %all-reduce.3.cloned.1.call-done = bf16[128,2,16,512]{3,2,1,0:T(8,128)(2,1)} async-done(((bf16[128,2,16,512]{3,2,1,0:T(8,128)(2,1)}), bf16[128,2,16,512]{3,2,1,0:T(8,128)(2,1)}) %all-reduce.3.cloned.1.call-update) | async-done | bytes 4194320 | tf_op jit(solution)/shard_map/psum | solution.py:39
  394.8 25.8 %bitcast_multiply_fusion = f32[128,512,256]{2,1,0:T(8,128)} fusion(bf16[128,2,16,512]{3,0,1,2:T(8,128)(2,1)} %all-gather.2.cloned.1.call-done, bf16[128,2,16,512]{3,2,1,0:T(8,128)(2,1)} %all-reduce.3.cloned.1.call-done, s32[]{:T(128)S(6)} %select_n.52), kind=kOutput, calls=%fused_computation | convolution fusion | flops 1090519040 | bytes 73400320 | tf_op jit(solution)/shard_map/fpsi,fpsj->fij/dot_general | solution.py:106
  420.7 148.2 %broadcast_multiply_fusion = f32[512,256,128]{2,1,0:T(8,128)} fusion(f32[128,512,256]{2,1,0:T(8,128)} %bitcast_multiply_fusion, s32[128]{0:T(128)S(1)} %iota_add_fusion), kind=kOutput, calls=%fused_computation.3 | convolution fusion | flops 25786810368 | bytes 134218240 | tf_op jit(solution)/shard_map/fij,fl->ijl/dot_general | solution.py:110
  (25 shorter events, 8.3 us)
Async XLA Ops:
  6.5 297.4 %all-gather.2.cloned.1.call-start = ((), (), s32[]{:S(2)}) async-start(), calls=%async_computation | async-start | bytes 4718592 | tf_op jit(solution)/shard_map/all_gather | solution.py:100
  10.9 16.3 %copy-start.4 = (f32[64]{0:T(128)S(1)}, f32[64]{0:T(128)}, u32[]{:S(2)}) copy-start(f32[64]{0:T(128)} %param.3) | copy-start | bytes 772
  10.9 50.7 %collective-permute-start = (bf16[512,1088]{0,1:T(8,128)(2,1)}, bf16[512,1088]{0,1:T(8,128)(2,1)S(1)}, u32[]{:S(2)}, u32[]{:S(2)}) collective-permute-start(bf16[512,1088]{0,1:T(8,128)(2,1)} %get-tuple-element.5), channel_id=1, source_target_pairs={{0,4},{4,8},{8,12},{12,16},{16,20},{20,24},{24,28},{1,5},{5,9},{9,... | collective-permute-start | bytes 3342344 | tf_op jit(solution)/shard_map/ppermute | solution.py:28
  14.2 47.3 %collective-permute-start.1 = (bf16[512,1088]{0,1:T(8,128)(2,1)}, bf16[512,1088]{0,1:T(8,128)(2,1)}, u32[]{:S(2)}, u32[]{:S(2)}) collective-permute-start(bf16[512,1088]{0,1:T(8,128)(2,1)} %get-tuple-element.6), channel_id=1, source_target_pairs={{4,0},{8,4},{12,8},{16,12},{20,16},{24,20},{28,24},{5,1},{9,5},{13... | collective-permute-start | bytes 3342344 | tf_op jit(solution)/shard_map/ppermute | solution.py:30
  187.0 3.2 copy-start
  195.4 3.7 copy-start.1
  199.1 24.4 %copy-start.2 = (f32[512,256,1]{0,1,2:T(8,128)S(1)}, f32[512,256,1]{0,1,2:T(8,128)}, u32[]{:S(2)}) copy-start(f32[512,256,1]{0,1,2:T(8,128)} %reshape.134) | copy-start | bytes 1572868
  199.2 26.3 %copy-start.3 = (f32[512,256,1]{0,1,2:T(8,128)S(1)}, f32[512,256,1]{0,1,2:T(8,128)}, u32[]{:S(2)}) copy-start(f32[512,256,1]{0,1,2:T(8,128)} %reshape.133) | copy-start | bytes 1572868
  228.5 166.3 %all-reduce.3.cloned.1.call-start = ((), (), s32[]{:S(2)}) async-start(), calls=%async_computation.1 | async-start | bytes 8388608 | tf_op jit(solution)/shard_map/psum | solution.py:39
Sparse Core Ops, SparseCore 0:
  228.6 75.2 all-gather.1
  310.7 84.1 all-reduce.2
where the time goes:
time: 584 us; the launch traced here: 576 us
  matrix products  202 us (35%)
  waiting for transfers between devices  181 us (31%)
  other arithmetic  142 us (24%)
  local copies, waits for them, and re-layouts  31.8 us (5%)
  between operations  13.8 us (2%)
    dot_general x1, matrix products, shards(): jnp.einsum('fij,fl->ijl', cross_spec, lag_cos, precision=lax.Precision.HI...  148 us
    another operation x1, other arithmetic, normalize(): lax.reduce_window(magnitude, jnp.zeros((), extended.dtype), lax.add, (1,...  120 us
    psum x1, waiting for transfers between devices, broadcast(): return lax.psum(jnp.where(mine, shard, jnp.zeros_like(shard)), axis)  84.3 us
    all_gather x1, waiting for transfers between devices, shards(): gathered = lax.all_gather(spectra, 'seg', axis=2, tiled=True)  75.3 us
    dot_general x1, matrix products, shards(): jnp.einsum('fpsi,fpsj->fij', gathered, partner, preferred_element_type=jn...  25.8 us
    dot_general x1, matrix products, filter_blocks(): jnp.einsum('cgw,wu->cgu', framed, band_matrix(fir_taps), precision=lax.Pr...  24.3 us
    ppermute x1, waiting for transfers between devices, with_halo(): lax.ppermute(tail, axis, [(i, (i + 1) % count) for i in range(ends)])  21.9 us
  transfers between devices with their start and end apart: 4, of which 3 were waited for; matrix products, arithmetic and copies ran while one was open for 4% of the time, Pallas kernels for 0%

commit v1 on v0

v1 whole, which is shorter than its diff:
```python
import functools
import math

import jax
import jax.numpy as jnp
import numpy as np
from jax import lax
from jax.experimental import pallas as pl
from jax.experimental.pallas import tpu as pltpu
from jax.sharding import PartitionSpec as P

NFFT = 1024
NBIN = 128
FLO = 8
LAGS = 128
TAPS = 64
RAMW = 32
HALF = NFFT // 2
EPSILON = 1e-06
LANE = 128
SPEC = 2 * NBIN
REACH = 10 * LANE
LEAD = LANE - TAPS // 2
GROUP = 8
GROUPS = NBIN // GROUP

bf16 = jnp.bfloat16
f32 = jnp.float32


def split(x):
    high = x.astype(bf16)
    return high, (x - high.astype(f32)).astype(bf16)


def half_dft_table():
    sample = np.arange(HALF)[:, None]
    freq = np.arange(NBIN)[None, :] + FLO
    phase = (sample * freq % NFFT) * (2 * math.pi / NFFT)
    table = np.stack([np.cos(phase), -np.sin(phase)], axis=2).reshape(HALF, SPEC) / math.sqrt(NFFT)
    return np.pad(table, ((32, 32), (0, 0))).astype(np.float32)


def lag_table(segs_total):
    freq = np.arange(NBIN)[:, None] + FLO
    lag = np.arange(LAGS)[None, :]
    table = np.cos((freq * lag % NFFT) * (2 * math.pi / NFFT)) / (segs_total * NBIN)
    high = table.astype(np.float32).astype(bf16)
    low = (table - high.astype(np.float64)).astype(np.float32).astype(bf16)
    row = np.concatenate([high, low], axis=1)
    return np.concatenate([row, row], axis=0)


def window_table():
    gap = np.arange(4 * LANE)[:, None] - LANE - np.arange(2 * LANE)[None, :]
    return (np.abs(gap) <= RAMW).astype(np.float32).astype(bf16)


def response_kernel(taps_ref, table_ref, high_ref, low_ref):
    row = lax.broadcasted_iota(jnp.int32, (64, 64), 0)
    col = lax.broadcasted_iota(jnp.int32, (64, 64), 1)
    index = row + 64 - 2 * col
    band = jnp.zeros((64, 64), f32)
    for k in range(TAPS):
        band = jnp.where(index == k, taps_ref[k], band)
    high_ref[...] = jnp.zeros_like(high_ref)
    low_ref[...] = jnp.zeros_like(low_ref)
    for block in range(17):
        part = jnp.dot(
            band,
            table_ref[32 * block : 32 * block + 64, :],
            precision=lax.Precision.HIGHEST,
            preferred_element_type=f32,
        )
        high, low = split(part)
        start = LEAD + 64 * block
        high_ref[start : start + 64, :] = high
        low_ref[start : start + 64, :] = low


def response(fir_taps):
    return pl.pallas_call(
        response_kernel,
        in_specs=[
            pl.BlockSpec(memory_space=pltpu.SMEM),
            pl.BlockSpec(memory_space=pltpu.VMEM),
        ],
        out_specs=[pl.BlockSpec(memory_space=pltpu.VMEM)] * 2,
        out_shape=[jax.ShapeDtypeStruct((REACH, SPEC), bf16)] * 2,
        name="response",
        cost_estimate=pl.CostEstimate(flops=2 * 6 * 64 * 64 * 17 * 256, bytes_accessed=2 << 20, transcendentals=0),
    )(fir_taps, jnp.asarray(half_dft_table()))


def spectrum_kernel(own_time, last_ref, left_ref, own_ref, right_ref, window_ref, high_ref, low_ref,
                    even_ref, first_ref, second_ref, normed_ref):
    rows = own_ref.shape[0]
    tiles = own_time // LANE + 2
    zero = jnp.zeros((rows, LANE), bf16)
    extended = jnp.concatenate([zero, left_ref[...], own_ref[...], right_ref[...], zero], axis=1)
    window = window_ref[...]
    for pair in range(tiles // 2):
        start = 2 * LANE * pair
        total = jnp.dot(
            jnp.abs(extended[:, start : start + 4 * LANE]), window, preferred_element_type=f32
        )
        centre = extended[:, start + LANE : start + 3 * LANE].astype(f32)
        normed_ref[:, start : start + 2 * LANE] = centre / (total * (1.0 / (2 * RAMW + 1)) + EPSILON)

    def transform(start, length):
        high, low = split(normed_ref[:, start : start + length])
        kept = high_ref[:length, :]
        out = jnp.dot(high, kept, preferred_element_type=f32)
        out += jnp.dot(low, kept, preferred_element_type=f32)
        out += jnp.dot(high, low_ref[:length, :], preferred_element_type=f32)
        return out.T

    freq = lax.broadcasted_iota(jnp.int32, (SPEC, rows), 0) // 2
    sign = jnp.where(lax.rem(freq, 2) == 0, 1.0, -1.0)
    first = transform(0, REACH)
    second = transform(NFFT, REACH)
    tail = transform(own_time, 2 * LANE)
    first_ref[...] = first
    even_ref[...] = (first + sign * second).astype(bf16)
    second_ref[...] = second + jnp.where(last_ref[0] == 1, sign * tail, jnp.zeros_like(tail))


def spectrum(last, left, own, right, high, low):
    channels, own_time = own.shape
    rows = min(128, channels)
    line = lambda i: (i, 0)
    whole = lambda i: (0, 0)
    across = lambda i: (0, i)
    return pl.pallas_call(
        functools.partial(spectrum_kernel, own_time),
        grid=(channels // rows,),
        in_specs=[
            pl.BlockSpec(memory_space=pltpu.SMEM),
            pl.BlockSpec((rows, LANE), line),
            pl.BlockSpec((rows, own_time), line),
            pl.BlockSpec((rows, LANE), line),
            pl.BlockSpec((4 * LANE, 2 * LANE), whole),
            pl.BlockSpec((REACH, SPEC), whole),
            pl.BlockSpec((REACH, SPEC), whole),
        ],
        out_specs=[pl.BlockSpec((SPEC, rows), across)] * 3,
        out_shape=[
            jax.ShapeDtypeStruct((SPEC, channels), bf16),
            jax.ShapeDtypeStruct((SPEC, channels), f32),
            jax.ShapeDtypeStruct((SPEC, channels), f32),
        ],
        scratch_shapes=[pltpu.VMEM((rows, own_time + 2 * LANE), f32)],
        compiler_params=pltpu.CompilerParams(vmem_limit_bytes=32 << 20),
        name="spectrum",
        cost_estimate=pl.CostEstimate(
            flops=2 * channels * SPEC * REACH * 6, bytes_accessed=6 << 20, transcendentals=0
        ),
    )(last, left, own, right, jnp.asarray(window_table()), high, low)


def correlate_kernel(pieces, rows, pitch, batch, *refs):
    row_refs = refs[:pieces]
    col_ref = refs[pieces]
    table_ref, out_ref, lhs_ref, cross_ref = refs[pieces + 1 :]
    width = col_ref.shape[2]
    depth = 2 * GROUP * pieces
    sub = lax.rem(pl.program_id(0), LANE // rows)

    @pl.when(sub == 0)
    def _():
        for g in range(GROUPS):
            part = jnp.concatenate([r[16 * g : 16 * g + 16, :] for r in row_refs], axis=0)
            lhs_ref[:, g * depth : (g + 1) * depth] = part.T

    lane = lax.broadcasted_iota(jnp.int32, (rows, depth), 1)
    freq = lax.rem(lane, 2 * GROUP) // 2
    start = pl.multiple_of(sub * rows, rows)
    for g in range(GROUPS):
        cols = jnp.concatenate([col_ref[d, 16 * g : 16 * g + 16, :] for d in range(pieces)], axis=0)
        part = lhs_ref[pl.ds(start, rows), g * depth : (g + 1) * depth]
        lhs = jnp.concatenate(
            [jnp.where(freq == q, part, jnp.zeros_like(part)) for q in range(GROUP)], axis=0
        )
        cross = jnp.dot(lhs, cols, preferred_element_type=f32)
        for q in range(GROUP):
            for h in range(width // LANE):
                base = (g * GROUP + q) * pitch
                cross_ref[h, base : base + rows, :] = cross[
                    q * rows : (q + 1) * rows, h * LANE : (h + 1) * LANE
                ]
    table = table_ref[...]

    def lags(b, carry):
        highs, lows = [], []
        for ii in range(batch):
            for h in range(width // LANE):
                by_freq = cross_ref[h, pl.ds(b * batch + ii, NBIN, stride=pitch), :]
                high, low = split(by_freq.T)
                highs.append(high)
                lows.append(low)
        lhs = jnp.concatenate([jnp.concatenate(highs, axis=0), jnp.concatenate(lows, axis=0)], axis=1)
        both = jnp.dot(lhs, table, preferred_element_type=f32)
        out = both[:, :LAGS] + both[:, LAGS:]
        out_ref[pl.ds(b * batch, batch)] = out.reshape(batch, width, LAGS)
        return carry

    lax.fori_loop(0, rows // batch, lags, 0)


def correlate(row_pieces, cols, table):
    pieces = len(row_pieces)
    channels = row_pieces[0].shape[1]
    width = cols.shape[2]
    rows, batch = 64, 16
    pitch = rows + 8
    per = LANE // rows
    return pl.pallas_call(
        functools.partial(correlate_kernel, pieces, rows, pitch, batch),
        grid=(channels // rows,),
        in_specs=[pl.BlockSpec((SPEC, LANE), lambda s: (0, s // per))] * pieces
        + [
            pl.BlockSpec((pieces, SPEC, width), lambda s: (0, 0, 0)),
            pl.BlockSpec((2 * NBIN, 2 * LAGS), lambda s: (0, 0)),
        ],
        out_specs=pl.BlockSpec((rows, width, LAGS), lambda s: (s, 0, 0)),
        out_shape=jax.ShapeDtypeStruct((channels, width, LAGS), f32),
        scratch_shapes=[
            pltpu.VMEM((LANE, SPEC * pieces), bf16),
            pltpu.VMEM((width // LANE, NBIN * pitch, LANE), f32),
        ],
        compiler_params=pltpu.CompilerParams(vmem_limit_bytes=56 << 20),
        name="correlate",
        cost_estimate=pl.CostEstimate(
            flops=2 * channels * width * NBIN * (256 + 512),
            bytes_accessed=channels * width * LAGS * 4,
            transcendentals=0,
        ),
    )(*row_pieces, cols, table)


def ring_pairs(count):
    order = list(range(0, count, 2)) + list(range(count - 1, 0, -2))
    forward = [(order[i], order[(i + 1) % count]) for i in range(count)]
    return forward, [(b, a) for a, b in forward]


def shards(strain_rate, fir_taps):
    channels, own_time = strain_rate.shape
    segs, blks = lax.axis_size("seg"), lax.axis_size("blk")
    seg, blk = lax.axis_index("seg"), lax.axis_index("blk")
    left = lax.ppermute(strain_rate[:, own_time - LANE :], "seg", [(i, i + 1) for i in range(segs - 1)])
    right = lax.ppermute(strain_rate[:, :LANE], "seg", [(i + 1, i) for i in range(segs - 1)])
    high, low = response(fir_taps)
    last = (seg == segs - 1).astype(jnp.int32).reshape(1)
    even, first, second = spectrum(last, left, strain_rate, right, high, low)
    following = lax.ppermute(first, "seg", [(i + 1, i) for i in range(segs - 1)])
    freq = lax.broadcasted_iota(jnp.int32, (SPEC, 1), 0) // 2
    odd = (second + jnp.where(freq % 2 == 0, 1.0, -1.0) * following).astype(bf16)

    forward, backward = ring_pairs(segs)
    row_pieces = []
    for own, steps in ((even, (segs // 2, segs - 1 - segs // 2)), (odd, (segs - 1 - segs // 2, segs // 2))):
        row_pieces.append(own)
        for pairs, count in zip((forward, backward), steps):
            moved = own
            for _ in range(count):
                moved = lax.ppermute(moved, "seg", pairs)
                row_pieces.append(moved)

    width = channels * blks // segs
    offset = (seg * width) % channels
    cols = jnp.stack([lax.dynamic_slice_in_dim(p, offset, width, 1) for p in row_pieces])
    owner = [s * width // channels for s in range(segs)]
    held = blk == (seg * width) // channels
    below = blks
    relation = jnp.bitwise_xor(blk, (seg * width) // channels)
    while below > 1:
        below //= 2
        pairs = []
        for s in range(segs):
            for high_bits in range(0, blks, 2 * below):
                source = owner[s] ^ high_bits
                pairs.append((s * blks + source, s * blks + (source ^ below)))
        moved = lax.ppermute(cols, ("seg", "blk"), pairs)
        cols = jnp.where(held, cols, moved)
        held = relation % below == 0
    return correlate(row_pieces, cols, jnp.asarray(lag_table(2 * segs)))


def solution(mesh):
    return jax.shard_map(
        shards,
        mesh=mesh,
        in_specs=(P("blk", "seg"), P()),
        out_specs=P("blk", "seg", None),
        check_vma=False,
    )
```

time: 584 us -> 165 us (0.28); the launches traced: 576 us -> 165 us
  matrix products: 202 us -> 0 us
  other arithmetic: 142 us -> 5.1 us
  waiting for transfers between devices: 181 us -> 77.7 us
  Pallas kernels: 0 us -> 50.5 us
  local copies, waits for them, and re-layouts: 31.8 us -> 9.8 us
  starting transfers between devices: 4.67 us -> 21.3 us
  between operations: 13.8 us -> 0.34 us
    dot_general x5 -> x0, matrix products: 202 us -> none  [the longest x1 148 us: shards(): jnp.einsum('fij,fl->ijl', cross_spec, lag_cos, precision=lax.Precision.HI...]
    another operation x2 -> x0, other arithmetic: 121 us -> none  [the longest x1 120 us: normalize(): lax.reduce_window(magnitude, jnp.zeros((), extended.dtype), lax.add, (1,...]
    psum x1 -> x0, waiting for transfers between devices: 84.3 us -> none  [broadcast(): return lax.psum(jnp.where(mine, shard, jnp.zeros_like(shard)), axis)]
    all_gather x1 -> x0, waiting for transfers between devices: 75.3 us -> none  [shards(): gathered = lax.all_gather(spectra, 'seg', axis=2, tiled=True)]
    ppermute x2 -> x19, waiting for transfers between devices: 21.9 us -> 77.7 us  [the longest x14 43.7 us: shards(): moved = lax.ppermute(moved, 'seg', pairs)]
    pallas_call x0 -> x3, Pallas kernels: none -> 50.5 us  [the longest x1 42.1 us: correlate(): pl.pallas_call(functools.partial(correlate_kernel, pieces, rows, pitch, b...]
    ppermute x2 -> x19, starting transfers between devices: 4.63 us -> 21.3 us  [the longest x14 11.4 us: shards(): moved = lax.ppermute(moved, 'seg', pairs)]
    slice x8 -> x1, local copies, waits for them, and re-layouts: 16.8 us -> 0.99 us  [shards(): strain_rate[:, :LANE]]
  transfers between devices with their start and end apart: 4 -> 19, of which waited for: 3 -> 10; matrix products, arithmetic and copies ran while one was open for 4% -> 3% of each run, Pallas kernels for 0% -> 2%
where the time goes in v1:
time: 165 us
  waiting for transfers between devices  77.7 us (47%)
  Pallas kernels  50.5 us (31%)
  starting transfers between devices  21.3 us (13%)
  local copies, waits for them, and re-layouts  9.8 us (6%)
  other arithmetic  5.1 us (3%)
    ppermute x14, waiting for transfers between devices, shards(): moved = lax.ppermute(moved, 'seg', pairs)  43.7 us
    pallas_call x1, Pallas kernels, correlate(): pl.pallas_call(functools.partial(correlate_kernel, pieces, rows, pitch, b...  42.1 us
    ppermute x2, waiting for transfers between devices, shards(): moved = lax.ppermute(cols, ('seg', 'blk'), pairs)  32.6 us
    ppermute x14, starting transfers between devices, shards(): moved = lax.ppermute(moved, 'seg', pairs)  11.4 us
    unnamed x49, local copies, waits for them, and re-layouts  8.8 us
    pallas_call x1, Pallas kernels, spectrum(): pl.pallas_call(functools.partial(spectrum_kernel, own_time), grid=(channe...  5.05 us
    select_n x2, other arithmetic, shards(): cols = jnp.where(held, cols, moved)  4.99 us
    ppermute x1, starting transfers between devices, shards(): lax.ppermute(strain_rate[:, own_time - LANE:], 'seg', [(i, i + 1) for i i...  3.99 us
  transfers between devices with their start and end apart: 19, of which 10 were waited for; matrix products, arithmetic and copies ran while one was open for 3% of the time, Pallas kernels for 2%

profile of v1, /device:TPU:3, one launch (start us, length us, event | category | flops | bytes accessed | tf_op | source)
XLA Modules:
  0.0 164.7 jit_solution(6208560142106755428)
XLA Ops:
  1.0 1.3 collective-permute-start.1
  2.3 4.0 %collective-permute-start = (bf16[512,128]{1,0:T(8,128)(2,1)S(1)}, bf16[512,128]{1,0:T(8,128)(2,1)S(1)}, u32[]{:S(2)}, u32[]{:S(2)}) collective-permute-start(bf16[512,128]{1,0:T(8,128)(2,1)S(1)} %get-tuple-element.16), channel_id=1, source_target_pairs={{0,4},{4,8},{8,12},{12,16},{16,20},{20,24},{24,28},{1,5},{5,9},{9,... | collective-permute-start | bytes 393224 | tf_op jit(solution)/shard_map/ppermute | solution.py:251
  6.3 3.3 %response.1 = (bf16[1280,256]{1,0:T(8,128)(2,1)}, bf16[1280,256]{1,0:T(8,128)(2,1)}) custom-call(f32[64]{0:T(128)} %taps_ref.1, f32[576,256]{1,0:T(8,128)} %constant.82.clone.table_ref), custom_call_target="tpu_custom_call" | custom-call | flops 213909504 | bytes 2097152 | tf_op jit(solution)/shard_map/response/pallas_call | solution.py:82
  9.6 1.4 collective-permute-done.left_ref
  11.1 1.6 copy-done.1
  15.8 5.0 %spectrum.1 = (bf16[256,512]{1,0:T(8,128)(2,1)S(1)}, f32[256,512]{1,0:T(8,128)S(1)}, f32[256,512]{1,0:T(8,128)S(1)}) custom-call(s32[1]{0:T(128)} %bitcast.last_ref, bf16[512,128]{1,0:T(8,128)(2,1)S(1)} %collective-permute-done.left_ref, bf16[512,2048]{1,0:T(8,128)(2,1)S(1)} %copy-done.1, bf16[512,128]{1,0:T(8,128)(2,1)S(1)} %collective-permute-done.1.right_ref, ...), custom_call_target="tpu_custom_call" | custom-call | flops 2013265920 | bytes 6291456 | tf_op jit(solution)/shard_map/spectrum/pallas_call | solution.py:134
  20.8 1.3 collective-permute-start.2
  23.4 5.9 %collective-permute-done.2.refs_1_ = bf16[256,512]{1,0:T(8,128)(2,1)S(1)} collective-permute-done((bf16[256,512]{1,0:T(8,128)(2,1)S(1)}, bf16[256,512]{1,0:T(8,128)(2,1)S(1)}, u32[]{:S(2)}, u32[]{:S(2)}) %collective-permute-start.2) | collective-permute-done | bytes 262176 | tf_op jit(solution)/shard_map/ppermute | solution.py:267
  29.4 1.5 collective-permute-start.6
  30.8 15.4 %collective-permute-done.3.refs_2_ = bf16[256,512]{1,0:T(8,128)(2,1)S(1)} collective-permute-done((bf16[256,512]{1,0:T(8,128)(2,1)S(1)}, bf16[256,512]{1,0:T(8,128)(2,1)S(1)}, u32[]{:S(2)}, u32[]{:S(2)}) %collective-permute-start.3) | collective-permute-done | bytes 262176 | tf_op jit(solution)/shard_map/ppermute | solution.py:267
  46.3 1.5 collective-permute-start.13
  47.9 1.5 collective-permute-start.7
  49.3 3.8 %collective-permute-done.4.refs_3_ = bf16[256,512]{1,0:T(8,128)(2,1)} collective-permute-done((bf16[256,512]{1,0:T(8,128)(2,1)S(1)}, bf16[256,512]{1,0:T(8,128)(2,1)}, u32[]{:S(2)}, u32[]{:S(2)}) %collective-permute-start.4) | collective-permute-done | bytes 262176 | tf_op jit(solution)/shard_map/ppermute | solution.py:267
  54.6 4.1 %collective-permute-done.10.refs_9_ = bf16[256,512]{1,0:T(8,128)(2,1)} collective-permute-done((bf16[256,512]{1,0:T(8,128)(2,1)S(1)}, bf16[256,512]{1,0:T(8,128)(2,1)}, u32[]{:S(2)}, u32[]{:S(2)}) %collective-permute-start.10) | collective-permute-done | bytes 262176 | tf_op jit(solution)/shard_map/ppermute | solution.py:267
  61.2 3.2 %collective-permute-done.14.refs_13_ = bf16[256,512]{1,0:T(8,128)(2,1)S(1)} collective-permute-done((bf16[256,512]{1,0:T(8,128)(2,1)}, bf16[256,512]{1,0:T(8,128)(2,1)S(1)}, u32[]{:S(2)}, u32[]{:S(2)}) %collective-permute-start.14) | collective-permute-done | bytes 262176 | tf_op jit(solution)/shard_map/ppermute | solution.py:267
  65.6 4.3 %collective-permute-done.11.refs_10_ = bf16[256,512]{1,0:T(8,128)(2,1)S(1)} collective-permute-done((bf16[256,512]{1,0:T(8,128)(2,1)}, bf16[256,512]{1,0:T(8,128)(2,1)S(1)}, u32[]{:S(2)}, u32[]{:S(2)}) %collective-permute-start.11) | collective-permute-done | bytes 262176 | tf_op jit(solution)/shard_map/ppermute | solution.py:267
  72.3 3.4 %collective-permute-done.15.refs_14_ = bf16[256,512]{1,0:T(8,128)(2,1)S(1)} collective-permute-done((bf16[256,512]{1,0:T(8,128)(2,1)S(1)}, bf16[256,512]{1,0:T(8,128)(2,1)S(1)}, u32[]{:S(2)}, u32[]{:S(2)}) %collective-permute-start.15) | collective-permute-done | bytes 262176 | tf_op jit(solution)/shard_map/ppermute | solution.py:267
  77.9 3.6 %collective-permute-done.16.refs_15_ = bf16[256,512]{1,0:T(8,128)(2,1)S(1)} collective-permute-done((bf16[256,512]{1,0:T(8,128)(2,1)S(1)}, bf16[256,512]{1,0:T(8,128)(2,1)S(1)}, u32[]{:S(2)}, u32[]{:S(2)}) %collective-permute-start.16) | collective-permute-done | bytes 262176 | tf_op jit(solution)/shard_map/ppermute | solution.py:267
  81.7 2.0 %collective-permute-start.17 = (bf16[16,256,256]{2,1,0:T(8,128)(2,1)S(1)}, bf16[16,256,256]{2,1,0:T(8,128)(2,1)}, u32[]{:S(2)}, u32[]{:S(2)}) collective-permute-start(bf16[16,256,256]{2,1,0:T(8,128)(2,1)S(1)} %bitcast_dynamic-update-slice_fusion), channel_id=1, source_target_pairs={{0,2},{4,6},{9,11},{13,15},{18,16},{22,20},{27,25},{31,29}} | collective-permute-start | bytes 6291464 | tf_op jit(solution)/shard_map/ppermute | solution.py:284
  83.7 1.8 %broadcast_select_fusion = bf16[16,256,256]{2,1,0:T(8,128)(2,1)S(1)} fusion(bf16[16,256,256]{2,1,0:T(8,128)(2,1)} %copy-done.5, bf16[16,256,256]{2,1,0:T(8,128)(2,1)} %collective-permute-done.17, pred[]{:T(512)S(6)} %eq.26), kind=kLoop, calls=%fused_computation | loop fusion | flops 1048576 | bytes 6291457 | tf_op jit(solution)/shard_map/jit(_where)/select_n | solution.py:285
  85.5 1.3 collective-permute-start.18
  86.9 32.6 %collective-permute-done.18 = bf16[16,256,256]{2,1,0:T(8,128)(2,1)} collective-permute-done((bf16[16,256,256]{2,1,0:T(8,128)(2,1)S(1)}, bf16[16,256,256]{2,1,0:T(8,128)(2,1)}, u32[]{:S(2)}, u32[]{:S(2)}) %collective-permute-start.18) | collective-permute-done | bytes 2097184 | tf_op jit(solution)/shard_map/ppermute | solution.py:284
  119.4 3.2 %broadcast_select_fusion.1.refs_16_ = bf16[16,256,256]{2,1,0:T(8,128)(2,1)} fusion(bf16[16,256,256]{2,1,0:T(8,128)(2,1)S(1)} %broadcast_select_fusion, bf16[16,256,256]{2,1,0:T(8,128)(2,1)} %collective-permute-done.18, pred[]{:T(512)S(6)} %eq.25), kind=kLoop, calls=%fused_computation.1 | loop fusion | flops 1048576 | bytes 6291457 | tf_op jit(solution)/shard_map/jit(_where)/select_n | solution.py:285
  122.6 42.1 %correlate.1 = f32[512,256,128]{2,1,0:T(8,128)} custom-call(bf16[256,512]{1,0:T(8,128)(2,1)} %copy-done, bf16[256,512]{1,0:T(8,128)(2,1)} %copy-done.7, bf16[256,512]{1,0:T(8,128)(2,1)} %copy-done.8, bf16[256,512]{1,0:T(8,128)(2,1)} %collective-permute-done.4.refs_3_, bf16[256,512]{1,0:T(8,128)(2,1)} %copy-done.10, bf16[256,512]{1,0:T(8,128)(2,1)} %copy-done.9, ...), custom_call_target="tpu_custom_call" | custom-call | flops 25769803776 | bytes 67108864 | tf_op jit(solution)/shard_map/correlate/pallas_call | solution.py:217
  (72 shorter events, 15.3 us)
Async XLA Ops:
  1.0 8.6 %collective-permute-start.1 = (bf16[512,128]{1,0:T(8,128)(2,1)S(1)}, bf16[512,128]{1,0:T(8,128)(2,1)S(1)}, u32[]{:S(2)}, u32[]{:S(2)}) collective-permute-start(bf16[512,128]{1,0:T(8,128)(2,1)S(1)} %get-tuple-element.15), channel_id=1, source_target_pairs={{4,0},{8,4},{12,8},{16,12},{20,16},{24,20},{28,24},{5,1},{9,5},{13... | collective-permute-start | bytes 393224 | tf_op jit(solution)/shard_map/ppermute | solution.py:252
  2.3 8.8 %collective-permute-start = (bf16[512,128]{1,0:T(8,128)(2,1)S(1)}, bf16[512,128]{1,0:T(8,128)(2,1)S(1)}, u32[]{:S(2)}, u32[]{:S(2)}) collective-permute-start(bf16[512,128]{1,0:T(8,128)(2,1)S(1)} %get-tuple-element.16), channel_id=1, source_target_pairs={{0,4},{4,8},{8,12},{12,16},{16,20},{20,24},{24,28},{1,5},{5,9},{9,... | collective-permute-start | bytes 393224 | tf_op jit(solution)/shard_map/ppermute | solution.py:251
  20.8 51.5 %copy-start = (bf16[256,512]{1,0:T(8,128)(2,1)}, bf16[256,512]{1,0:T(8,128)(2,1)S(1)}, u32[]{:S(2)}) copy-start(bf16[256,512]{1,0:T(8,128)(2,1)S(1)} %get-tuple-element.12.refs_0_) | copy-start | bytes 786436
  20.8 8.5 %collective-permute-start.2 = (bf16[256,512]{1,0:T(8,128)(2,1)S(1)}, bf16[256,512]{1,0:T(8,128)(2,1)S(1)}, u32[]{:S(2)}, u32[]{:S(2)}) collective-permute-start(bf16[256,512]{1,0:T(8,128)(2,1)S(1)} %get-tuple-element.12.refs_0_), channel_id=1, source_target_pairs={{0,8},{8,16},{16,24},{24,28},{28,20},{20,12},{12,4},{4,0},{1,9},{9... | collective-permute-start | bytes 786440 | tf_op jit(solution)/shard_map/ppermute | solution.py:267
  22.2 24.1 %collective-permute-start.9 = (f32[256,512]{1,0:T(8,128)S(1)}, f32[256,512]{1,0:T(8,128)S(1)}, u32[]{:S(2)}, u32[]{:S(2)}) collective-permute-start(f32[256,512]{1,0:T(8,128)S(1)} %get-tuple-element.14), channel_id=1, source_target_pairs={{4,0},{8,4},{12,8},{16,12},{20,16},{24,20},{28,24},{5,1},{9,5},{13... | collective-permute-start | bytes 1572872 | tf_op jit(solution)/shard_map/ppermute | solution.py:256
  29.4 42.9 %copy-start.7 = (bf16[256,512]{1,0:T(8,128)(2,1)}, bf16[256,512]{1,0:T(8,128)(2,1)S(1)}, u32[]{:S(2)}) copy-start(bf16[256,512]{1,0:T(8,128)(2,1)S(1)} %collective-permute-done.2.refs_1_) | copy-start | bytes 786436
  29.4 16.9 %collective-permute-start.3 = (bf16[256,512]{1,0:T(8,128)(2,1)S(1)}, bf16[256,512]{1,0:T(8,128)(2,1)S(1)}, u32[]{:S(2)}, u32[]{:S(2)}) collective-permute-start(bf16[256,512]{1,0:T(8,128)(2,1)S(1)} %collective-permute-done.2.refs_1_), channel_id=1, source_target_pairs={{0,8},{8,16},{16,24},{24,28},{28,20},{20,12},{12,4},{4,0},{1,9},{9... | collective-permute-start | bytes 786440 | tf_op jit(solution)/shard_map/ppermute | solution.py:267
  29.4 18.5 %collective-permute-start.6 = (bf16[256,512]{1,0:T(8,128)(2,1)S(1)}, bf16[256,512]{1,0:T(8,128)(2,1)S(1)}, u32[]{:S(2)}, u32[]{:S(2)}) collective-permute-start(bf16[256,512]{1,0:T(8,128)(2,1)S(1)} %get-tuple-element.12.refs_0_), channel_id=1, source_target_pairs={{8,0},{16,8},{24,16},{28,24},{20,28},{12,20},{4,12},{0,4},{9,1},{1... | collective-permute-start | bytes 786440 | tf_op jit(solution)/shard_map/ppermute | solution.py:267
  46.2 26.1 %copy-start.8 = (bf16[256,512]{1,0:T(8,128)(2,1)}, bf16[256,512]{1,0:T(8,128)(2,1)S(1)}, u32[]{:S(2)}) copy-start(bf16[256,512]{1,0:T(8,128)(2,1)S(1)} %collective-permute-done.3.refs_2_) | copy-start | bytes 786436
  46.2 6.9 %collective-permute-start.4 = (bf16[256,512]{1,0:T(8,128)(2,1)S(1)}, bf16[256,512]{1,0:T(8,128)(2,1)}, u32[]{:S(2)}, u32[]{:S(2)}) collective-permute-start(bf16[256,512]{1,0:T(8,128)(2,1)S(1)} %collective-permute-done.3.refs_2_), channel_id=1, source_target_pairs={{0,8},{8,16},{16,24},{24,28},{28,20},{20,12},{12,4},{4,0},{1,9},{9... | collective-permute-start | bytes 786440 | tf_op jit(solution)/shard_map/ppermute | solution.py:267
  46.3 35.2 %copy-start.6 = (bf16[256,512]{1,0:T(8,128)(2,1)}, bf16[256,512]{1,0:T(8,128)(2,1)S(1)}, u32[]{:S(2)}) copy-start(bf16[256,512]{1,0:T(8,128)(2,1)S(1)} %add_convert_fusion.refs_8_) | copy-start | bytes 786436
  46.3 7.1 %collective-permute-start.13 = (bf16[256,512]{1,0:T(8,128)(2,1)S(1)}, bf16[256,512]{1,0:T(8,128)(2,1)}, u32[]{:S(2)}, u32[]{:S(2)}) collective-permute-start(bf16[256,512]{1,0:T(8,128)(2,1)S(1)} %add_convert_fusion.refs_8_), channel_id=1, source_target_pairs={{8,0},{16,8},{24,16},{28,24},{20,28},{12,20},{4,12},{0,4},{9,1},{1... | collective-permute-start | bytes 786440 | tf_op jit(solution)/shard_map/ppermute | solution.py:267
  47.9 10.9 %collective-permute-start.10 = (bf16[256,512]{1,0:T(8,128)(2,1)S(1)}, bf16[256,512]{1,0:T(8,128)(2,1)}, u32[]{:S(2)}, u32[]{:S(2)}) collective-permute-start(bf16[256,512]{1,0:T(8,128)(2,1)S(1)} %add_convert_fusion.refs_8_), channel_id=1, source_target_pairs={{0,8},{8,16},{16,24},{24,28},{28,20},{20,12},{12,4},{4,0},{1,9},{9... | collective-permute-start | bytes 786440 | tf_op jit(solution)/shard_map/ppermute | solution.py:267
  47.9 33.7 %copy-start.9 = (bf16[256,512]{1,0:T(8,128)(2,1)}, bf16[256,512]{1,0:T(8,128)(2,1)S(1)}, u32[]{:S(2)}) copy-start(bf16[256,512]{1,0:T(8,128)(2,1)S(1)} %collective-permute-done.6.refs_5_) | copy-start | bytes 786436
  47.9 11.2 %collective-permute-start.7 = (bf16[256,512]{1,0:T(8,128)(2,1)S(1)}, bf16[256,512]{1,0:T(8,128)(2,1)}, u32[]{:S(2)}, u32[]{:S(2)}) collective-permute-start(bf16[256,512]{1,0:T(8,128)(2,1)S(1)} %collective-permute-done.6.refs_5_), channel_id=1, source_target_pairs={{8,0},{16,8},{24,16},{28,24},{20,28},{12,20},{4,12},{0,4},{9,1},{1... | collective-permute-start | bytes 786440 | tf_op jit(solution)/shard_map/ppermute | solution.py:267
  53.1 17.1 %collective-permute-start.5 = (bf16[256,512]{1,0:T(8,128)(2,1)}, bf16[256,512]{1,0:T(8,128)(2,1)S(1)}, u32[]{:S(2)}, u32[]{:S(2)}) collective-permute-start(bf16[256,512]{1,0:T(8,128)(2,1)} %collective-permute-done.4.refs_3_), channel_id=1, source_target_pairs={{0,8},{8,16},{16,24},{24,28},{28,20},{20,12},{12,4},{4,0},{1,9},{9... | collective-permute-start | bytes 786440 | tf_op jit(solution)/shard_map/ppermute | solution.py:267
  53.4 11.0 %collective-permute-start.14 = (bf16[256,512]{1,0:T(8,128)(2,1)}, bf16[256,512]{1,0:T(8,128)(2,1)S(1)}, u32[]{:S(2)}, u32[]{:S(2)}) collective-permute-start(bf16[256,512]{1,0:T(8,128)(2,1)} %collective-permute-done.13.refs_12_), channel_id=1, source_target_pairs={{8,0},{16,8},{24,16},{28,24},{20,28},{12,20},{4,12},{0,4},{9,1},{1... | collective-permute-start | bytes 786440 | tf_op jit(solution)/shard_map/ppermute | solution.py:267
  58.7 11.1 %collective-permute-start.11 = (bf16[256,512]{1,0:T(8,128)(2,1)}, bf16[256,512]{1,0:T(8,128)(2,1)S(1)}, u32[]{:S(2)}, u32[]{:S(2)}) collective-permute-start(bf16[256,512]{1,0:T(8,128)(2,1)} %collective-permute-done.10.refs_9_), channel_id=1, source_target_pairs={{0,8},{8,16},{16,24},{24,28},{28,20},{20,12},{12,4},{4,0},{1,9},{9... | collective-permute-start | bytes 786440 | tf_op jit(solution)/shard_map/ppermute | solution.py:267
  59.1 12.1 %collective-permute-start.8 = (bf16[256,512]{1,0:T(8,128)(2,1)}, bf16[256,512]{1,0:T(8,128)(2,1)S(1)}, u32[]{:S(2)}, u32[]{:S(2)}) collective-permute-start(bf16[256,512]{1,0:T(8,128)(2,1)} %collective-permute-done.7.refs_6_), channel_id=1, source_target_pairs={{8,0},{16,8},{24,16},{28,24},{20,28},{12,20},{4,12},{0,4},{9,1},{1... | collective-permute-start | bytes 786440 | tf_op jit(solution)/shard_map/ppermute | solution.py:267
  64.4 11.2 %collective-permute-start.15 = (bf16[256,512]{1,0:T(8,128)(2,1)S(1)}, bf16[256,512]{1,0:T(8,128)(2,1)S(1)}, u32[]{:S(2)}, u32[]{:S(2)}) collective-permute-start(bf16[256,512]{1,0:T(8,128)(2,1)S(1)} %collective-permute-done.14.refs_13_), channel_id=1, source_target_pairs={{8,0},{16,8},{24,16},{28,24},{20,28},{12,20},{4,12},{0,4},{9,1},{1... | collective-permute-start | bytes 786440 | tf_op jit(solution)/shard_map/ppermute | solution.py:267
  69.9 7.0 %collective-permute-start.12 = (bf16[256,512]{1,0:T(8,128)(2,1)S(1)}, bf16[256,512]{1,0:T(8,128)(2,1)S(1)}, u32[]{:S(2)}, u32[]{:S(2)}) collective-permute-start(bf16[256,512]{1,0:T(8,128)(2,1)S(1)} %collective-permute-done.11.refs_10_), channel_id=1, source_target_pairs={{0,8},{8,16},{16,24},{24,28},{28,20},{20,12},{12,4},{4,0},{1,9},{9... | collective-permute-start | bytes 786440 | tf_op jit(solution)/shard_map/ppermute | solution.py:267
  75.7 5.9 %collective-permute-start.16 = (bf16[256,512]{1,0:T(8,128)(2,1)S(1)}, bf16[256,512]{1,0:T(8,128)(2,1)S(1)}, u32[]{:S(2)}, u32[]{:S(2)}) collective-permute-start(bf16[256,512]{1,0:T(8,128)(2,1)S(1)} %collective-permute-done.15.refs_14_), channel_id=1, source_target_pairs={{8,0},{16,8},{24,16},{28,24},{20,28},{12,20},{4,12},{0,4},{9,1},{1... | collective-permute-start | bytes 786440 | tf_op jit(solution)/shard_map/ppermute | solution.py:267
  81.7 2.0 %collective-permute-start.17 = (bf16[16,256,256]{2,1,0:T(8,128)(2,1)S(1)}, bf16[16,256,256]{2,1,0:T(8,128)(2,1)}, u32[]{:S(2)}, u32[]{:S(2)}) collective-permute-start(bf16[16,256,256]{2,1,0:T(8,128)(2,1)S(1)} %bitcast_dynamic-update-slice_fusion), channel_id=1, source_target_pairs={{0,2},{4,6},{9,11},{13,15},{18,16},{22,20},{27,25},{31,29}} | collective-permute-start | bytes 6291464 | tf_op jit(solution)/shard_map/ppermute | solution.py:284
  85.5 33.9 %collective-permute-start.18 = (bf16[16,256,256]{2,1,0:T(8,128)(2,1)S(1)}, bf16[16,256,256]{2,1,0:T(8,128)(2,1)}, u32[]{:S(2)}, u32[]{:S(2)}) collective-permute-start(bf16[16,256,256]{2,1,0:T(8,128)(2,1)S(1)} %broadcast_select_fusion), channel_id=1, source_target_pairs={{0,1},{2,3},{4,5},{6,7},{9,8},{11,10},{13,12},{15,14},{18,19},{16,... | collective-permute-start | bytes 6291464 | tf_op jit(solution)/shard_map/ppermute | solution.py:284
  (12 other events, 72.2 us)

commit v2 on v1

--- a/solution.py
+++ b/solution.py
@@ -150,7 +150,7 @@
             jax.ShapeDtypeStruct((SPEC, channels), f32),
         ],
         scratch_shapes=[pltpu.VMEM((rows, own_time + 2 * LANE), f32)],
-        compiler_params=pltpu.CompilerParams(vmem_limit_bytes=32 << 20),
+        compiler_params=pltpu.CompilerParams(vmem_limit_bytes=60 << 20),
         name="spectrum",
         cost_estimate=pl.CostEstimate(
             flops=2 * channels * SPEC * REACH * 6, bytes_accessed=6 << 20, transcendentals=0
@@ -158,11 +158,11 @@
     )(last, left, own, right, jnp.asarray(window_table()), high, low)
 
 
-def correlate_kernel(pieces, rows, pitch, batch, *refs):
+def correlate_kernel(pieces, batches, rows, pitch, batch, *refs):
     row_refs = refs[:pieces]
-    col_ref = refs[pieces]
-    table_ref, out_ref, lhs_ref, cross_ref = refs[pieces + 1 :]
-    width = col_ref.shape[2]
+    col_refs = refs[pieces : pieces + batches]
+    table_ref, out_ref, lhs_ref, cross_ref = refs[pieces + batches :]
+    width = out_ref.shape[1]
     depth = 2 * GROUP * pieces
     sub = lax.rem(pl.program_id(0), LANE // rows)
 
@@ -176,7 +176,9 @@
     freq = lax.rem(lane, 2 * GROUP) // 2
     start = pl.multiple_of(sub * rows, rows)
     for g in range(GROUPS):
-        cols = jnp.concatenate([col_ref[d, 16 * g : 16 * g + 16, :] for d in range(pieces)], axis=0)
+        cols = jnp.concatenate(
+            [r[d, 16 * g : 16 * g + 16, :] for r in col_refs for d in range(r.shape[0])], axis=0
+        )
         part = lhs_ref[pl.ds(start, rows), g * depth : (g + 1) * depth]
         lhs = jnp.concatenate(
             [jnp.where(freq == q, part, jnp.zeros_like(part)) for q in range(GROUP)], axis=0
@@ -207,21 +209,19 @@
     lax.fori_loop(0, rows // batch, lags, 0)
 
 
-def correlate(row_pieces, cols, table):
+def correlate(row_pieces, col_batches, table):
     pieces = len(row_pieces)
     channels = row_pieces[0].shape[1]
-    width = cols.shape[2]
-    rows, batch = 64, 16
+    width = col_batches[0].shape[2]
+    rows, batch = 64, 32
     pitch = rows + 8
     per = LANE // rows
     return pl.pallas_call(
-        functools.partial(correlate_kernel, pieces, rows, pitch, batch),
+        functools.partial(correlate_kernel, pieces, len(col_batches), rows, pitch, batch),
         grid=(channels // rows,),
         in_specs=[pl.BlockSpec((SPEC, LANE), lambda s: (0, s // per))] * pieces
-        + [
-            pl.BlockSpec((pieces, SPEC, width), lambda s: (0, 0, 0)),
-            pl.BlockSpec((2 * NBIN, 2 * LAGS), lambda s: (0, 0)),
-        ],
+        + [pl.BlockSpec(c.shape, lambda s: (0, 0, 0)) for c in col_batches]
+        + [pl.BlockSpec((2 * NBIN, 2 * LAGS), lambda s: (0, 0))],
         out_specs=pl.BlockSpec((rows, width, LAGS), lambda s: (s, 0, 0)),
         out_shape=jax.ShapeDtypeStruct((channels, width, LAGS), f32),
         scratch_shapes=[
@@ -235,13 +235,32 @@
             bytes_accessed=channels * width * LAGS * 4,
             transcendentals=0,
         ),
-    )(*row_pieces, cols, table)
+    )(*row_pieces, *col_batches, table)
 
 
 def ring_pairs(count):
     order = list(range(0, count, 2)) + list(range(count - 1, 0, -2))
     forward = [(order[i], order[(i + 1) % count]) for i in range(count)]
     return forward, [(b, a) for a, b in forward]
+
+
+def partner(row_pieces, segs, blks, seg, blk):
+    channels = row_pieces[0].shape[1]
+    width = channels * blks // segs
+    offset = (seg * width) % channels
+    cols = jnp.stack([lax.dynamic_slice_in_dim(p, offset, width, 1) for p in row_pieces])
+    relation = jnp.bitwise_xor(blk, (seg * width) // channels)
+    bit = blks
+    while bit > 1:
+        held = relation % bit == 0
+        bit //= 2
+        pairs = []
+        for s in range(segs):
+            for other in range(0, blks, 2 * bit):
+                source = (s * width // channels) ^ other
+                pairs.append((s * blks + source, s * blks + (source ^ bit)))
+        cols = jnp.where(held, cols, lax.ppermute(cols, ("seg", "blk"), pairs))
+    return cols
 
 
 def shards(strain_rate, fir_taps):
@@ -258,33 +277,17 @@
     odd = (second + jnp.where(freq % 2 == 0, 1.0, -1.0) * following).astype(bf16)
 
     forward, backward = ring_pairs(segs)
-    row_pieces = []
-    for own, steps in ((even, (segs // 2, segs - 1 - segs // 2)), (odd, (segs - 1 - segs // 2, segs // 2))):
-        row_pieces.append(own)
-        for pairs, count in zip((forward, backward), steps):
+    longer, shorter = segs // 2, segs - 1 - segs // 2
+    early, late = [], []
+    for own, steps, held_back in ((even, (longer, shorter), (1, 0)), (odd, (shorter, longer), (1, 2))):
+        early.append(own)
+        for pairs, count, after in zip((forward, backward), steps, held_back):
             moved = own
-            for _ in range(count):
+            for step in range(count):
                 moved = lax.ppermute(moved, "seg", pairs)
-                row_pieces.append(moved)
-
-    width = channels * blks // segs
-    offset = (seg * width) % channels
-    cols = jnp.stack([lax.dynamic_slice_in_dim(p, offset, width, 1) for p in row_pieces])
-    owner = [s * width // channels for s in range(segs)]
-    held = blk == (seg * width) // channels
-    below = blks
-    relation = jnp.bitwise_xor(blk, (seg * width) // channels)
-    while below > 1:
-        below //= 2
-        pairs = []
-        for s in range(segs):
-            for high_bits in range(0, blks, 2 * below):
-                source = owner[s] ^ high_bits
-                pairs.append((s * blks + source, s * blks + (source ^ below)))
-        moved = lax.ppermute(cols, ("seg", "blk"), pairs)
-        cols = jnp.where(held, cols, moved)
-        held = relation % below == 0
-    return correlate(row_pieces, cols, jnp.asarray(lag_table(2 * segs)))
+                (early if step < count - after else late).append(moved)
+    col_batches = [partner(batch, segs, blks, seg, blk) for batch in (early, late)]
+    return correlate(early + late, col_batches, jnp.asarray(lag_table(2 * segs)))
 
 
 def solution(mesh):

time: 165 us -> 153 us (0.927)
  waiting for transfers between devices: 77.7 us -> 61.6 us
  starting transfers between devices: 21.3 us -> 28.6 us
  local copies, waits for them, and re-layouts: 9.8 us -> 4.63 us
  other arithmetic: 5.1 us -> 7.68 us
    ppermute x2 -> x4, waiting for transfers between devices: 32.6 us -> 20.4 us  [partner(): cols = jnp.where(held, cols, lax.ppermute(cols, ('seg', 'blk'), pairs))]
    unnamed x49 -> x43, local copies, waits for them, and re-layouts: 8.8 us -> 2.66 us
    ppermute x14, starting transfers between devices: 11.4 us -> 16.9 us  [shards(): moved = lax.ppermute(moved, 'seg', pairs)]
    ppermute x14, waiting for transfers between devices: 43.7 us -> 39.9 us  [shards(): moved = lax.ppermute(moved, 'seg', pairs)]
    pallas_call x1, Pallas kernels: 42.1 us -> 38.7 us  [correlate(): pl.pallas_call(functools.partial(correlate_kernel, pieces, len(col_batche...]
    pallas_call x1, Pallas kernels: 5.05 us -> 7.35 us  [spectrum(): pl.pallas_call(functools.partial(spectrum_kernel, own_time), grid=(channe...]
    ppermute x2 -> x4, starting transfers between devices: 3.33 us -> 5.14 us  [partner(): cols = jnp.where(held, cols, lax.ppermute(cols, ('seg', 'blk'), pairs))]
    select_n x2 -> x4, other arithmetic: 4.99 us -> 6.46 us  [partner(): cols = jnp.where(held, cols, lax.ppermute(cols, ('seg', 'blk'), pairs))]
  transfers between devices with their start and end apart: 19 -> 21, of which waited for: 10 -> 12; matrix products, arithmetic and copies ran while one was open for 3% -> 3% of each run, Pallas kernels for 2% -> 2%
where the time goes in v2:
time: 153 us; the launch traced here: 152 us
  waiting for transfers between devices  61.6 us (40%)
  Pallas kernels  49.3 us (32%)
  starting transfers between devices  28.6 us (19%)
  other arithmetic  7.68 us (5%)
  local copies, waits for them, and re-layouts  4.63 us (3%)
    ppermute x14, waiting for transfers between devices, shards(): moved = lax.ppermute(moved, 'seg', pairs)  39.9 us
    pallas_call x1, Pallas kernels, correlate(): pl.pallas_call(functools.partial(correlate_kernel, pieces, len(col_batche...  38.7 us
    ppermute x4, waiting for transfers between devices, partner(): cols = jnp.where(held, cols, lax.ppermute(cols, ('seg', 'blk'), pairs))  20.4 us
    ppermute x14, starting transfers between devices, shards(): moved = lax.ppermute(moved, 'seg', pairs)  16.9 us
    pallas_call x1, Pallas kernels, spectrum(): pl.pallas_call(functools.partial(spectrum_kernel, own_time), grid=(channe...  7.35 us
    select_n x4, other arithmetic, partner(): cols = jnp.where(held, cols, lax.ppermute(cols, ('seg', 'blk'), pairs))  6.46 us
    ppermute x4, starting transfers between devices, partner(): cols = jnp.where(held, cols, lax.ppermute(cols, ('seg', 'blk'), pairs))  5.14 us
    ppermute x1, starting transfers between devices, shards(): lax.ppermute(strain_rate[:, own_time - LANE:], 'seg', [(i, i + 1) for i i...  3.99 us
  transfers between devices with their start and end apart: 21, of which 12 were waited for; matrix products, arithmetic and copies ran while one was open for 3% of the time, Pallas kernels for 2%

profile of v2, /device:TPU:3, one launch (start us, length us, event | category | flops | bytes accessed | tf_op | source)
XLA Modules:
  0.0 152.3 jit_solution(14720452182523413269)
XLA Ops:
  1.0 1.3 collective-permute-start.1
  2.3 4.0 %collective-permute-start = (bf16[512,128]{1,0:T(8,128)(2,1)S(1)}, bf16[512,128]{1,0:T(8,128)(2,1)S(1)}, u32[]{:S(2)}, u32[]{:S(2)}) collective-permute-start(bf16[512,128]{1,0:T(8,128)(2,1)S(1)} %get-tuple-element.16), channel_id=1, source_target_pairs={{0,4},{4,8},{8,12},{12,16},{16,20},{20,24},{24,28},{1,5},{5,9},{9,... | collective-permute-start | bytes 393224 | tf_op jit(solution)/shard_map/ppermute | solution.py:270
  6.3 3.3 %response.1 = (bf16[1280,256]{1,0:T(8,128)(2,1)}, bf16[1280,256]{1,0:T(8,128)(2,1)}) custom-call(f32[64]{0:T(128)} %taps_ref.1, f32[576,256]{1,0:T(8,128)} %constant.98.clone.table_ref), custom_call_target="tpu_custom_call" | custom-call | flops 213909504 | bytes 2097152 | tf_op jit(solution)/shard_map/response/pallas_call | solution.py:82
  9.6 1.4 collective-permute-done.left_ref
  11.7 7.3 %spectrum.1 = (bf16[256,512]{1,0:T(8,128)(2,1)}, f32[256,512]{1,0:T(8,128)}, f32[256,512]{1,0:T(8,128)}) custom-call(s32[1]{0:T(128)} %bitcast.last_ref, bf16[512,128]{1,0:T(8,128)(2,1)} %copy-done.15, bf16[512,2048]{1,0:T(8,128)(2,1)} %own_ref.1, bf16[512,128]{1,0:T(8,128)(2,1)} %copy-done.14, bf16[512,256]{1,0:T(8,128)(2,1)} %constant.99.clone.window_ref, ...), custom_call_target="tpu_custom_call" | custom-call | flops 2013265920 | bytes 6291456 | tf_op jit(solution)/shard_map/spectrum/pallas_call | solution.py:134
  20.3 4.0 %collective-permute-start.2 = (bf16[256,512]{1,0:T(8,128)(2,1)}, bf16[256,512]{1,0:T(8,128)(2,1)S(1)}, u32[]{:S(2)}, u32[]{:S(2)}) collective-permute-start(bf16[256,512]{1,0:T(8,128)(2,1)} %get-tuple-element.12.refs_0_), channel_id=1, source_target_pairs={{0,8},{8,16},{16,24},{24,28},{28,20},{20,12},{12,4},{4,0},{1,9},{9... | collective-permute-start | bytes 786440 | tf_op jit(solution)/shard_map/ppermute | solution.py:287
  24.4 16.4 %collective-permute-done.2.refs_1_ = bf16[256,512]{1,0:T(8,128)(2,1)S(1)} collective-permute-done((bf16[256,512]{1,0:T(8,128)(2,1)}, bf16[256,512]{1,0:T(8,128)(2,1)S(1)}, u32[]{:S(2)}, u32[]{:S(2)}) %collective-permute-start.2) | collective-permute-done | bytes 262176 | tf_op jit(solution)/shard_map/ppermute | solution.py:287
  41.7 2.0 %collective-permute-start.6 = (bf16[256,512]{1,0:T(8,128)(2,1)S(1)}, bf16[256,512]{1,0:T(8,128)(2,1)S(1)}, u32[]{:S(2)}, u32[]{:S(2)}) collective-permute-start(bf16[256,512]{1,0:T(8,128)(2,1)S(1)} %collective-permute-done.5.refs_4_), channel_id=1, source_target_pairs={{8,0},{16,8},{24,16},{28,24},{20,28},{12,20},{4,12},{0,4},{9,1},{1... | collective-permute-start | bytes 786440 | tf_op jit(solution)/shard_map/ppermute | solution.py:287
  45.0 1.4 collective-permute-start.9
  48.9 2.2 %collective-permute-start.7 = (bf16[256,512]{1,0:T(8,128)(2,1)S(1)}, bf16[256,512]{1,0:T(8,128)(2,1)S(1)}, u32[]{:S(2)}, u32[]{:S(2)}) collective-permute-start(bf16[256,512]{1,0:T(8,128)(2,1)S(1)} %collective-permute-done.6.refs_5_), channel_id=1, source_target_pairs={{8,0},{16,8},{24,16},{28,24},{20,28},{12,20},{4,12},{0,4},{9,1},{1... | collective-permute-start | bytes 786440 | tf_op jit(solution)/shard_map/ppermute | solution.py:287
  51.1 3.4 %collective-permute-done.11.refs_10_ = bf16[256,512]{1,0:T(8,128)(2,1)S(1)} collective-permute-done((bf16[256,512]{1,0:T(8,128)(2,1)S(1)}, bf16[256,512]{1,0:T(8,128)(2,1)S(1)}, u32[]{:S(2)}, u32[]{:S(2)}) %collective-permute-start.11) | collective-permute-done | bytes 262176 | tf_op jit(solution)/shard_map/ppermute | solution.py:287
  54.5 2.2 %collective-permute-start.12 = (bf16[256,512]{1,0:T(8,128)(2,1)S(1)}, bf16[256,512]{1,0:T(8,128)(2,1)}, u32[]{:S(2)}, u32[]{:S(2)}) collective-permute-start(bf16[256,512]{1,0:T(8,128)(2,1)S(1)} %collective-permute-done.11.refs_10_), channel_id=1, source_target_pairs={{8,0},{16,8},{24,16},{28,24},{20,28},{12,20},{4,12},{0,4},{9,1},{1... | collective-permute-start | bytes 786440 | tf_op jit(solution)/shard_map/ppermute | solution.py:287
  56.7 2.3 %collective-permute-done.4.refs_3_ = bf16[256,512]{1,0:T(8,128)(2,1)S(1)} collective-permute-done((bf16[256,512]{1,0:T(8,128)(2,1)S(1)}, bf16[256,512]{1,0:T(8,128)(2,1)S(1)}, u32[]{:S(2)}, u32[]{:S(2)}) %collective-permute-start.4) | collective-permute-done | bytes 262176 | tf_op jit(solution)/shard_map/ppermute | solution.py:287
  60.2 3.8 %collective-permute-done.10.refs_9_ = bf16[256,512]{1,0:T(8,128)(2,1)} collective-permute-done((bf16[256,512]{1,0:T(8,128)(2,1)S(1)}, bf16[256,512]{1,0:T(8,128)(2,1)}, u32[]{:S(2)}, u32[]{:S(2)}) %collective-permute-start.10) | collective-permute-done | bytes 262176 | tf_op jit(solution)/shard_map/ppermute | solution.py:287
  66.7 1.9 %collective-permute-start.17 = (bf16[12,256,256]{2,1,0:T(8,128)(2,1)S(1)}, bf16[12,256,256]{2,1,0:T(8,128)(2,1)}, u32[]{:S(2)}, u32[]{:S(2)}) collective-permute-start(bf16[12,256,256]{2,1,0:T(8,128)(2,1)S(1)} %bitcast_dynamic-update-slice_fusion), channel_id=1, source_target_pairs={{0,2},{4,6},{9,11},{13,15},{18,16},{22,20},{27,25},{31,29}} | collective-permute-start | bytes 4718600 | tf_op jit(solution)/shard_map/ppermute | solution.py:262
  68.5 2.3 %collective-permute-start.15 = (bf16[256,512]{1,0:T(8,128)(2,1)}, bf16[256,512]{1,0:T(8,128)(2,1)S(1)}, u32[]{:S(2)}, u32[]{:S(2)}) collective-permute-start(bf16[256,512]{1,0:T(8,128)(2,1)} %collective-permute-done.12.refs_11_), channel_id=1, source_target_pairs={{8,0},{16,8},{24,16},{28,24},{20,28},{12,20},{4,12},{0,4},{9,1},{1... | collective-permute-start | bytes 786440 | tf_op jit(solution)/shard_map/ppermute | solution.py:287
  71.0 5.0 %collective-permute-done.15.refs_14_ = bf16[256,512]{1,0:T(8,128)(2,1)S(1)} collective-permute-done((bf16[256,512]{1,0:T(8,128)(2,1)}, bf16[256,512]{1,0:T(8,128)(2,1)S(1)}, u32[]{:S(2)}, u32[]{:S(2)}) %collective-permute-start.15) | collective-permute-done | bytes 262176 | tf_op jit(solution)/shard_map/ppermute | solution.py:287
  76.0 2.2 %collective-permute-start.16 = (bf16[256,512]{1,0:T(8,128)(2,1)S(1)}, bf16[256,512]{1,0:T(8,128)(2,1)S(1)}, u32[]{:S(2)}, u32[]{:S(2)}) collective-permute-start(bf16[256,512]{1,0:T(8,128)(2,1)S(1)} %collective-permute-done.15.refs_14_), channel_id=1, source_target_pairs={{8,0},{16,8},{24,16},{28,24},{20,28},{12,20},{4,12},{0,4},{9,1},{1... | collective-permute-start | bytes 786440 | tf_op jit(solution)/shard_map/ppermute | solution.py:287
  78.2 5.0 %collective-permute-done.14.refs_13_ = bf16[256,512]{1,0:T(8,128)(2,1)S(1)} collective-permute-done((bf16[256,512]{1,0:T(8,128)(2,1)}, bf16[256,512]{1,0:T(8,128)(2,1)S(1)}, u32[]{:S(2)}, u32[]{:S(2)}) %collective-permute-start.14) | collective-permute-done | bytes 262176 | tf_op jit(solution)/shard_map/ppermute | solution.py:287
  83.4 1.7 %broadcast_select_fusion = bf16[12,256,256]{2,1,0:T(8,128)(2,1)S(1)} fusion(bf16[12,256,256]{2,1,0:T(8,128)(2,1)} %copy-done, bf16[12,256,256]{2,1,0:T(8,128)(2,1)} %collective-permute-done.17, pred[]{:T(512)S(6)} %eq.32), kind=kLoop, calls=%fused_computation | loop fusion | flops 786432 | bytes 4718593 | tf_op jit(solution)/shard_map/jit(_where)/select_n | solution.py:262
  88.6 20.3 %collective-permute-done.20 = bf16[4,256,256]{2,1,0:T(8,128)(2,1)} collective-permute-done((bf16[4,256,256]{2,1,0:T(8,128)(2,1)S(1)}, bf16[4,256,256]{2,1,0:T(8,128)(2,1)}, u32[]{:S(2)}, u32[]{:S(2)}) %collective-permute-start.20) | collective-permute-done | bytes 524320 | tf_op jit(solution)/shard_map/ppermute | solution.py:262
  108.9 1.9 %broadcast_select_fusion.3.refs_17_ = bf16[4,256,256]{2,1,0:T(8,128)(2,1)} fusion(bf16[4,256,256]{2,1,0:T(8,128)(2,1)} %collective-permute-done.20, pred[]{:T(512)S(6)} %eq.31, bf16[4,256,256]{2,1,0:T(8,128)(2,1)S(1)} %collective-permute-done.19, bf16[1,256,256]{2,1,0:T(8,128)(2,1)S(1)} %dynamic-slice_bitcast_fusion, ...), kind=kLoop, calls=%fused_computation.5 | loop fusion | flops 1310720 | bytes 2097154 | tf_op jit(solution)/shard_map/jit(_where)/select_n | solution.py:262
  110.8 2.8 %broadcast_select_fusion.1.refs_16_ = bf16[12,256,256]{2,1,0:T(8,128)(2,1)} fusion(bf16[12,256,256]{2,1,0:T(8,128)(2,1)S(1)} %broadcast_select_fusion, bf16[12,256,256]{2,1,0:T(8,128)(2,1)} %collective-permute-done.18, pred[]{:T(512)S(6)} %eq.31), kind=kLoop, calls=%fused_computation.1 | loop fusion | flops 786432 | bytes 4718593 | tf_op jit(solution)/shard_map/jit(_where)/select_n | solution.py:262
  113.6 38.7 %correlate.1 = f32[512,256,128]{2,1,0:T(8,128)} custom-call(bf16[256,512]{1,0:T(8,128)(2,1)} %get-tuple-element.12.refs_0_, bf16[256,512]{1,0:T(8,128)(2,1)} %copy-done.2, bf16[256,512]{1,0:T(8,128)(2,1)} %copy-done.4, bf16[256,512]{1,0:T(8,128)(2,1)} %copy-done.8, bf16[256,512]{1,0:T(8,128)(2,1)} %copy-done.3, bf16[256,512]{1,0:T(8,128)(2,1)} %copy-done.5, ...), custom_call_target="tpu_custom_call" | custom-call | flops 25769803776 | bytes 67108864 | tf_op jit(solution)/shard_map/correlate/pallas_call | solution.py:219
  (77 shorter events, 15.0 us)
Async XLA Ops:
  1.0 8.6 %collective-permute-start.1 = (bf16[512,128]{1,0:T(8,128)(2,1)S(1)}, bf16[512,128]{1,0:T(8,128)(2,1)S(1)}, u32[]{:S(2)}, u32[]{:S(2)}) collective-permute-start(bf16[512,128]{1,0:T(8,128)(2,1)S(1)} %get-tuple-element.15), channel_id=1, source_target_pairs={{4,0},{8,4},{12,8},{16,12},{20,16},{24,20},{28,24},{5,1},{9,5},{13... | collective-permute-start | bytes 393224 | tf_op jit(solution)/shard_map/ppermute | solution.py:271
  2.3 8.8 %collective-permute-start = (bf16[512,128]{1,0:T(8,128)(2,1)S(1)}, bf16[512,128]{1,0:T(8,128)(2,1)S(1)}, u32[]{:S(2)}, u32[]{:S(2)}) collective-permute-start(bf16[512,128]{1,0:T(8,128)(2,1)S(1)} %get-tuple-element.16), channel_id=1, source_target_pairs={{0,4},{4,8},{8,12},{12,16},{16,20},{20,24},{24,28},{1,5},{5,9},{9,... | collective-permute-start | bytes 393224 | tf_op jit(solution)/shard_map/ppermute | solution.py:270
  19.0 24.7 %collective-permute-start.8 = (f32[256,512]{1,0:T(8,128)}, f32[256,512]{1,0:T(8,128)S(1)}, u32[]{:S(2)}, u32[]{:S(2)}) collective-permute-start(f32[256,512]{1,0:T(8,128)} %get-tuple-element.14), channel_id=1, source_target_pairs={{4,0},{8,4},{12,8},{16,12},{20,16},{24,20},{28,24},{5,1},{9,5},{13... | collective-permute-start | bytes 1572872 | tf_op jit(solution)/shard_map/ppermute | solution.py:275
  20.3 20.5 %collective-permute-start.2 = (bf16[256,512]{1,0:T(8,128)(2,1)}, bf16[256,512]{1,0:T(8,128)(2,1)S(1)}, u32[]{:S(2)}, u32[]{:S(2)}) collective-permute-start(bf16[256,512]{1,0:T(8,128)(2,1)} %get-tuple-element.12.refs_0_), channel_id=1, source_target_pairs={{0,8},{8,16},{16,24},{24,28},{28,20},{20,12},{12,4},{4,0},{1,9},{9... | collective-permute-start | bytes 786440 | tf_op jit(solution)/shard_map/ppermute | solution.py:287
  24.4 17.3 %collective-permute-start.5 = (bf16[256,512]{1,0:T(8,128)(2,1)}, bf16[256,512]{1,0:T(8,128)(2,1)S(1)}, u32[]{:S(2)}, u32[]{:S(2)}) collective-permute-start(bf16[256,512]{1,0:T(8,128)(2,1)} %get-tuple-element.12.refs_0_), channel_id=1, source_target_pairs={{8,0},{16,8},{24,16},{28,24},{20,28},{12,20},{4,12},{0,4},{9,1},{1... | collective-permute-start | bytes 786440 | tf_op jit(solution)/shard_map/ppermute | solution.py:287
  40.8 19.3 %copy-start.2 = (bf16[256,512]{1,0:T(8,128)(2,1)}, bf16[256,512]{1,0:T(8,128)(2,1)S(1)}, u32[]{:S(2)}) copy-start(bf16[256,512]{1,0:T(8,128)(2,1)S(1)} %collective-permute-done.2.refs_1_) | copy-start | bytes 786436
  40.8 6.8 %collective-permute-start.3 = (bf16[256,512]{1,0:T(8,128)(2,1)S(1)}, bf16[256,512]{1,0:T(8,128)(2,1)S(1)}, u32[]{:S(2)}, u32[]{:S(2)}) collective-permute-start(bf16[256,512]{1,0:T(8,128)(2,1)S(1)} %collective-permute-done.2.refs_1_), channel_id=1, source_target_pairs={{0,8},{8,16},{16,24},{24,28},{28,20},{20,12},{12,4},{4,0},{1,9},{9... | collective-permute-start | bytes 786440 | tf_op jit(solution)/shard_map/ppermute | solution.py:287
  41.7 7.2 %collective-permute-start.6 = (bf16[256,512]{1,0:T(8,128)(2,1)S(1)}, bf16[256,512]{1,0:T(8,128)(2,1)S(1)}, u32[]{:S(2)}, u32[]{:S(2)}) collective-permute-start(bf16[256,512]{1,0:T(8,128)(2,1)S(1)} %collective-permute-done.5.refs_4_), channel_id=1, source_target_pairs={{8,0},{16,8},{24,16},{28,24},{20,28},{12,20},{4,12},{0,4},{9,1},{1... | collective-permute-start | bytes 786440 | tf_op jit(solution)/shard_map/ppermute | solution.py:287
  44.9 21.8 %copy-start.1 = (bf16[256,512]{1,0:T(8,128)(2,1)}, bf16[256,512]{1,0:T(8,128)(2,1)S(1)}, u32[]{:S(2)}) copy-start(bf16[256,512]{1,0:T(8,128)(2,1)S(1)} %add_convert_fusion.refs_7_) | copy-start | bytes 786436
  44.9 9.6 %collective-permute-start.11 = (bf16[256,512]{1,0:T(8,128)(2,1)S(1)}, bf16[256,512]{1,0:T(8,128)(2,1)S(1)}, u32[]{:S(2)}, u32[]{:S(2)}) collective-permute-start(bf16[256,512]{1,0:T(8,128)(2,1)S(1)} %add_convert_fusion.refs_7_), channel_id=1, source_target_pairs={{8,0},{16,8},{24,16},{28,24},{20,28},{12,20},{4,12},{0,4},{9,1},{1... | collective-permute-start | bytes 786440 | tf_op jit(solution)/shard_map/ppermute | solution.py:287
  45.0 11.7 %collective-permute-start.9 = (bf16[256,512]{1,0:T(8,128)(2,1)S(1)}, bf16[256,512]{1,0:T(8,128)(2,1)S(1)}, u32[]{:S(2)}, u32[]{:S(2)}) collective-permute-start(bf16[256,512]{1,0:T(8,128)(2,1)S(1)} %add_convert_fusion.refs_7_), channel_id=1, source_target_pairs={{0,8},{8,16},{16,24},{24,28},{28,20},{20,12},{12,4},{4,0},{1,9},{9... | collective-permute-start | bytes 786440 | tf_op jit(solution)/shard_map/ppermute | solution.py:287
  47.6 11.4 %collective-permute-start.4 = (bf16[256,512]{1,0:T(8,128)(2,1)S(1)}, bf16[256,512]{1,0:T(8,128)(2,1)S(1)}, u32[]{:S(2)}, u32[]{:S(2)}) collective-permute-start(bf16[256,512]{1,0:T(8,128)(2,1)S(1)} %collective-permute-done.3.refs_2_), channel_id=1, source_target_pairs={{0,8},{8,16},{16,24},{24,28},{28,20},{20,12},{12,4},{4,0},{1,9},{9... | collective-permute-start | bytes 786440 | tf_op jit(solution)/shard_map/ppermute | solution.py:287
  48.9 29.3 %copy-start.5 = (bf16[256,512]{1,0:T(8,128)(2,1)}, bf16[256,512]{1,0:T(8,128)(2,1)S(1)}, u32[]{:S(2)}) copy-start(bf16[256,512]{1,0:T(8,128)(2,1)S(1)} %collective-permute-done.6.refs_5_) | copy-start | bytes 786436
  48.9 11.2 %collective-permute-start.7 = (bf16[256,512]{1,0:T(8,128)(2,1)S(1)}, bf16[256,512]{1,0:T(8,128)(2,1)S(1)}, u32[]{:S(2)}, u32[]{:S(2)}) collective-permute-start(bf16[256,512]{1,0:T(8,128)(2,1)S(1)} %collective-permute-done.6.refs_5_), channel_id=1, source_target_pairs={{8,0},{16,8},{24,16},{28,24},{20,28},{12,20},{4,12},{0,4},{9,1},{1... | collective-permute-start | bytes 786440 | tf_op jit(solution)/shard_map/ppermute | solution.py:287
  54.5 11.2 %collective-permute-start.12 = (bf16[256,512]{1,0:T(8,128)(2,1)S(1)}, bf16[256,512]{1,0:T(8,128)(2,1)}, u32[]{:S(2)}, u32[]{:S(2)}) collective-permute-start(bf16[256,512]{1,0:T(8,128)(2,1)S(1)} %collective-permute-done.11.refs_10_), channel_id=1, source_target_pairs={{8,0},{16,8},{24,16},{28,24},{20,28},{12,20},{4,12},{0,4},{9,1},{1... | collective-permute-start | bytes 786440 | tf_op jit(solution)/shard_map/ppermute | solution.py:287
  56.7 7.3 %collective-permute-start.10 = (bf16[256,512]{1,0:T(8,128)(2,1)S(1)}, bf16[256,512]{1,0:T(8,128)(2,1)}, u32[]{:S(2)}, u32[]{:S(2)}) collective-permute-start(bf16[256,512]{1,0:T(8,128)(2,1)S(1)} %collective-permute-done.9.refs_8_), channel_id=1, source_target_pairs={{0,8},{8,16},{16,24},{24,28},{28,20},{20,12},{12,4},{4,0},{1,9},{9... | collective-permute-start | bytes 786440 | tf_op jit(solution)/shard_map/ppermute | solution.py:287
  66.7 16.7 %collective-permute-start.17 = (bf16[12,256,256]{2,1,0:T(8,128)(2,1)S(1)}, bf16[12,256,256]{2,1,0:T(8,128)(2,1)}, u32[]{:S(2)}, u32[]{:S(2)}) collective-permute-start(bf16[12,256,256]{2,1,0:T(8,128)(2,1)S(1)} %bitcast_dynamic-update-slice_fusion), channel_id=1, source_target_pairs={{0,2},{4,6},{9,11},{13,15},{18,16},{22,20},{27,25},{31,29}} | collective-permute-start | bytes 4718600 | tf_op jit(solution)/shard_map/ppermute | solution.py:262
  68.5 7.4 %collective-permute-start.15 = (bf16[256,512]{1,0:T(8,128)(2,1)}, bf16[256,512]{1,0:T(8,128)(2,1)S(1)}, u32[]{:S(2)}, u32[]{:S(2)}) collective-permute-start(bf16[256,512]{1,0:T(8,128)(2,1)} %collective-permute-done.12.refs_11_), channel_id=1, source_target_pairs={{8,0},{16,8},{24,16},{28,24},{20,28},{12,20},{4,12},{0,4},{9,1},{1... | collective-permute-start | bytes 786440 | tf_op jit(solution)/shard_map/ppermute | solution.py:287
  70.9 7.3 %collective-permute-start.13 = (bf16[256,512]{1,0:T(8,128)(2,1)S(1)}, bf16[256,512]{1,0:T(8,128)(2,1)S(1)}, u32[]{:S(2)}, u32[]{:S(2)}) collective-permute-start(bf16[256,512]{1,0:T(8,128)(2,1)S(1)} %collective-permute-done.4.refs_3_), channel_id=1, source_target_pairs={{0,8},{8,16},{16,24},{24,28},{28,20},{20,12},{12,4},{4,0},{1,9},{9... | collective-permute-start | bytes 786440 | tf_op jit(solution)/shard_map/ppermute | solution.py:287
  70.9 12.4 %collective-permute-start.14 = (bf16[256,512]{1,0:T(8,128)(2,1)}, bf16[256,512]{1,0:T(8,128)(2,1)S(1)}, u32[]{:S(2)}, u32[]{:S(2)}) collective-permute-start(bf16[256,512]{1,0:T(8,128)(2,1)} %collective-permute-done.10.refs_9_), channel_id=1, source_target_pairs={{0,8},{8,16},{16,24},{24,28},{28,20},{20,12},{12,4},{4,0},{1,9},{9... | collective-permute-start | bytes 786440 | tf_op jit(solution)/shard_map/ppermute | solution.py:287
  76.0 7.3 %collective-permute-start.16 = (bf16[256,512]{1,0:T(8,128)(2,1)S(1)}, bf16[256,512]{1,0:T(8,128)(2,1)S(1)}, u32[]{:S(2)}, u32[]{:S(2)}) collective-permute-start(bf16[256,512]{1,0:T(8,128)(2,1)S(1)} %collective-permute-done.15.refs_14_), channel_id=1, source_target_pairs={{8,0},{16,8},{24,16},{28,24},{20,28},{12,20},{4,12},{0,4},{9,1},{1... | collective-permute-start | bytes 786440 | tf_op jit(solution)/shard_map/ppermute | solution.py:287
  85.1 25.8 %collective-permute-start.18 = (bf16[12,256,256]{2,1,0:T(8,128)(2,1)S(1)}, bf16[12,256,256]{2,1,0:T(8,128)(2,1)}, u32[]{:S(2)}, u32[]{:S(2)}) collective-permute-start(bf16[12,256,256]{2,1,0:T(8,128)(2,1)S(1)} %broadcast_select_fusion), channel_id=1, source_target_pairs={{0,1},{2,3},{4,5},{6,7},{9,8},{11,10},{13,12},{15,14},{18,19},{16,... | collective-permute-start | bytes 4718600 | tf_op jit(solution)/shard_map/ppermute | solution.py:262
  86.4 0.7 collective-permute-start.19
  87.3 21.7 %collective-permute-start.20 = (bf16[4,256,256]{2,1,0:T(8,128)(2,1)S(1)}, bf16[4,256,256]{2,1,0:T(8,128)(2,1)}, u32[]{:S(2)}, u32[]{:S(2)}) collective-permute-start(bf16[4,256,256]{2,1,0:T(8,128)(2,1)S(1)} %broadcast_select_fusion.2), channel_id=1, source_target_pairs={{0,1},{2,3},{4,5},{6,7},{9,8},{11,10},{13,12},{15,14},{18,19},{16,... | collective-permute-start | bytes 1572872 | tf_op jit(solution)/shard_map/ppermute | solution.py:262
  (13 other events, 132.1 us)

commit v3 on v2

--- a/solution.py
+++ b/solution.py
@@ -92,70 +92,110 @@
     )(fir_taps, jnp.asarray(half_dft_table()))
 
 
-def spectrum_kernel(own_time, last_ref, left_ref, own_ref, right_ref, window_ref, high_ref, low_ref,
-                    even_ref, first_ref, second_ref, normed_ref):
-    rows = own_ref.shape[0]
-    tiles = own_time // LANE + 2
-    zero = jnp.zeros((rows, LANE), bf16)
-    extended = jnp.concatenate([zero, left_ref[...], own_ref[...], right_ref[...], zero], axis=1)
-    window = window_ref[...]
-    for pair in range(tiles // 2):
-        start = 2 * LANE * pair
+def normalize(extended, window, normed_ref):
+    for start in range(0, extended.shape[1] - 2 * LANE, 2 * LANE):
         total = jnp.dot(
             jnp.abs(extended[:, start : start + 4 * LANE]), window, preferred_element_type=f32
         )
         centre = extended[:, start + LANE : start + 3 * LANE].astype(f32)
         normed_ref[:, start : start + 2 * LANE] = centre / (total * (1.0 / (2 * RAMW + 1)) + EPSILON)
 
-    def transform(start, length):
-        high, low = split(normed_ref[:, start : start + length])
-        kept = high_ref[:length, :]
-        out = jnp.dot(high, kept, preferred_element_type=f32)
-        out += jnp.dot(low, kept, preferred_element_type=f32)
-        out += jnp.dot(high, low_ref[:length, :], preferred_element_type=f32)
-        return out.T
-
-    freq = lax.broadcasted_iota(jnp.int32, (SPEC, rows), 0) // 2
-    sign = jnp.where(lax.rem(freq, 2) == 0, 1.0, -1.0)
-    first = transform(0, REACH)
-    second = transform(NFFT, REACH)
-    tail = transform(own_time, 2 * LANE)
+
+def transform(normed, kept, rest):
+    high, low = split(normed)
+    out = jnp.dot(high, kept, preferred_element_type=f32)
+    out += jnp.dot(low, kept, preferred_element_type=f32)
+    out += jnp.dot(high, rest, preferred_element_type=f32)
+    return out.T
+
+
+def signs(shape):
+    freq = lax.broadcasted_iota(jnp.int32, shape, 0) // 2
+    return jnp.where(lax.rem(freq, 2) == 0, 1.0, -1.0)
+
+
+def inner_kernel(own_ref, window_ref, high_ref, low_ref, first_ref, second_ref, normed_ref):
+    normalize(own_ref[...], window_ref[...], normed_ref)
+    edge = 2 * LANE
+    first_ref[...] = transform(normed_ref[:, :NFFT], high_ref[edge:, :], low_ref[edge:, :])
+    second_ref[...] = transform(
+        normed_ref[:, NFFT - edge : 2 * NFFT - edge], high_ref[:NFFT, :], low_ref[:NFFT, :]
+    )
+
+
+def spectra_inner(own, tables):
+    channels, own_time = own.shape
+    rows = min(LANE, channels)
+    whole = lambda i: (0, 0)
+    return pl.pallas_call(
+        inner_kernel,
+        grid=(channels // rows,),
+        in_specs=[
+            pl.BlockSpec((rows, own_time), lambda i: (i, 0)),
+            pl.BlockSpec((4 * LANE, 2 * LANE), whole),
+            pl.BlockSpec((REACH, SPEC), whole),
+            pl.BlockSpec((REACH, SPEC), whole),
+        ],
+        out_specs=[pl.BlockSpec((SPEC, rows), lambda i: (0, i))] * 2,
+        out_shape=[jax.ShapeDtypeStruct((SPEC, channels), f32)] * 2,
+        scratch_shapes=[pltpu.VMEM((rows, own_time - 2 * LANE), f32)],
+        compiler_params=pltpu.CompilerParams(vmem_limit_bytes=60 << 20),
+        name="spectra_inner",
+        cost_estimate=pl.CostEstimate(
+            flops=2 * channels * SPEC * REACH * 6, bytes_accessed=6 << 20, transcendentals=0
+        ),
+    )(own, jnp.asarray(window_table()), *tables)
+
+
+def edge_kernel(last_ref, left_ref, head_ref, end_ref, right_ref, first_in, second_in, window_ref,
+                high0_ref, low0_ref, high1_ref, low1_ref, first_ref, even_ref, second_ref, normed_ref):
+    zero = jnp.zeros(right_ref.shape, bf16)
+    window = window_ref[...]
+    head, low_head = high0_ref[...], low0_ref[...]
+    normalize(jnp.concatenate([zero, left_ref[...], head_ref[...]], axis=1), window, normed_ref)
+    first = first_in[...] + transform(normed_ref[...], head, low_head)
     first_ref[...] = first
+    normalize(jnp.concatenate([end_ref[...], right_ref[...], zero], axis=1), window, normed_ref)
+    second = second_in[...] + transform(normed_ref[...], high1_ref[...], low1_ref[...])
+    sign = signs(second.shape)
     even_ref[...] = (first + sign * second).astype(bf16)
+    tail = transform(normed_ref[...], head, low_head)
     second_ref[...] = second + jnp.where(last_ref[0] == 1, sign * tail, jnp.zeros_like(tail))
 
 
-def spectrum(last, left, own, right, high, low):
+def spectra_edge(last, left, own, right, first, second, tables):
     channels, own_time = own.shape
-    rows = min(128, channels)
+    rows = min(2 * LANE, channels)
+    edge = 2 * LANE
+    across = lambda i: (0, i)
     line = lambda i: (i, 0)
-    whole = lambda i: (0, 0)
-    across = lambda i: (0, i)
+    high, low = tables
     return pl.pallas_call(
-        functools.partial(spectrum_kernel, own_time),
+        edge_kernel,
         grid=(channels // rows,),
         in_specs=[
             pl.BlockSpec(memory_space=pltpu.SMEM),
             pl.BlockSpec((rows, LANE), line),
-            pl.BlockSpec((rows, own_time), line),
+            pl.BlockSpec((rows, edge), line),
+            pl.BlockSpec((rows, edge), lambda i: (i, own_time // edge - 1)),
             pl.BlockSpec((rows, LANE), line),
-            pl.BlockSpec((4 * LANE, 2 * LANE), whole),
-            pl.BlockSpec((REACH, SPEC), whole),
-            pl.BlockSpec((REACH, SPEC), whole),
+            pl.BlockSpec((SPEC, rows), across),
+            pl.BlockSpec((SPEC, rows), across),
+            pl.BlockSpec((2 * edge, edge), lambda i: (0, 0)),
+            pl.BlockSpec((edge, SPEC), lambda i: (0, 0)),
+            pl.BlockSpec((edge, SPEC), lambda i: (0, 0)),
+            pl.BlockSpec((edge, SPEC), lambda i: (REACH // edge - 1, 0)),
+            pl.BlockSpec((edge, SPEC), lambda i: (REACH // edge - 1, 0)),
         ],
         out_specs=[pl.BlockSpec((SPEC, rows), across)] * 3,
-        out_shape=[
-            jax.ShapeDtypeStruct((SPEC, channels), bf16),
-            jax.ShapeDtypeStruct((SPEC, channels), f32),
-            jax.ShapeDtypeStruct((SPEC, channels), f32),
-        ],
-        scratch_shapes=[pltpu.VMEM((rows, own_time + 2 * LANE), f32)],
+        out_shape=[jax.ShapeDtypeStruct((SPEC, channels), dtype) for dtype in (f32, bf16, f32)],
+        scratch_shapes=[pltpu.VMEM((rows, edge), f32)],
         compiler_params=pltpu.CompilerParams(vmem_limit_bytes=60 << 20),
-        name="spectrum",
+        name="spectra_edge",
         cost_estimate=pl.CostEstimate(
-            flops=2 * channels * SPEC * REACH * 6, bytes_accessed=6 << 20, transcendentals=0
+            flops=2 * channels * SPEC * edge * 9, bytes_accessed=4 << 20, transcendentals=0
         ),
-    )(last, left, own, right, jnp.asarray(window_table()), high, low)
+    )(last, left, own, own, right, first, second, jnp.asarray(window_table()), high, low, high, low)
 
 
 def correlate_kernel(pieces, batches, rows, pitch, batch, *refs):
@@ -206,7 +246,7 @@
         out_ref[pl.ds(b * batch, batch)] = out.reshape(batch, width, LAGS)
         return carry
 
-    lax.fori_loop(0, rows // batch, lags, 0)
+    lax.fori_loop(0, rows // batch, lags, 0, unroll=2)
 
 
 def correlate(row_pieces, col_batches, table):
@@ -238,15 +278,23 @@
     )(*row_pieces, *col_batches, table)
 
 
+def ring_order(count):
+    return list(range(0, count, 2)) + list(range(count - 1, 0, -2))
+
+
 def ring_pairs(count):
-    order = list(range(0, count, 2)) + list(range(count - 1, 0, -2))
+    order = ring_order(count)
     forward = [(order[i], order[(i + 1) % count]) for i in range(count)]
     return forward, [(b, a) for a, b in forward]
 
 
+def partner_width(channels, segs, blks):
+    return channels * blks // segs
+
+
 def partner(row_pieces, segs, blks, seg, blk):
     channels = row_pieces[0].shape[1]
-    width = channels * blks // segs
+    width = partner_width(channels, segs, blks)
     offset = (seg * width) % channels
     cols = jnp.stack([lax.dynamic_slice_in_dim(p, offset, width, 1) for p in row_pieces])
     relation = jnp.bitwise_xor(blk, (seg * width) // channels)
@@ -264,30 +312,36 @@
 
 
 def shards(strain_rate, fir_taps):
-    channels, own_time = strain_rate.shape
+    own_time = strain_rate.shape[1]
     segs, blks = lax.axis_size("seg"), lax.axis_size("blk")
     seg, blk = lax.axis_index("seg"), lax.axis_index("blk")
-    left = lax.ppermute(strain_rate[:, own_time - LANE :], "seg", [(i, i + 1) for i in range(segs - 1)])
-    right = lax.ppermute(strain_rate[:, :LANE], "seg", [(i + 1, i) for i in range(segs - 1)])
-    high, low = response(fir_taps)
+    upward = [(i, i + 1) for i in range(segs - 1)]
+    downward = [(i + 1, i) for i in range(segs - 1)]
+    tables = response(fir_taps)
+    source, tables = lax.optimization_barrier((strain_rate, tables))
+    left = lax.ppermute(source[:, own_time - LANE :], "seg", upward)
+    right = lax.ppermute(source[:, :LANE], "seg", downward)
+    first, second = spectra_inner(strain_rate, tables)
     last = (seg == segs - 1).astype(jnp.int32).reshape(1)
-    even, first, second = spectrum(last, left, strain_rate, right, high, low)
-    following = lax.ppermute(first, "seg", [(i + 1, i) for i in range(segs - 1)])
-    freq = lax.broadcasted_iota(jnp.int32, (SPEC, 1), 0) // 2
-    odd = (second + jnp.where(freq % 2 == 0, 1.0, -1.0) * following).astype(bf16)
+    first, even, second = spectra_edge(last, left, strain_rate, right, first, second, tables)
+    following = lax.ppermute(first, "seg", downward)
+    odd = (second + signs((SPEC, 1)) * following).astype(bf16)
+    even_later, odd = lax.optimization_barrier((even, odd))
 
     forward, backward = ring_pairs(segs)
     longer, shorter = segs // 2, segs - 1 - segs // 2
-    early, late = [], []
-    for own, steps, held_back in ((even, (longer, shorter), (1, 0)), (odd, (shorter, longer), (1, 2))):
-        early.append(own)
-        for pairs, count, after in zip((forward, backward), steps, held_back):
-            moved = own
-            for step in range(count):
-                moved = lax.ppermute(moved, "seg", pairs)
-                (early if step < count - after else late).append(moved)
-    col_batches = [partner(batch, segs, blks, seg, blk) for batch in (early, late)]
-    return correlate(early + late, col_batches, jnp.asarray(lag_table(2 * segs)))
+    early, middle, late = [even, odd], [], []
+    chains = ((even, backward, longer, 0), (even_later, forward, shorter, 1),
+              (odd, backward, longer, 1), (odd, forward, shorter, 1))
+    for moved, pairs, count, lag in chains:
+        for step in range(1, count + 1):
+            moved = lax.ppermute(moved, "seg", pairs)
+            if step + lag <= segs // 4:
+                early.append(moved)
+            else:
+                (middle if step + lag < segs // 2 else late).append(moved)
+    col_batches = [partner(batch, segs, blks, seg, blk) for batch in (early, middle, late)]
+    return correlate(early + middle + late, col_batches, jnp.asarray(lag_table(2 * segs)))
 
 
 def solution(mesh):

time: 153 us -> 141 us (0.922)
  waiting for transfers between devices: 61.6 us -> 50.3 us
  local copies, waits for them, and re-layouts: 4.63 us -> 2.88 us
    ppermute x4 -> x6, waiting for transfers between devices: 20.4 us -> 10.7 us  [partner(): cols = jnp.where(held, cols, lax.ppermute(cols, ('seg', 'blk'), pairs))]
    pallas_call x1 -> x2, Pallas kernels: 7.35 us -> 10.5 us  [the longest x1 6.37 us: spectra_inner(): pl.pallas_call(inner_kernel, grid=(channels // rows,), in_specs=[pl.Block...]
    pallas_call x1, Pallas kernels: 38.7 us -> 36.7 us  [correlate(): pl.pallas_call(functools.partial(correlate_kernel, pieces, len(col_batche...]
    ppermute x4 -> x6, starting transfers between devices: 5.14 us -> 5.98 us  [partner(): cols = jnp.where(held, cols, lax.ppermute(cols, ('seg', 'blk'), pairs))]
    select_n x4 -> x6, other arithmetic: 6.46 us -> 6.01 us  [partner(): cols = jnp.where(held, cols, lax.ppermute(cols, ('seg', 'blk'), pairs))]
  transfers between devices with their start and end apart: 21 -> 23, of which waited for: 12 -> 11; matrix products, arithmetic and copies ran while one was open for 3% -> 5% of each run, Pallas kernels for 2% -> 5%
where the time goes in v3:
time: 141 us; the launch traced here: 140 us
  Pallas kernels  50.5 us (36%)
  waiting for transfers between devices  50.3 us (36%)
  starting transfers between devices  28.9 us (20%)
  other arithmetic  7.24 us (5%)
  local copies, waits for them, and re-layouts  2.88 us (2%)
    ppermute x14, waiting for transfers between devices, shards(): moved = lax.ppermute(moved, 'seg', pairs)  39.6 us
    pallas_call x1, Pallas kernels, correlate(): pl.pallas_call(functools.partial(correlate_kernel, pieces, len(col_batche...  36.7 us
    ppermute x14, starting transfers between devices, shards(): moved = lax.ppermute(moved, 'seg', pairs)  16.3 us
    ppermute x6, waiting for transfers between devices, partner(): cols = jnp.where(held, cols, lax.ppermute(cols, ('seg', 'blk'), pairs))  10.7 us
    pallas_call x1, Pallas kernels, spectra_inner(): pl.pallas_call(inner_kernel, grid=(channels // rows,), in_specs=[pl.Block...  6.37 us
    select_n x6, other arithmetic, partner(): cols = jnp.where(held, cols, lax.ppermute(cols, ('seg', 'blk'), pairs))  6.01 us
    ppermute x6, starting transfers between devices, partner(): cols = jnp.where(held, cols, lax.ppermute(cols, ('seg', 'blk'), pairs))  5.98 us
    pallas_call x1, Pallas kernels, spectra_edge(): pl.pallas_call(edge_kernel, grid=(channels // rows,), in_specs=[pl.BlockS...  4.1 us
  transfers between devices with their start and end apart: 23, of which 11 were waited for; matrix products, arithmetic and copies ran while one was open for 5% of the time, Pallas kernels for 5%

profile of v3, /device:TPU:3, one launch (start us, length us, event | category | flops | bytes accessed | tf_op | source)
XLA Modules:
  0.0 140.2 jit_solution(5740327769960902940)
XLA Ops:
  0.0 3.3 %response.1 = (bf16[1280,256]{1,0:T(8,128)(2,1)}, bf16[1280,256]{1,0:T(8,128)(2,1)}) custom-call(f32[64]{0:T(128)} %taps_ref.1, f32[576,256]{1,0:T(8,128)} %constant.101.clone.table_ref), custom_call_target="tpu_custom_call" | custom-call | flops 213909504 | bytes 2097152 | tf_op jit(solution)/shard_map/response/pallas_call | solution.py:82
  4.3 1.3 collective-permute-start.1
  5.6 4.0 %collective-permute-start = (bf16[512,128]{1,0:T(8,128)(2,1)S(1)}, bf16[512,128]{1,0:T(8,128)(2,1)S(1)}, u32[]{:S(2)}, u32[]{:S(2)}) collective-permute-start(bf16[512,128]{1,0:T(8,128)(2,1)S(1)} %get-tuple-element.30), channel_id=1, source_target_pairs={{0,4},{4,8},{8,12},{12,16},{16,20},{20,24},{24,28},{1,5},{5,9},{9,... | collective-permute-start | bytes 393224 | tf_op jit(solution)/shard_map/ppermute | solution.py:322
  9.6 6.4 %spectra_inner.1 = (f32[256,512]{1,0:T(8,128)}, f32[256,512]{1,0:T(8,128)}) custom-call(bf16[512,2048]{1,0:T(8,128)(2,1)} %end_ref.1, bf16[512,256]{1,0:T(8,128)(2,1)} %constant.102.clone.window_ref, bf16[1280,256]{1,0:T(8,128)(2,1)} %get-tuple-element.20.high_ref.high0_ref.high1_ref, bf16[1280,256]{1,0:T(8,128)(2,1)} %get-tuple-element.21.low_ref.low0_ref.low1_ref), custom_call_target="tpu_custom_call" | custom-call | flops 2013265920 | bytes 6291456 | tf_op jit(solution)/shard_map/spectra_inner/pallas_call | solution.py:130
  16.7 4.1 %spectra_edge.1 = (f32[256,512]{1,0:T(8,128)}, bf16[256,512]{1,0:T(8,128)(2,1)}, f32[256,512]{1,0:T(8,128)}) custom-call(s32[1]{0:T(128)} %bitcast.last_ref, bf16[512,128]{1,0:T(8,128)(2,1)} %copy-done.2, bf16[512,2048]{1,0:T(8,128)(2,1)} %end_ref.1, bf16[512,2048]{1,0:T(8,128)(2,1)} %end_ref.1, bf16[512,128]{1,0:T(8,128)(2,1)} %copy-done.1, ...), custom_call_target="tpu_custom_call" | custom-call | flops 603979776 | bytes 4194304 | tf_op jit(solution)/shard_map/spectra_edge/pallas_call | solution.py:173
  22.1 2.8 %collective-permute-start.3 = (bf16[256,512]{1,0:T(8,128)(2,1)}, bf16[256,512]{1,0:T(8,128)(2,1)S(1)}, u32[]{:S(2)}, u32[]{:S(2)}) collective-permute-start(bf16[256,512]{1,0:T(8,128)(2,1)} %get-tuple-element.28.refs_0_), channel_id=1, source_target_pairs={{8,0},{16,8},{24,16},{28,24},{20,28},{12,20},{4,12},{0,4},{9,1},{1... | collective-permute-start | bytes 786440 | tf_op jit(solution)/shard_map/ppermute | solution.py:338
  25.8 16.8 %collective-permute-done.3.refs_2_ = bf16[256,512]{1,0:T(8,128)(2,1)S(1)} collective-permute-done((bf16[256,512]{1,0:T(8,128)(2,1)}, bf16[256,512]{1,0:T(8,128)(2,1)S(1)}, u32[]{:S(2)}, u32[]{:S(2)}) %collective-permute-start.3) | collective-permute-done | bytes 262176 | tf_op jit(solution)/shard_map/ppermute | solution.py:338
  46.8 1.5 %collective-permute-done.4.refs_3_ = bf16[256,512]{1,0:T(8,128)(2,1)S(1)} collective-permute-done((bf16[256,512]{1,0:T(8,128)(2,1)S(1)}, bf16[256,512]{1,0:T(8,128)(2,1)S(1)}, u32[]{:S(2)}, u32[]{:S(2)}) %collective-permute-start.4) | collective-permute-done | bytes 262176 | tf_op jit(solution)/shard_map/ppermute | solution.py:338
  48.3 1.8 %collective-permute-start.8 = (bf16[256,512]{1,0:T(8,128)(2,1)S(1)}, bf16[256,512]{1,0:T(8,128)(2,1)S(1)}, u32[]{:S(2)}, u32[]{:S(2)}) collective-permute-start(bf16[256,512]{1,0:T(8,128)(2,1)S(1)} %collective-permute-done.4.refs_3_), channel_id=1, source_target_pairs={{8,0},{16,8},{24,16},{28,24},{20,28},{12,20},{4,12},{0,4},{9,1},{1... | collective-permute-start | bytes 786440 | tf_op jit(solution)/shard_map/ppermute | solution.py:338
  50.2 6.5 %collective-permute-done.5.refs_4_ = bf16[256,512]{1,0:T(8,128)(2,1)S(1)} collective-permute-done((bf16[256,512]{1,0:T(8,128)(2,1)}, bf16[256,512]{1,0:T(8,128)(2,1)S(1)}, u32[]{:S(2)}, u32[]{:S(2)}) %collective-permute-start.5) | collective-permute-done | bytes 262176 | tf_op jit(solution)/shard_map/ppermute | solution.py:338
  56.7 1.5 %collective-permute-start.10 = (bf16[256,512]{1,0:T(8,128)(2,1)S(1)}, bf16[256,512]{1,0:T(8,128)(2,1)S(1)}, u32[]{:S(2)}, u32[]{:S(2)}) collective-permute-start(bf16[256,512]{1,0:T(8,128)(2,1)S(1)} %collective-permute-done.6.refs_5_), channel_id=1, source_target_pairs={{8,0},{16,8},{24,16},{28,24},{20,28},{12,20},{4,12},{0,4},{9,1},{1... | collective-permute-start | bytes 786440 | tf_op jit(solution)/shard_map/ppermute | solution.py:338
  59.7 1.7 %collective-permute-start.12 = (bf16[256,512]{1,0:T(8,128)(2,1)S(1)}, bf16[256,512]{1,0:T(8,128)(2,1)S(1)}, u32[]{:S(2)}, u32[]{:S(2)}) collective-permute-start(bf16[256,512]{1,0:T(8,128)(2,1)S(1)} %collective-permute-done.8.refs_7_), channel_id=1, source_target_pairs={{8,0},{16,8},{24,16},{28,24},{20,28},{12,20},{4,12},{0,4},{9,1},{1... | collective-permute-start | bytes 786440 | tf_op jit(solution)/shard_map/ppermute | solution.py:338
  62.2 3.0 %collective-permute-done.10.refs_9_ = bf16[256,512]{1,0:T(8,128)(2,1)S(1)} collective-permute-done((bf16[256,512]{1,0:T(8,128)(2,1)S(1)}, bf16[256,512]{1,0:T(8,128)(2,1)S(1)}, u32[]{:S(2)}, u32[]{:S(2)}) %collective-permute-start.10) | collective-permute-done | bytes 262176 | tf_op jit(solution)/shard_map/ppermute | solution.py:338
  65.2 1.8 %collective-permute-start.14 = (bf16[256,512]{1,0:T(8,128)(2,1)S(1)}, bf16[256,512]{1,0:T(8,128)(2,1)S(1)}, u32[]{:S(2)}, u32[]{:S(2)}) collective-permute-start(bf16[256,512]{1,0:T(8,128)(2,1)S(1)} %collective-permute-done.10.refs_9_), channel_id=1, source_target_pairs={{8,0},{16,8},{24,16},{28,24},{20,28},{12,20},{4,12},{0,4},{9,1},{1... | collective-permute-start | bytes 786440 | tf_op jit(solution)/shard_map/ppermute | solution.py:338
  68.3 2.4 %collective-permute-done.12.refs_11_ = bf16[256,512]{1,0:T(8,128)(2,1)S(1)} collective-permute-done((bf16[256,512]{1,0:T(8,128)(2,1)S(1)}, bf16[256,512]{1,0:T(8,128)(2,1)S(1)}, u32[]{:S(2)}, u32[]{:S(2)}) %collective-permute-start.12) | collective-permute-done | bytes 262176 | tf_op jit(solution)/shard_map/ppermute | solution.py:338
  71.9 4.5 %collective-permute-done.14.refs_13_ = bf16[256,512]{1,0:T(8,128)(2,1)S(1)} collective-permute-done((bf16[256,512]{1,0:T(8,128)(2,1)S(1)}, bf16[256,512]{1,0:T(8,128)(2,1)S(1)}, u32[]{:S(2)}, u32[]{:S(2)}) %collective-permute-start.14) | collective-permute-done | bytes 262176 | tf_op jit(solution)/shard_map/ppermute | solution.py:338
  76.4 1.9 %collective-permute-start.15 = (bf16[256,512]{1,0:T(8,128)(2,1)S(1)}, bf16[256,512]{1,0:T(8,128)(2,1)S(1)}, u32[]{:S(2)}, u32[]{:S(2)}) collective-permute-start(bf16[256,512]{1,0:T(8,128)(2,1)S(1)} %collective-permute-done.14.refs_13_), channel_id=1, source_target_pairs={{8,0},{16,8},{24,16},{28,24},{20,28},{12,20},{4,12},{0,4},{9,1},{1... | collective-permute-start | bytes 786440 | tf_op jit(solution)/shard_map/ppermute | solution.py:338
  78.4 3.6 %collective-permute-done.15.refs_14_ = bf16[256,512]{1,0:T(8,128)(2,1)S(1)} collective-permute-done((bf16[256,512]{1,0:T(8,128)(2,1)S(1)}, bf16[256,512]{1,0:T(8,128)(2,1)S(1)}, u32[]{:S(2)}, u32[]{:S(2)}) %collective-permute-start.15) | collective-permute-done | bytes 262176 | tf_op jit(solution)/shard_map/ppermute | solution.py:338
  82.9 1.3 collective-permute-start.18
  87.8 4.8 %collective-permute-done.20 = bf16[4,256,256]{2,1,0:T(8,128)(2,1)} collective-permute-done((bf16[4,256,256]{2,1,0:T(8,128)(2,1)}, bf16[4,256,256]{2,1,0:T(8,128)(2,1)}, u32[]{:S(2)}, u32[]{:S(2)}) %collective-permute-start.20) | collective-permute-done | bytes 524320 | tf_op jit(solution)/shard_map/ppermute | solution.py:310
  92.7 1.9 %broadcast_select_fusion.5.refs_17_ = bf16[4,256,256]{2,1,0:T(8,128)(2,1)} fusion(bf16[4,256,256]{2,1,0:T(8,128)(2,1)} %collective-permute-done.20, pred[]{:T(512)S(6)} %eq.34, bf16[4,256,256]{2,1,0:T(8,128)(2,1)S(1)} %collective-permute-done.19, bf16[1,256,256]{2,1,0:T(8,128)(2,1)S(1)} %dynamic-slice_bitcast_fusion, ...), kind=kLoop, calls=%fused_computation.7 | loop fusion | flops 1310720 | bytes 2097154 | tf_op jit(solution)/shard_map/jit(_where)/select_n | solution.py:310
  95.7 5.8 %collective-permute-done.22 = bf16[5,256,256]{2,1,0:T(8,128)(2,1)} collective-permute-done((bf16[5,256,256]{2,1,0:T(8,128)(2,1)S(1)}, bf16[5,256,256]{2,1,0:T(8,128)(2,1)}, u32[]{:S(2)}, u32[]{:S(2)}) %collective-permute-start.22) | collective-permute-done | bytes 655392 | tf_op jit(solution)/shard_map/ppermute | solution.py:310
  101.5 2.0 %broadcast_select_fusion.3.refs_18_ = bf16[5,256,256]{2,1,0:T(8,128)(2,1)} fusion(bf16[5,256,256]{2,1,0:T(8,128)(2,1)S(1)} %broadcast_select_fusion.2, bf16[5,256,256]{2,1,0:T(8,128)(2,1)} %collective-permute-done.22, pred[]{:T(512)S(6)} %eq.34), kind=kLoop, calls=%fused_computation.3 | loop fusion | flops 327680 | bytes 1966081 | tf_op jit(solution)/shard_map/jit(_where)/select_n | solution.py:310
  103.5 36.7 %correlate.1 = f32[512,256,128]{2,1,0:T(8,128)} custom-call(bf16[256,512]{1,0:T(8,128)(2,1)} %get-tuple-element.28.refs_0_, bf16[256,512]{1,0:T(8,128)(2,1)} %copy-done, bf16[256,512]{1,0:T(8,128)(2,1)} %copy-done.3, bf16[256,512]{1,0:T(8,128)(2,1)} %copy-done.4, bf16[256,512]{1,0:T(8,128)(2,1)} %copy-done.7, bf16[256,512]{1,0:T(8,128)(2,1)} %copy-done.6, ...), custom_call_target="tpu_custom_call" | custom-call | flops 25769803776 | bytes 67108864 | tf_op jit(solution)/shard_map/correlate/pallas_call | solution.py:259
  (86 shorter events, 18.3 us)
Async XLA Ops:
  4.3 11.7 %collective-permute-start.1 = (bf16[512,128]{1,0:T(8,128)(2,1)S(1)}, bf16[512,128]{1,0:T(8,128)(2,1)S(1)}, u32[]{:S(2)}, u32[]{:S(2)}) collective-permute-start(bf16[512,128]{1,0:T(8,128)(2,1)S(1)} %get-tuple-element.29), channel_id=1, source_target_pairs={{4,0},{8,4},{12,8},{16,12},{20,16},{24,20},{28,24},{5,1},{9,5},{13... | collective-permute-start | bytes 393224 | tf_op jit(solution)/shard_map/ppermute | solution.py:323
  5.6 10.4 %collective-permute-start = (bf16[512,128]{1,0:T(8,128)(2,1)S(1)}, bf16[512,128]{1,0:T(8,128)(2,1)S(1)}, u32[]{:S(2)}, u32[]{:S(2)}) collective-permute-start(bf16[512,128]{1,0:T(8,128)(2,1)S(1)} %get-tuple-element.30), channel_id=1, source_target_pairs={{0,4},{4,8},{8,12},{12,16},{16,20},{20,24},{24,28},{1,5},{5,9},{9,... | collective-permute-start | bytes 393224 | tf_op jit(solution)/shard_map/ppermute | solution.py:322
  20.8 22.9 %collective-permute-start.2 = (f32[256,512]{1,0:T(8,128)}, f32[256,512]{1,0:T(8,128)S(1)}, u32[]{:S(2)}, u32[]{:S(2)}) collective-permute-start(f32[256,512]{1,0:T(8,128)} %get-tuple-element.26), channel_id=1, source_target_pairs={{4,0},{8,4},{12,8},{16,12},{20,16},{24,20},{28,24},{5,1},{9,5},{13... | collective-permute-start | bytes 1572872 | tf_op jit(solution)/shard_map/ppermute | solution.py:327
  22.1 20.5 %collective-permute-start.3 = (bf16[256,512]{1,0:T(8,128)(2,1)}, bf16[256,512]{1,0:T(8,128)(2,1)S(1)}, u32[]{:S(2)}, u32[]{:S(2)}) collective-permute-start(bf16[256,512]{1,0:T(8,128)(2,1)} %get-tuple-element.28.refs_0_), channel_id=1, source_target_pairs={{8,0},{16,8},{24,16},{28,24},{20,28},{12,20},{4,12},{0,4},{9,1},{1... | collective-permute-start | bytes 786440 | tf_op jit(solution)/shard_map/ppermute | solution.py:338
  42.6 5.7 %collective-permute-start.4 = (bf16[256,512]{1,0:T(8,128)(2,1)S(1)}, bf16[256,512]{1,0:T(8,128)(2,1)S(1)}, u32[]{:S(2)}, u32[]{:S(2)}) collective-permute-start(bf16[256,512]{1,0:T(8,128)(2,1)S(1)} %collective-permute-done.3.refs_2_), channel_id=1, source_target_pairs={{8,0},{16,8},{24,16},{28,24},{20,28},{12,20},{4,12},{0,4},{9,1},{1... | collective-permute-start | bytes 786440 | tf_op jit(solution)/shard_map/ppermute | solution.py:338
  44.8 33.5 %copy-start = (bf16[256,512]{1,0:T(8,128)(2,1)}, bf16[256,512]{1,0:T(8,128)(2,1)S(1)}, u32[]{:S(2)}) copy-start(bf16[256,512]{1,0:T(8,128)(2,1)S(1)} %add_convert_fusion.refs_1_) | copy-start | bytes 786436
  44.9 13.3 %collective-permute-start.7 = (bf16[256,512]{1,0:T(8,128)(2,1)S(1)}, bf16[256,512]{1,0:T(8,128)(2,1)S(1)}, u32[]{:S(2)}, u32[]{:S(2)}) collective-permute-start(bf16[256,512]{1,0:T(8,128)(2,1)S(1)} %add_convert_fusion.refs_1_), channel_id=1, source_target_pairs={{0,8},{8,16},{16,24},{24,28},{28,20},{20,12},{12,4},{4,0},{1,9},{9... | collective-permute-start | bytes 786440 | tf_op jit(solution)/shard_map/ppermute | solution.py:338
  45.3 11.4 %collective-permute-start.6 = (bf16[256,512]{1,0:T(8,128)(2,1)S(1)}, bf16[256,512]{1,0:T(8,128)(2,1)S(1)}, u32[]{:S(2)}, u32[]{:S(2)}) collective-permute-start(bf16[256,512]{1,0:T(8,128)(2,1)S(1)} %add_convert_fusion.refs_1_), channel_id=1, source_target_pairs={{8,0},{16,8},{24,16},{28,24},{20,28},{12,20},{4,12},{0,4},{9,1},{1... | collective-permute-start | bytes 786440 | tf_op jit(solution)/shard_map/ppermute | solution.py:338
  46.4 10.3 %collective-permute-start.5 = (bf16[256,512]{1,0:T(8,128)(2,1)}, bf16[256,512]{1,0:T(8,128)(2,1)S(1)}, u32[]{:S(2)}, u32[]{:S(2)}) collective-permute-start(bf16[256,512]{1,0:T(8,128)(2,1)} %get-tuple-element.28.refs_0_), channel_id=1, source_target_pairs={{0,8},{8,16},{16,24},{24,28},{28,20},{20,12},{12,4},{4,0},{1,9},{9... | collective-permute-start | bytes 786440 | tf_op jit(solution)/shard_map/ppermute | solution.py:338
  48.3 11.3 %collective-permute-start.8 = (bf16[256,512]{1,0:T(8,128)(2,1)S(1)}, bf16[256,512]{1,0:T(8,128)(2,1)S(1)}, u32[]{:S(2)}, u32[]{:S(2)}) collective-permute-start(bf16[256,512]{1,0:T(8,128)(2,1)S(1)} %collective-permute-done.4.refs_3_), channel_id=1, source_target_pairs={{8,0},{16,8},{24,16},{28,24},{20,28},{12,20},{4,12},{0,4},{9,1},{1... | collective-permute-start | bytes 786440 | tf_op jit(solution)/shard_map/ppermute | solution.py:338
  56.7 5.5 %collective-permute-start.9 = (bf16[256,512]{1,0:T(8,128)(2,1)S(1)}, bf16[256,512]{1,0:T(8,128)(2,1)S(1)}, u32[]{:S(2)}, u32[]{:S(2)}) collective-permute-start(bf16[256,512]{1,0:T(8,128)(2,1)S(1)} %collective-permute-done.5.refs_4_), channel_id=1, source_target_pairs={{0,8},{8,16},{16,24},{24,28},{28,20},{20,12},{12,4},{4,0},{1,9},{9... | collective-permute-start | bytes 786440 | tf_op jit(solution)/shard_map/ppermute | solution.py:338
  56.7 8.5 %collective-permute-start.10 = (bf16[256,512]{1,0:T(8,128)(2,1)S(1)}, bf16[256,512]{1,0:T(8,128)(2,1)S(1)}, u32[]{:S(2)}, u32[]{:S(2)}) collective-permute-start(bf16[256,512]{1,0:T(8,128)(2,1)S(1)} %collective-permute-done.6.refs_5_), channel_id=1, source_target_pairs={{8,0},{16,8},{24,16},{28,24},{20,28},{12,20},{4,12},{0,4},{9,1},{1... | collective-permute-start | bytes 786440 | tf_op jit(solution)/shard_map/ppermute | solution.py:338
  58.2 24.6 %collective-permute-start.17 = (bf16[7,256,256]{2,1,0:T(8,128)(2,1)S(1)}, bf16[7,256,256]{2,1,0:T(8,128)(2,1)S(1)}, u32[]{:S(2)}, u32[]{:S(2)}) collective-permute-start(bf16[7,256,256]{2,1,0:T(8,128)(2,1)S(1)} %bitcast_dynamic-update-slice_fusion.5), channel_id=1, source_target_pairs={{0,2},{4,6},{9,11},{13,15},{18,16},{22,20},{27,25},{31,29}} | collective-permute-start | bytes 2752520 | tf_op jit(solution)/shard_map/ppermute | solution.py:310
  59.0 8.6 %collective-permute-start.11 = (bf16[256,512]{1,0:T(8,128)(2,1)S(1)}, bf16[256,512]{1,0:T(8,128)(2,1)S(1)}, u32[]{:S(2)}, u32[]{:S(2)}) collective-permute-start(bf16[256,512]{1,0:T(8,128)(2,1)S(1)} %collective-permute-done.7.refs_6_), channel_id=1, source_target_pairs={{0,8},{8,16},{16,24},{24,28},{28,20},{20,12},{12,4},{4,0},{1,9},{9... | collective-permute-start | bytes 786440 | tf_op jit(solution)/shard_map/ppermute | solution.py:338
  59.7 11.1 %collective-permute-start.12 = (bf16[256,512]{1,0:T(8,128)(2,1)S(1)}, bf16[256,512]{1,0:T(8,128)(2,1)S(1)}, u32[]{:S(2)}, u32[]{:S(2)}) collective-permute-start(bf16[256,512]{1,0:T(8,128)(2,1)S(1)} %collective-permute-done.8.refs_7_), channel_id=1, source_target_pairs={{8,0},{16,8},{24,16},{28,24},{20,28},{12,20},{4,12},{0,4},{9,1},{1... | collective-permute-start | bytes 786440 | tf_op jit(solution)/shard_map/ppermute | solution.py:338
  62.2 16.1 %collective-permute-start.13 = (bf16[256,512]{1,0:T(8,128)(2,1)S(1)}, bf16[256,512]{1,0:T(8,128)(2,1)S(1)}, u32[]{:S(2)}, u32[]{:S(2)}) collective-permute-start(bf16[256,512]{1,0:T(8,128)(2,1)S(1)} %collective-permute-done.9.refs_8_), channel_id=1, source_target_pairs={{0,8},{8,16},{16,24},{24,28},{28,20},{20,12},{12,4},{4,0},{1,9},{9... | collective-permute-start | bytes 786440 | tf_op jit(solution)/shard_map/ppermute | solution.py:338
  65.2 11.2 %collective-permute-start.14 = (bf16[256,512]{1,0:T(8,128)(2,1)S(1)}, bf16[256,512]{1,0:T(8,128)(2,1)S(1)}, u32[]{:S(2)}, u32[]{:S(2)}) collective-permute-start(bf16[256,512]{1,0:T(8,128)(2,1)S(1)} %collective-permute-done.10.refs_9_), channel_id=1, source_target_pairs={{8,0},{16,8},{24,16},{28,24},{20,28},{12,20},{4,12},{0,4},{9,1},{1... | collective-permute-start | bytes 786440 | tf_op jit(solution)/shard_map/ppermute | solution.py:338
  67.6 16.6 %collective-permute-start.19 = (bf16[4,256,256]{2,1,0:T(8,128)(2,1)S(1)}, bf16[4,256,256]{2,1,0:T(8,128)(2,1)S(1)}, u32[]{:S(2)}, u32[]{:S(2)}) collective-permute-start(bf16[4,256,256]{2,1,0:T(8,128)(2,1)S(1)} %pad_maximum_fusion), channel_id=1, source_target_pairs={{0,2},{4,6},{9,11},{13,15},{18,16},{22,20},{27,25},{31,29}} | collective-permute-start | bytes 1572872 | tf_op jit(solution)/shard_map/ppermute | solution.py:310
  70.8 11.2 %collective-permute-start.16 = (bf16[256,512]{1,0:T(8,128)(2,1)S(1)}, bf16[256,512]{1,0:T(8,128)(2,1)S(1)}, u32[]{:S(2)}, u32[]{:S(2)}) collective-permute-start(bf16[256,512]{1,0:T(8,128)(2,1)S(1)} %collective-permute-done.11.refs_10_), channel_id=1, source_target_pairs={{0,8},{8,16},{16,24},{24,28},{28,20},{20,12},{12,4},{4,0},{1,9},{9... | collective-permute-start | bytes 786440 | tf_op jit(solution)/shard_map/ppermute | solution.py:338
  76.4 5.6 %collective-permute-start.15 = (bf16[256,512]{1,0:T(8,128)(2,1)S(1)}, bf16[256,512]{1,0:T(8,128)(2,1)S(1)}, u32[]{:S(2)}, u32[]{:S(2)}) collective-permute-start(bf16[256,512]{1,0:T(8,128)(2,1)S(1)} %collective-permute-done.14.refs_13_), channel_id=1, source_target_pairs={{8,0},{16,8},{24,16},{28,24},{20,28},{12,20},{4,12},{0,4},{9,1},{1... | collective-permute-start | bytes 786440 | tf_op jit(solution)/shard_map/ppermute | solution.py:338
  82.0 4.4 %collective-permute-start.21 = (bf16[5,256,256]{2,1,0:T(8,128)(2,1)S(1)}, bf16[5,256,256]{2,1,0:T(8,128)(2,1)S(1)}, u32[]{:S(2)}, u32[]{:S(2)}) collective-permute-start(bf16[5,256,256]{2,1,0:T(8,128)(2,1)S(1)} %bitcast_dynamic-update-slice_fusion), channel_id=1, source_target_pairs={{0,2},{4,6},{9,11},{13,15},{18,16},{22,20},{27,25},{31,29}} | collective-permute-start | bytes 1966088 | tf_op jit(solution)/shard_map/ppermute | solution.py:310
  82.9 11.7 %collective-permute-start.18 = (bf16[7,256,256]{2,1,0:T(8,128)(2,1)S(1)}, bf16[7,256,256]{2,1,0:T(8,128)(2,1)S(1)}, u32[]{:S(2)}, u32[]{:S(2)}) collective-permute-start(bf16[7,256,256]{2,1,0:T(8,128)(2,1)S(1)} %broadcast_select_fusion), channel_id=1, source_target_pairs={{0,1},{2,3},{4,5},{6,7},{9,8},{11,10},{13,12},{15,14},{18,19},{16,... | collective-permute-start | bytes 2752520 | tf_op jit(solution)/shard_map/ppermute | solution.py:310
  85.1 7.5 %collective-permute-start.20 = (bf16[4,256,256]{2,1,0:T(8,128)(2,1)}, bf16[4,256,256]{2,1,0:T(8,128)(2,1)}, u32[]{:S(2)}, u32[]{:S(2)}) collective-permute-start(bf16[4,256,256]{2,1,0:T(8,128)(2,1)} %broadcast_select_fusion.4), channel_id=1, source_target_pairs={{0,1},{2,3},{4,5},{6,7},{9,8},{11,10},{13,12},{15,14},{18,19},{16,... | collective-permute-start | bytes 1572872 | tf_op jit(solution)/shard_map/ppermute | solution.py:310
  86.5 15.0 %collective-permute-start.22 = (bf16[5,256,256]{2,1,0:T(8,128)(2,1)S(1)}, bf16[5,256,256]{2,1,0:T(8,128)(2,1)}, u32[]{:S(2)}, u32[]{:S(2)}) collective-permute-start(bf16[5,256,256]{2,1,0:T(8,128)(2,1)S(1)} %broadcast_select_fusion.2), channel_id=1, source_target_pairs={{0,1},{2,3},{4,5},{6,7},{9,8},{11,10},{13,12},{15,14},{18,19},{16,... | collective-permute-start | bytes 1966088 | tf_op jit(solution)/shard_map/ppermute | solution.py:310
  (16 other events, 195.4 us)

commit v4 on v3

--- a/solution.py
+++ b/solution.py
@@ -125,7 +125,7 @@
 
 def spectra_inner(own, tables):
     channels, own_time = own.shape
-    rows = min(LANE, channels)
+    rows = min(2 * LANE, channels)
     whole = lambda i: (0, 0)
     return pl.pallas_call(
         inner_kernel,
@@ -332,10 +332,12 @@
     longer, shorter = segs // 2, segs - 1 - segs // 2
     early, middle, late = [even, odd], [], []
     chains = ((even, backward, longer, 0), (even_later, forward, shorter, 1),
-              (odd, backward, longer, 1), (odd, forward, shorter, 1))
+              (odd, backward, shorter, 1), (odd, forward, longer, 1))
     for moved, pairs, count, lag in chains:
         for step in range(1, count + 1):
             moved = lax.ppermute(moved, "seg", pairs)
+            if lag == 0 and step == 1:
+                moved = lax.optimization_barrier((moved, odd))[0]
             if step + lag <= segs // 4:
                 early.append(moved)
             else:

time: 141 us -> 139 us (0.986)
  starting transfers between devices: 28.9 us -> 26.8 us
    ppermute x14, waiting for transfers between devices: 39.6 us -> 27.9 us  [shards(): moved = lax.ppermute(moved, 'seg', pairs)]
    ppermute x1, waiting for transfers between devices: 0.01 us -> 11.1 us  [shards(): following = lax.ppermute(first, 'seg', downward)]
    ppermute x14, starting transfers between devices: 16.3 us -> 14.3 us  [shards(): moved = lax.ppermute(moved, 'seg', pairs)]
  transfers between devices with their start and end apart: 23 -> 23, of which waited for: 11 -> 14; matrix products, arithmetic and copies ran while one was open for 5% -> 5% of each run, Pallas kernels for 5% -> 4%
where the time goes in v4:
time: 139 us; the launch traced here: 138 us
  waiting for transfers between devices  50.7 us (36%)
  Pallas kernels  50.1 us (36%)
  starting transfers between devices  26.8 us (19%)
  other arithmetic  7.24 us (5%)
  local copies, waits for them, and re-layouts  2.89 us (2%)
    pallas_call x1, Pallas kernels, correlate(): pl.pallas_call(functools.partial(correlate_kernel, pieces, len(col_batche...  36.7 us
    ppermute x14, waiting for transfers between devices, shards(): moved = lax.ppermute(moved, 'seg', pairs)  27.9 us
    ppermute x14, starting transfers between devices, shards(): moved = lax.ppermute(moved, 'seg', pairs)  14.3 us
    ppermute x6, waiting for transfers between devices, partner(): cols = jnp.where(held, cols, lax.ppermute(cols, ('seg', 'blk'), pairs))  11.7 us
    ppermute x1, waiting for transfers between devices, shards(): following = lax.ppermute(first, 'seg', downward)  11.1 us
    select_n x6, other arithmetic, partner(): cols = jnp.where(held, cols, lax.ppermute(cols, ('seg', 'blk'), pairs))  6.01 us
    pallas_call x1, Pallas kernels, spectra_inner(): pl.pallas_call(inner_kernel, grid=(channels // rows,), in_specs=[pl.Block...  5.99 us
    ppermute x6, starting transfers between devices, partner(): cols = jnp.where(held, cols, lax.ppermute(cols, ('seg', 'blk'), pairs))  5.97 us
  transfers between devices with their start and end apart: 23, of which 14 were waited for; matrix products, arithmetic and copies ran while one was open for 5% of the time, Pallas kernels for 4%

profile of v4, /device:TPU:3, one launch (start us, length us, event | category | flops | bytes accessed | tf_op | source)
XLA Modules:
  0.0 138.2 jit_solution(14625837205759791684)
XLA Ops:
  0.0 3.3 %response.1 = (bf16[1280,256]{1,0:T(8,128)(2,1)}, bf16[1280,256]{1,0:T(8,128)(2,1)}) custom-call(f32[64]{0:T(128)} %taps_ref.1, f32[576,256]{1,0:T(8,128)} %constant.101.clone.table_ref), custom_call_target="tpu_custom_call" | custom-call | flops 213909504 | bytes 2097152 | tf_op jit(solution)/shard_map/response/pallas_call | solution.py:82
  5.6 4.0 %collective-permute-start = (bf16[512,128]{1,0:T(8,128)(2,1)S(1)}, bf16[512,128]{1,0:T(8,128)(2,1)S(1)}, u32[]{:S(2)}, u32[]{:S(2)}) collective-permute-start(bf16[512,128]{1,0:T(8,128)(2,1)S(1)} %get-tuple-element.32), channel_id=1, source_target_pairs={{0,4},{4,8},{8,12},{12,16},{16,20},{20,24},{24,28},{1,5},{5,9},{9,... | collective-permute-start | bytes 393224 | tf_op jit(solution)/shard_map/ppermute | solution.py:322
  9.6 6.0 %spectra_inner.1 = (f32[256,512]{1,0:T(8,128)}, f32[256,512]{1,0:T(8,128)}) custom-call(bf16[512,2048]{1,0:T(8,128)(2,1)} %end_ref.1, bf16[512,256]{1,0:T(8,128)(2,1)} %constant.102.clone.window_ref, bf16[1280,256]{1,0:T(8,128)(2,1)} %get-tuple-element.21.high_ref.high0_ref.high1_ref, bf16[1280,256]{1,0:T(8,128)(2,1)} %get-tuple-element.22.low_ref.low0_ref.low1_ref), custom_call_target="tpu_custom_call" | custom-call | flops 2013265920 | bytes 6291456 | tf_op jit(solution)/shard_map/spectra_inner/pallas_call | solution.py:130
  16.3 4.1 %spectra_edge.1 = (f32[256,512]{1,0:T(8,128)}, bf16[256,512]{1,0:T(8,128)(2,1)}, f32[256,512]{1,0:T(8,128)}) custom-call(s32[1]{0:T(128)} %bitcast.last_ref, bf16[512,128]{1,0:T(8,128)(2,1)} %copy-done.2, bf16[512,2048]{1,0:T(8,128)(2,1)} %end_ref.1, bf16[512,2048]{1,0:T(8,128)(2,1)} %end_ref.1, bf16[512,128]{1,0:T(8,128)(2,1)} %copy-done.1, ...), custom_call_target="tpu_custom_call" | custom-call | flops 603979776 | bytes 4194304 | tf_op jit(solution)/shard_map/spectra_edge/pallas_call | solution.py:173
  21.7 2.8 %collective-permute-start.3 = (bf16[256,512]{1,0:T(8,128)(2,1)}, bf16[256,512]{1,0:T(8,128)(2,1)S(1)}, u32[]{:S(2)}, u32[]{:S(2)}) collective-permute-start(bf16[256,512]{1,0:T(8,128)(2,1)} %get-tuple-element.30.refs_0_), channel_id=1, source_target_pairs={{8,0},{16,8},{24,16},{28,24},{20,28},{12,20},{4,12},{0,4},{9,1},{1... | collective-permute-start | bytes 786440 | tf_op jit(solution)/shard_map/ppermute | solution.py:338
  24.5 11.1 %collective-permute-done.2 = f32[256,512]{1,0:T(8,128)S(1)} collective-permute-done((f32[256,512]{1,0:T(8,128)}, f32[256,512]{1,0:T(8,128)S(1)}, u32[]{:S(2)}, u32[]{:S(2)}) %collective-permute-start.2) | collective-permute-done | bytes 524320 | tf_op jit(solution)/shard_map/ppermute | solution.py:327
  38.1 4.1 %collective-permute-done.3.refs_2_ = bf16[256,512]{1,0:T(8,128)(2,1)S(1)} collective-permute-done((bf16[256,512]{1,0:T(8,128)(2,1)}, bf16[256,512]{1,0:T(8,128)(2,1)S(1)}, u32[]{:S(2)}, u32[]{:S(2)}) %collective-permute-start.3) | collective-permute-done | bytes 262176 | tf_op jit(solution)/shard_map/ppermute | solution.py:338
  45.8 2.1 %collective-permute-done.4.refs_3_ = bf16[256,512]{1,0:T(8,128)(2,1)S(1)} collective-permute-done((bf16[256,512]{1,0:T(8,128)(2,1)S(1)}, bf16[256,512]{1,0:T(8,128)(2,1)S(1)}, u32[]{:S(2)}, u32[]{:S(2)}) %collective-permute-start.4) | collective-permute-done | bytes 262176 | tf_op jit(solution)/shard_map/ppermute | solution.py:338
  47.9 1.8 %collective-permute-start.8 = (bf16[256,512]{1,0:T(8,128)(2,1)S(1)}, bf16[256,512]{1,0:T(8,128)(2,1)S(1)}, u32[]{:S(2)}, u32[]{:S(2)}) collective-permute-start(bf16[256,512]{1,0:T(8,128)(2,1)S(1)} %collective-permute-done.4.refs_3_), channel_id=1, source_target_pairs={{8,0},{16,8},{24,16},{28,24},{20,28},{12,20},{4,12},{0,4},{9,1},{1... | collective-permute-start | bytes 786440 | tf_op jit(solution)/shard_map/ppermute | solution.py:338
  51.5 2.0 %collective-permute-done.6.refs_5_ = bf16[256,512]{1,0:T(8,128)(2,1)S(1)} collective-permute-done((bf16[256,512]{1,0:T(8,128)(2,1)S(1)}, bf16[256,512]{1,0:T(8,128)(2,1)S(1)}, u32[]{:S(2)}, u32[]{:S(2)}) %collective-permute-start.6) | collective-permute-done | bytes 262176 | tf_op jit(solution)/shard_map/ppermute | solution.py:338
  54.3 1.9 %collective-permute-start.10 = (bf16[256,512]{1,0:T(8,128)(2,1)S(1)}, bf16[256,512]{1,0:T(8,128)(2,1)S(1)}, u32[]{:S(2)}, u32[]{:S(2)}) collective-permute-start(bf16[256,512]{1,0:T(8,128)(2,1)S(1)} %collective-permute-done.6.refs_5_), channel_id=1, source_target_pairs={{8,0},{16,8},{24,16},{28,24},{20,28},{12,20},{4,12},{0,4},{9,1},{1... | collective-permute-start | bytes 786440 | tf_op jit(solution)/shard_map/ppermute | solution.py:338
  56.1 3.0 %collective-permute-done.8.refs_7_ = bf16[256,512]{1,0:T(8,128)(2,1)S(1)} collective-permute-done((bf16[256,512]{1,0:T(8,128)(2,1)S(1)}, bf16[256,512]{1,0:T(8,128)(2,1)S(1)}, u32[]{:S(2)}, u32[]{:S(2)}) %collective-permute-start.8) | collective-permute-done | bytes 262176 | tf_op jit(solution)/shard_map/ppermute | solution.py:338
  59.1 1.9 %collective-permute-start.12 = (bf16[256,512]{1,0:T(8,128)(2,1)S(1)}, bf16[256,512]{1,0:T(8,128)(2,1)S(1)}, u32[]{:S(2)}, u32[]{:S(2)}) collective-permute-start(bf16[256,512]{1,0:T(8,128)(2,1)S(1)} %collective-permute-done.8.refs_7_), channel_id=1, source_target_pairs={{8,0},{16,8},{24,16},{28,24},{20,28},{12,20},{4,12},{0,4},{9,1},{1... | collective-permute-start | bytes 786440 | tf_op jit(solution)/shard_map/ppermute | solution.py:338
  62.0 2.7 %collective-permute-done.10.refs_9_ = bf16[256,512]{1,0:T(8,128)(2,1)S(1)} collective-permute-done((bf16[256,512]{1,0:T(8,128)(2,1)S(1)}, bf16[256,512]{1,0:T(8,128)(2,1)S(1)}, u32[]{:S(2)}, u32[]{:S(2)}) %collective-permute-start.10) | collective-permute-done | bytes 262176 | tf_op jit(solution)/shard_map/ppermute | solution.py:338
  64.8 1.9 %collective-permute-start.14 = (bf16[256,512]{1,0:T(8,128)(2,1)S(1)}, bf16[256,512]{1,0:T(8,128)(2,1)S(1)}, u32[]{:S(2)}, u32[]{:S(2)}) collective-permute-start(bf16[256,512]{1,0:T(8,128)(2,1)S(1)} %collective-permute-done.10.refs_9_), channel_id=1, source_target_pairs={{8,0},{16,8},{24,16},{28,24},{20,28},{12,20},{4,12},{0,4},{9,1},{1... | collective-permute-start | bytes 786440 | tf_op jit(solution)/shard_map/ppermute | solution.py:338
  66.7 3.6 %collective-permute-done.12.refs_11_ = bf16[256,512]{1,0:T(8,128)(2,1)S(1)} collective-permute-done((bf16[256,512]{1,0:T(8,128)(2,1)S(1)}, bf16[256,512]{1,0:T(8,128)(2,1)S(1)}, u32[]{:S(2)}, u32[]{:S(2)}) %collective-permute-start.12) | collective-permute-done | bytes 262176 | tf_op jit(solution)/shard_map/ppermute | solution.py:338
  71.1 2.1 %collective-permute-done.15.refs_14_ = bf16[256,512]{1,0:T(8,128)(2,1)S(1)} collective-permute-done((bf16[256,512]{1,0:T(8,128)(2,1)S(1)}, bf16[256,512]{1,0:T(8,128)(2,1)S(1)}, u32[]{:S(2)}, u32[]{:S(2)}) %collective-permute-start.15) | collective-permute-done | bytes 262176 | tf_op jit(solution)/shard_map/ppermute | solution.py:338
  73.3 2.7 %collective-permute-done.14.refs_13_ = bf16[256,512]{1,0:T(8,128)(2,1)S(1)} collective-permute-done((bf16[256,512]{1,0:T(8,128)(2,1)S(1)}, bf16[256,512]{1,0:T(8,128)(2,1)S(1)}, u32[]{:S(2)}, u32[]{:S(2)}) %collective-permute-start.14) | collective-permute-done | bytes 262176 | tf_op jit(solution)/shard_map/ppermute | solution.py:338
  76.0 3.0 %collective-permute-done.16.refs_15_ = bf16[256,512]{1,0:T(8,128)(2,1)S(1)} collective-permute-done((bf16[256,512]{1,0:T(8,128)(2,1)S(1)}, bf16[256,512]{1,0:T(8,128)(2,1)S(1)}, u32[]{:S(2)}, u32[]{:S(2)}) %collective-permute-start.16) | collective-permute-done | bytes 262176 | tf_op jit(solution)/shard_map/ppermute | solution.py:338
  84.9 6.1 %collective-permute-done.20 = bf16[4,256,256]{2,1,0:T(8,128)(2,1)} collective-permute-done((bf16[4,256,256]{2,1,0:T(8,128)(2,1)}, bf16[4,256,256]{2,1,0:T(8,128)(2,1)}, u32[]{:S(2)}, u32[]{:S(2)}) %collective-permute-start.20) | collective-permute-done | bytes 524320 | tf_op jit(solution)/shard_map/ppermute | solution.py:310
  91.0 1.9 %broadcast_select_fusion.5.refs_17_ = bf16[4,256,256]{2,1,0:T(8,128)(2,1)} fusion(bf16[4,256,256]{2,1,0:T(8,128)(2,1)} %collective-permute-done.20, pred[]{:T(512)S(6)} %eq.34, bf16[4,256,256]{2,1,0:T(8,128)(2,1)S(1)} %collective-permute-done.19, bf16[1,256,256]{2,1,0:T(8,128)(2,1)S(1)} %dynamic-slice_bitcast_fusion, ...), kind=kLoop, calls=%fused_computation.7 | loop fusion | flops 1310720 | bytes 2097154 | tf_op jit(solution)/shard_map/jit(_where)/select_n | solution.py:310
  94.0 5.6 %collective-permute-done.22 = bf16[5,256,256]{2,1,0:T(8,128)(2,1)} collective-permute-done((bf16[5,256,256]{2,1,0:T(8,128)(2,1)S(1)}, bf16[5,256,256]{2,1,0:T(8,128)(2,1)}, u32[]{:S(2)}, u32[]{:S(2)}) %collective-permute-start.22) | collective-permute-done | bytes 655392 | tf_op jit(solution)/shard_map/ppermute | solution.py:310
  99.5 2.0 %broadcast_select_fusion.3.refs_18_ = bf16[5,256,256]{2,1,0:T(8,128)(2,1)} fusion(bf16[5,256,256]{2,1,0:T(8,128)(2,1)S(1)} %broadcast_select_fusion.2, bf16[5,256,256]{2,1,0:T(8,128)(2,1)} %collective-permute-done.22, pred[]{:T(512)S(6)} %eq.34), kind=kLoop, calls=%fused_computation.3 | loop fusion | flops 327680 | bytes 1966081 | tf_op jit(solution)/shard_map/jit(_where)/select_n | solution.py:310
  101.5 36.7 %correlate.1 = f32[512,256,128]{2,1,0:T(8,128)} custom-call(bf16[256,512]{1,0:T(8,128)(2,1)} %get-tuple-element.30.refs_0_, bf16[256,512]{1,0:T(8,128)(2,1)} %copy-done, bf16[256,512]{1,0:T(8,128)(2,1)} %copy-done.3, bf16[256,512]{1,0:T(8,128)(2,1)} %copy-done.5, bf16[256,512]{1,0:T(8,128)(2,1)} %copy-done.6, bf16[256,512]{1,0:T(8,128)(2,1)} %copy-done.7, ...), custom_call_target="tpu_custom_call" | custom-call | flops 25769803776 | bytes 67108864 | tf_op jit(solution)/shard_map/correlate/pallas_call | solution.py:259
  (86 shorter events, 21.4 us)
Async XLA Ops:
  4.3 11.3 %collective-permute-start.1 = (bf16[512,128]{1,0:T(8,128)(2,1)S(1)}, bf16[512,128]{1,0:T(8,128)(2,1)S(1)}, u32[]{:S(2)}, u32[]{:S(2)}) collective-permute-start(bf16[512,128]{1,0:T(8,128)(2,1)S(1)} %get-tuple-element.31), channel_id=1, source_target_pairs={{4,0},{8,4},{12,8},{16,12},{20,16},{24,20},{28,24},{5,1},{9,5},{13... | collective-permute-start | bytes 393224 | tf_op jit(solution)/shard_map/ppermute | solution.py:323
  5.6 10.0 %collective-permute-start = (bf16[512,128]{1,0:T(8,128)(2,1)S(1)}, bf16[512,128]{1,0:T(8,128)(2,1)S(1)}, u32[]{:S(2)}, u32[]{:S(2)}) collective-permute-start(bf16[512,128]{1,0:T(8,128)(2,1)S(1)} %get-tuple-element.32), channel_id=1, source_target_pairs={{0,4},{4,8},{8,12},{12,16},{16,20},{20,24},{24,28},{1,5},{5,9},{9,... | collective-permute-start | bytes 393224 | tf_op jit(solution)/shard_map/ppermute | solution.py:322
  20.4 15.2 %collective-permute-start.2 = (f32[256,512]{1,0:T(8,128)}, f32[256,512]{1,0:T(8,128)S(1)}, u32[]{:S(2)}, u32[]{:S(2)}) collective-permute-start(f32[256,512]{1,0:T(8,128)} %get-tuple-element.27), channel_id=1, source_target_pairs={{4,0},{8,4},{12,8},{16,12},{20,16},{24,20},{28,24},{5,1},{9,5},{13... | collective-permute-start | bytes 1572872 | tf_op jit(solution)/shard_map/ppermute | solution.py:327
  21.7 20.5 %collective-permute-start.3 = (bf16[256,512]{1,0:T(8,128)(2,1)}, bf16[256,512]{1,0:T(8,128)(2,1)S(1)}, u32[]{:S(2)}, u32[]{:S(2)}) collective-permute-start(bf16[256,512]{1,0:T(8,128)(2,1)} %get-tuple-element.30.refs_0_), channel_id=1, source_target_pairs={{8,0},{16,8},{24,16},{28,24},{20,28},{12,20},{4,12},{0,4},{9,1},{1... | collective-permute-start | bytes 786440 | tf_op jit(solution)/shard_map/ppermute | solution.py:338
  36.8 36.5 %copy-start = (bf16[256,512]{1,0:T(8,128)(2,1)}, bf16[256,512]{1,0:T(8,128)(2,1)S(1)}, u32[]{:S(2)}) copy-start(bf16[256,512]{1,0:T(8,128)(2,1)S(1)} %add_convert_fusion.refs_1_) | copy-start | bytes 786436
  36.8 14.6 %collective-permute-start.7 = (bf16[256,512]{1,0:T(8,128)(2,1)S(1)}, bf16[256,512]{1,0:T(8,128)(2,1)S(1)}, u32[]{:S(2)}, u32[]{:S(2)}) collective-permute-start(bf16[256,512]{1,0:T(8,128)(2,1)S(1)} %add_convert_fusion.refs_1_), channel_id=1, source_target_pairs={{0,8},{8,16},{16,24},{24,28},{28,20},{20,12},{12,4},{4,0},{1,9},{9... | collective-permute-start | bytes 786440 | tf_op jit(solution)/shard_map/ppermute | solution.py:338
  42.2 5.7 %collective-permute-start.4 = (bf16[256,512]{1,0:T(8,128)(2,1)S(1)}, bf16[256,512]{1,0:T(8,128)(2,1)S(1)}, u32[]{:S(2)}, u32[]{:S(2)}) collective-permute-start(bf16[256,512]{1,0:T(8,128)(2,1)S(1)} %collective-permute-done.3.refs_2_), channel_id=1, source_target_pairs={{8,0},{16,8},{24,16},{28,24},{20,28},{12,20},{4,12},{0,4},{9,1},{1... | collective-permute-start | bytes 786440 | tf_op jit(solution)/shard_map/ppermute | solution.py:338
  43.3 8.1 %collective-permute-start.5 = (bf16[256,512]{1,0:T(8,128)(2,1)}, bf16[256,512]{1,0:T(8,128)(2,1)S(1)}, u32[]{:S(2)}, u32[]{:S(2)}) collective-permute-start(bf16[256,512]{1,0:T(8,128)(2,1)} %get-tuple-element.30.refs_0_), channel_id=1, source_target_pairs={{0,8},{8,16},{16,24},{24,28},{28,20},{20,12},{12,4},{4,0},{1,9},{9... | collective-permute-start | bytes 786440 | tf_op jit(solution)/shard_map/ppermute | solution.py:338
  44.6 8.9 %collective-permute-start.6 = (bf16[256,512]{1,0:T(8,128)(2,1)S(1)}, bf16[256,512]{1,0:T(8,128)(2,1)S(1)}, u32[]{:S(2)}, u32[]{:S(2)}) collective-permute-start(bf16[256,512]{1,0:T(8,128)(2,1)S(1)} %add_convert_fusion.refs_1_), channel_id=1, source_target_pairs={{8,0},{16,8},{24,16},{28,24},{20,28},{12,20},{4,12},{0,4},{9,1},{1... | collective-permute-start | bytes 786440 | tf_op jit(solution)/shard_map/ppermute | solution.py:338
  47.9 11.2 %collective-permute-start.8 = (bf16[256,512]{1,0:T(8,128)(2,1)S(1)}, bf16[256,512]{1,0:T(8,128)(2,1)S(1)}, u32[]{:S(2)}, u32[]{:S(2)}) collective-permute-start(bf16[256,512]{1,0:T(8,128)(2,1)S(1)} %collective-permute-done.4.refs_3_), channel_id=1, source_target_pairs={{8,0},{16,8},{24,16},{28,24},{20,28},{12,20},{4,12},{0,4},{9,1},{1... | collective-permute-start | bytes 786440 | tf_op jit(solution)/shard_map/ppermute | solution.py:338
  51.4 9.6 %collective-permute-start.9 = (bf16[256,512]{1,0:T(8,128)(2,1)S(1)}, bf16[256,512]{1,0:T(8,128)(2,1)S(1)}, u32[]{:S(2)}, u32[]{:S(2)}) collective-permute-start(bf16[256,512]{1,0:T(8,128)(2,1)S(1)} %collective-permute-done.5.refs_4_), channel_id=1, source_target_pairs={{0,8},{8,16},{16,24},{24,28},{28,20},{20,12},{12,4},{4,0},{1,9},{9... | collective-permute-start | bytes 786440 | tf_op jit(solution)/shard_map/ppermute | solution.py:338
  51.4 10.6 %collective-permute-start.11 = (bf16[256,512]{1,0:T(8,128)(2,1)S(1)}, bf16[256,512]{1,0:T(8,128)(2,1)S(1)}, u32[]{:S(2)}, u32[]{:S(2)}) collective-permute-start(bf16[256,512]{1,0:T(8,128)(2,1)S(1)} %collective-permute-done.7.refs_6_), channel_id=1, source_target_pairs={{0,8},{8,16},{16,24},{24,28},{28,20},{20,12},{12,4},{4,0},{1,9},{9... | collective-permute-start | bytes 786440 | tf_op jit(solution)/shard_map/ppermute | solution.py:338
  53.5 26.3 %collective-permute-start.17 = (bf16[7,256,256]{2,1,0:T(8,128)(2,1)S(1)}, bf16[7,256,256]{2,1,0:T(8,128)(2,1)S(1)}, u32[]{:S(2)}, u32[]{:S(2)}) collective-permute-start(bf16[7,256,256]{2,1,0:T(8,128)(2,1)S(1)} %bitcast_dynamic-update-slice_fusion.5), channel_id=1, source_target_pairs={{0,2},{4,6},{9,11},{13,15},{18,16},{22,20},{27,25},{31,29}} | collective-permute-start | bytes 2752520 | tf_op jit(solution)/shard_map/ppermute | solution.py:310
  54.3 10.5 %collective-permute-start.10 = (bf16[256,512]{1,0:T(8,128)(2,1)S(1)}, bf16[256,512]{1,0:T(8,128)(2,1)S(1)}, u32[]{:S(2)}, u32[]{:S(2)}) collective-permute-start(bf16[256,512]{1,0:T(8,128)(2,1)S(1)} %collective-permute-done.6.refs_5_), channel_id=1, source_target_pairs={{8,0},{16,8},{24,16},{28,24},{20,28},{12,20},{4,12},{0,4},{9,1},{1... | collective-permute-start | bytes 786440 | tf_op jit(solution)/shard_map/ppermute | solution.py:338
  59.1 11.2 %collective-permute-start.12 = (bf16[256,512]{1,0:T(8,128)(2,1)S(1)}, bf16[256,512]{1,0:T(8,128)(2,1)S(1)}, u32[]{:S(2)}, u32[]{:S(2)}) collective-permute-start(bf16[256,512]{1,0:T(8,128)(2,1)S(1)} %collective-permute-done.8.refs_7_), channel_id=1, source_target_pairs={{8,0},{16,8},{24,16},{28,24},{20,28},{12,20},{4,12},{0,4},{9,1},{1... | collective-permute-start | bytes 786440 | tf_op jit(solution)/shard_map/ppermute | solution.py:338
  61.0 12.2 %collective-permute-start.13 = (bf16[256,512]{1,0:T(8,128)(2,1)S(1)}, bf16[256,512]{1,0:T(8,128)(2,1)S(1)}, u32[]{:S(2)}, u32[]{:S(2)}) collective-permute-start(bf16[256,512]{1,0:T(8,128)(2,1)S(1)} %collective-permute-done.9.refs_8_), channel_id=1, source_target_pairs={{0,8},{8,16},{16,24},{24,28},{28,20},{20,12},{12,4},{4,0},{1,9},{9... | collective-permute-start | bytes 786440 | tf_op jit(solution)/shard_map/ppermute | solution.py:338
  62.0 11.2 %collective-permute-start.15 = (bf16[256,512]{1,0:T(8,128)(2,1)S(1)}, bf16[256,512]{1,0:T(8,128)(2,1)S(1)}, u32[]{:S(2)}, u32[]{:S(2)}) collective-permute-start(bf16[256,512]{1,0:T(8,128)(2,1)S(1)} %collective-permute-done.11.refs_10_), channel_id=1, source_target_pairs={{0,8},{8,16},{16,24},{24,28},{28,20},{20,12},{12,4},{4,0},{1,9},{9... | collective-permute-start | bytes 786440 | tf_op jit(solution)/shard_map/ppermute | solution.py:338
  64.8 11.2 %collective-permute-start.14 = (bf16[256,512]{1,0:T(8,128)(2,1)S(1)}, bf16[256,512]{1,0:T(8,128)(2,1)S(1)}, u32[]{:S(2)}, u32[]{:S(2)}) collective-permute-start(bf16[256,512]{1,0:T(8,128)(2,1)S(1)} %collective-permute-done.10.refs_9_), channel_id=1, source_target_pairs={{8,0},{16,8},{24,16},{28,24},{20,28},{12,20},{4,12},{0,4},{9,1},{1... | collective-permute-start | bytes 786440 | tf_op jit(solution)/shard_map/ppermute | solution.py:338
  70.4 10.9 %collective-permute-start.19 = (bf16[4,256,256]{2,1,0:T(8,128)(2,1)S(1)}, bf16[4,256,256]{2,1,0:T(8,128)(2,1)S(1)}, u32[]{:S(2)}, u32[]{:S(2)}) collective-permute-start(bf16[4,256,256]{2,1,0:T(8,128)(2,1)S(1)} %pad_maximum_fusion), channel_id=1, source_target_pairs={{0,2},{4,6},{9,11},{13,15},{18,16},{22,20},{27,25},{31,29}} | collective-permute-start | bytes 1572872 | tf_op jit(solution)/shard_map/ppermute | solution.py:310
  73.1 5.9 %collective-permute-start.16 = (bf16[256,512]{1,0:T(8,128)(2,1)S(1)}, bf16[256,512]{1,0:T(8,128)(2,1)S(1)}, u32[]{:S(2)}, u32[]{:S(2)}) collective-permute-start(bf16[256,512]{1,0:T(8,128)(2,1)S(1)} %collective-permute-done.15.refs_14_), channel_id=1, source_target_pairs={{0,8},{8,16},{16,24},{24,28},{28,20},{20,12},{12,4},{4,0},{1,9},{9... | collective-permute-start | bytes 786440 | tf_op jit(solution)/shard_map/ppermute | solution.py:338
  79.1 4.4 %collective-permute-start.21 = (bf16[5,256,256]{2,1,0:T(8,128)(2,1)S(1)}, bf16[5,256,256]{2,1,0:T(8,128)(2,1)S(1)}, u32[]{:S(2)}, u32[]{:S(2)}) collective-permute-start(bf16[5,256,256]{2,1,0:T(8,128)(2,1)S(1)} %bitcast_dynamic-update-slice_fusion), channel_id=1, source_target_pairs={{0,2},{4,6},{9,11},{13,15},{18,16},{22,20},{27,25},{31,29}} | collective-permute-start | bytes 1966088 | tf_op jit(solution)/shard_map/ppermute | solution.py:310
  80.0 12.9 %collective-permute-start.18 = (bf16[7,256,256]{2,1,0:T(8,128)(2,1)S(1)}, bf16[7,256,256]{2,1,0:T(8,128)(2,1)S(1)}, u32[]{:S(2)}, u32[]{:S(2)}) collective-permute-start(bf16[7,256,256]{2,1,0:T(8,128)(2,1)S(1)} %broadcast_select_fusion), channel_id=1, source_target_pairs={{0,1},{2,3},{4,5},{6,7},{9,8},{11,10},{13,12},{15,14},{18,19},{16,... | collective-permute-start | bytes 2752520 | tf_op jit(solution)/shard_map/ppermute | solution.py:310
  82.2 8.8 %collective-permute-start.20 = (bf16[4,256,256]{2,1,0:T(8,128)(2,1)}, bf16[4,256,256]{2,1,0:T(8,128)(2,1)}, u32[]{:S(2)}, u32[]{:S(2)}) collective-permute-start(bf16[4,256,256]{2,1,0:T(8,128)(2,1)} %broadcast_select_fusion.4), channel_id=1, source_target_pairs={{0,1},{2,3},{4,5},{6,7},{9,8},{11,10},{13,12},{15,14},{18,19},{16,... | collective-permute-start | bytes 1572872 | tf_op jit(solution)/shard_map/ppermute | solution.py:310
  83.5 16.0 %collective-permute-start.22 = (bf16[5,256,256]{2,1,0:T(8,128)(2,1)S(1)}, bf16[5,256,256]{2,1,0:T(8,128)(2,1)}, u32[]{:S(2)}, u32[]{:S(2)}) collective-permute-start(bf16[5,256,256]{2,1,0:T(8,128)(2,1)S(1)} %broadcast_select_fusion.2), channel_id=1, source_target_pairs={{0,1},{2,3},{4,5},{6,7},{9,8},{11,10},{13,12},{15,14},{18,19},{16,... | collective-permute-start | bytes 1966088 | tf_op jit(solution)/shard_map/ppermute | solution.py:310
  (16 other events, 190.7 us)

commit v5 on v4

--- a/solution.py
+++ b/solution.py
@@ -165,7 +165,7 @@
 
 def spectra_edge(last, left, own, right, first, second, tables):
     channels, own_time = own.shape
-    rows = min(2 * LANE, channels)
+    rows = min(4 * LANE, channels)
     edge = 2 * LANE
     across = lambda i: (0, i)
     line = lambda i: (i, 0)
@@ -198,24 +198,26 @@
     )(last, left, own, own, right, first, second, jnp.asarray(window_table()), high, low, high, low)
 
 
-def correlate_kernel(pieces, batches, rows, pitch, batch, *refs):
+def correlate_kernel(pieces, batches, rows, pitch, steps, *refs):
     row_refs = refs[:pieces]
     col_refs = refs[pieces : pieces + batches]
-    table_ref, out_ref, lhs_ref, cross_ref = refs[pieces + batches :]
+    table_ref, out_ref, lhs_ref, even_ref, odd_ref = refs[pieces + batches :]
     width = out_ref.shape[1]
     depth = 2 * GROUP * pieces
-    sub = lax.rem(pl.program_id(0), LANE // rows)
-
-    @pl.when(sub == 0)
+    step = pl.program_id(0)
+    sub = lax.rem(step, LANE // rows)
+    parity = lax.rem(step, 2)
+    start = pl.multiple_of(sub * rows, rows)
+
+    @pl.when((sub == 0) & (step < steps))
     def _():
         for g in range(GROUPS):
             part = jnp.concatenate([r[16 * g : 16 * g + 16, :] for r in row_refs], axis=0)
             lhs_ref[:, g * depth : (g + 1) * depth] = part.T
 
-    lane = lax.broadcasted_iota(jnp.int32, (rows, depth), 1)
-    freq = lax.rem(lane, 2 * GROUP) // 2
-    start = pl.multiple_of(sub * rows, rows)
-    for g in range(GROUPS):
+    def cross_spectra(g, cross_ref):
+        lane = lax.broadcasted_iota(jnp.int32, (rows, depth), 1)
+        freq = lax.rem(lane, 2 * GROUP) // 2
         cols = jnp.concatenate(
             [r[d, 16 * g : 16 * g + 16, :] for r in col_refs for d in range(r.shape[0])], axis=0
         )
@@ -230,44 +232,53 @@
                 cross_ref[h, base : base + rows, :] = cross[
                     q * rows : (q + 1) * rows, h * LANE : (h + 1) * LANE
                 ]
-    table = table_ref[...]
-
-    def lags(b, carry):
+
+    def lags(begin, count, cross_ref):
         highs, lows = [], []
-        for ii in range(batch):
+        for i in range(begin, begin + count):
             for h in range(width // LANE):
-                by_freq = cross_ref[h, pl.ds(b * batch + ii, NBIN, stride=pitch), :]
-                high, low = split(by_freq.T)
+                high, low = split(cross_ref[h, pl.ds(i, NBIN, stride=pitch), :].T)
                 highs.append(high)
                 lows.append(low)
         lhs = jnp.concatenate([jnp.concatenate(highs, axis=0), jnp.concatenate(lows, axis=0)], axis=1)
-        both = jnp.dot(lhs, table, preferred_element_type=f32)
+        both = jnp.dot(lhs, table_ref[...], preferred_element_type=f32)
         out = both[:, :LAGS] + both[:, LAGS:]
-        out_ref[pl.ds(b * batch, batch)] = out.reshape(batch, width, LAGS)
-        return carry
-
-    lax.fori_loop(0, rows // batch, lags, 0, unroll=2)
+        out_ref[begin : begin + count] = out.reshape(count, width, LAGS)
+
+    def run(into, source):
+        quarter = GROUPS // 4
+        for part in range(4):
+            if into is not None:
+                for g in range(part * quarter, (part + 1) * quarter):
+                    cross_spectra(g, into)
+            if source is not None:
+                lags(part * (rows // 4), rows // 4, source)
+
+    inside = (step > 0) & (step < steps)
+    pl.when(step == 0)(lambda: run(even_ref, None))
+    pl.when(inside & (parity == 0))(lambda: run(even_ref, odd_ref))
+    pl.when(inside & (parity == 1))(lambda: run(odd_ref, even_ref))
+    pl.when(step == steps)(lambda: run(None, odd_ref if steps % 2 == 0 else even_ref))
 
 
 def correlate(row_pieces, col_batches, table):
     pieces = len(row_pieces)
     channels = row_pieces[0].shape[1]
     width = col_batches[0].shape[2]
-    rows, batch = 64, 32
+    rows = 64
     pitch = rows + 8
     per = LANE // rows
+    steps = channels // rows
     return pl.pallas_call(
-        functools.partial(correlate_kernel, pieces, len(col_batches), rows, pitch, batch),
-        grid=(channels // rows,),
-        in_specs=[pl.BlockSpec((SPEC, LANE), lambda s: (0, s // per))] * pieces
-        + [pl.BlockSpec(c.shape, lambda s: (0, 0, 0)) for c in col_batches]
+        functools.partial(correlate_kernel, pieces, len(col_batches), rows, pitch, steps),
+        grid=(steps + 1,),
+        in_specs=[pl.BlockSpec((SPEC, LANE), lambda s: (0, jnp.minimum(s, steps - 1) // per))] * pieces
+        + [pl.BlockSpec(c.shape, lambda s: (0, 0, 0), pipeline_mode=pl.Buffered(1)) for c in col_batches]
         + [pl.BlockSpec((2 * NBIN, 2 * LAGS), lambda s: (0, 0))],
-        out_specs=pl.BlockSpec((rows, width, LAGS), lambda s: (s, 0, 0)),
+        out_specs=pl.BlockSpec((rows, width, LAGS), lambda s: (jnp.maximum(s - 1, 0), 0, 0)),
         out_shape=jax.ShapeDtypeStruct((channels, width, LAGS), f32),
-        scratch_shapes=[
-            pltpu.VMEM((LANE, SPEC * pieces), bf16),
-            pltpu.VMEM((width // LANE, NBIN * pitch, LANE), f32),
-        ],
+        scratch_shapes=[pltpu.VMEM((LANE, SPEC * pieces), bf16)]
+        + [pltpu.VMEM((width // LANE, NBIN * pitch, LANE), f32)] * 2,
         compiler_params=pltpu.CompilerParams(vmem_limit_bytes=56 << 20),
         name="correlate",
         cost_estimate=pl.CostEstimate(

time: 139 us -> 138 us (level)
  no operation moved by 1% of the time
where the time goes in v5:
time: 138 us; the launch traced here: 137 us
  waiting for transfers between devices  50.6 us (37%)
  Pallas kernels  48.9 us (35%)
  starting transfers between devices  27 us (20%)
  other arithmetic  7.24 us (5%)
  local copies, waits for them, and re-layouts  2.89 us (2%)
    pallas_call x1, Pallas kernels, correlate(): pl.pallas_call(functools.partial(correlate_kernel, pieces, len(col_batche...  35.8 us
    ppermute x14, waiting for transfers between devices, shards(): moved = lax.ppermute(moved, 'seg', pairs)  27.9 us
    ppermute x14, starting transfers between devices, shards(): moved = lax.ppermute(moved, 'seg', pairs)  14.3 us
    ppermute x6, waiting for transfers between devices, partner(): cols = jnp.where(held, cols, lax.ppermute(cols, ('seg', 'blk'), pairs))  11.5 us
    ppermute x1, waiting for transfers between devices, shards(): following = lax.ppermute(first, 'seg', downward)  11.1 us
    ppermute x6, starting transfers between devices, partner(): cols = jnp.where(held, cols, lax.ppermute(cols, ('seg', 'blk'), pairs))  6.15 us
    select_n x6, other arithmetic, partner(): cols = jnp.where(held, cols, lax.ppermute(cols, ('seg', 'blk'), pairs))  6.01 us
    pallas_call x1, Pallas kernels, spectra_inner(): pl.pallas_call(inner_kernel, grid=(channels // rows,), in_specs=[pl.Block...  5.99 us
  transfers between devices with their start and end apart: 23, of which 14 were waited for; matrix products, arithmetic and copies ran while one was open for 5% of the time, Pallas kernels for 4%

profile of v5, /device:TPU:3, one launch (start us, length us, event | category | flops | bytes accessed | tf_op | source)
XLA Modules:
  0.0 137.2 jit_solution(2695585233462023216)
XLA Ops:
  0.0 3.3 %response.1 = (bf16[1280,256]{1,0:T(8,128)(2,1)}, bf16[1280,256]{1,0:T(8,128)(2,1)}) custom-call(f32[64]{0:T(128)} %taps_ref.1, f32[576,256]{1,0:T(8,128)} %constant.101.clone.table_ref), custom_call_target="tpu_custom_call" | custom-call | flops 213909504 | bytes 2097152 | tf_op jit(solution)/shard_map/response/pallas_call | solution.py:82
  5.6 4.0 %collective-permute-start = (bf16[512,128]{1,0:T(8,128)(2,1)S(1)}, bf16[512,128]{1,0:T(8,128)(2,1)S(1)}, u32[]{:S(2)}, u32[]{:S(2)}) collective-permute-start(bf16[512,128]{1,0:T(8,128)(2,1)S(1)} %get-tuple-element.32), channel_id=1, source_target_pairs={{0,4},{4,8},{8,12},{12,16},{16,20},{20,24},{24,28},{1,5},{5,9},{9,... | collective-permute-start | bytes 393224 | tf_op jit(solution)/shard_map/ppermute | solution.py:333
  9.6 6.0 %spectra_inner.1 = (f32[256,512]{1,0:T(8,128)}, f32[256,512]{1,0:T(8,128)}) custom-call(bf16[512,2048]{1,0:T(8,128)(2,1)} %end_ref.1, bf16[512,256]{1,0:T(8,128)(2,1)} %constant.102.clone.window_ref, bf16[1280,256]{1,0:T(8,128)(2,1)} %get-tuple-element.21.high_ref.high0_ref.high1_ref, bf16[1280,256]{1,0:T(8,128)(2,1)} %get-tuple-element.22.low_ref.low0_ref.low1_ref), custom_call_target="tpu_custom_call" | custom-call | flops 2013265920 | bytes 6291456 | tf_op jit(solution)/shard_map/spectra_inner/pallas_call | solution.py:130
  16.3 3.9 %spectra_edge.1 = (f32[256,512]{1,0:T(8,128)}, bf16[256,512]{1,0:T(8,128)(2,1)}, f32[256,512]{1,0:T(8,128)}) custom-call(s32[1]{0:T(128)} %bitcast.last_ref, bf16[512,128]{1,0:T(8,128)(2,1)} %copy-done.2, bf16[512,2048]{1,0:T(8,128)(2,1)} %end_ref.1, bf16[512,2048]{1,0:T(8,128)(2,1)} %end_ref.1, bf16[512,128]{1,0:T(8,128)(2,1)} %copy-done.1, ...), custom_call_target="tpu_custom_call" | custom-call | flops 603979776 | bytes 4194304 | tf_op jit(solution)/shard_map/spectra_edge/pallas_call | solution.py:173
  21.4 2.8 %collective-permute-start.3 = (bf16[256,512]{1,0:T(8,128)(2,1)}, bf16[256,512]{1,0:T(8,128)(2,1)S(1)}, u32[]{:S(2)}, u32[]{:S(2)}) collective-permute-start(bf16[256,512]{1,0:T(8,128)(2,1)} %get-tuple-element.30.refs_0_), channel_id=1, source_target_pairs={{8,0},{16,8},{24,16},{28,24},{20,28},{12,20},{4,12},{0,4},{9,1},{1... | collective-permute-start | bytes 786440 | tf_op jit(solution)/shard_map/ppermute | solution.py:349
  24.3 11.1 %collective-permute-done.2 = f32[256,512]{1,0:T(8,128)S(1)} collective-permute-done((f32[256,512]{1,0:T(8,128)}, f32[256,512]{1,0:T(8,128)S(1)}, u32[]{:S(2)}, u32[]{:S(2)}) %collective-permute-start.2) | collective-permute-done | bytes 524320 | tf_op jit(solution)/shard_map/ppermute | solution.py:338
  37.9 4.1 %collective-permute-done.3.refs_2_ = bf16[256,512]{1,0:T(8,128)(2,1)S(1)} collective-permute-done((bf16[256,512]{1,0:T(8,128)(2,1)}, bf16[256,512]{1,0:T(8,128)(2,1)S(1)}, u32[]{:S(2)}, u32[]{:S(2)}) %collective-permute-start.3) | collective-permute-done | bytes 262176 | tf_op jit(solution)/shard_map/ppermute | solution.py:349
  45.6 2.1 %collective-permute-done.4.refs_3_ = bf16[256,512]{1,0:T(8,128)(2,1)S(1)} collective-permute-done((bf16[256,512]{1,0:T(8,128)(2,1)S(1)}, bf16[256,512]{1,0:T(8,128)(2,1)S(1)}, u32[]{:S(2)}, u32[]{:S(2)}) %collective-permute-start.4) | collective-permute-done | bytes 262176 | tf_op jit(solution)/shard_map/ppermute | solution.py:349
  47.7 1.8 %collective-permute-start.8 = (bf16[256,512]{1,0:T(8,128)(2,1)S(1)}, bf16[256,512]{1,0:T(8,128)(2,1)S(1)}, u32[]{:S(2)}, u32[]{:S(2)}) collective-permute-start(bf16[256,512]{1,0:T(8,128)(2,1)S(1)} %collective-permute-done.4.refs_3_), channel_id=1, source_target_pairs={{8,0},{16,8},{24,16},{28,24},{20,28},{12,20},{4,12},{0,4},{9,1},{1... | collective-permute-start | bytes 786440 | tf_op jit(solution)/shard_map/ppermute | solution.py:349
  51.3 2.0 %collective-permute-done.6.refs_5_ = bf16[256,512]{1,0:T(8,128)(2,1)S(1)} collective-permute-done((bf16[256,512]{1,0:T(8,128)(2,1)S(1)}, bf16[256,512]{1,0:T(8,128)(2,1)S(1)}, u32[]{:S(2)}, u32[]{:S(2)}) %collective-permute-start.6) | collective-permute-done | bytes 262176 | tf_op jit(solution)/shard_map/ppermute | solution.py:349
  54.1 1.9 %collective-permute-start.10 = (bf16[256,512]{1,0:T(8,128)(2,1)S(1)}, bf16[256,512]{1,0:T(8,128)(2,1)S(1)}, u32[]{:S(2)}, u32[]{:S(2)}) collective-permute-start(bf16[256,512]{1,0:T(8,128)(2,1)S(1)} %collective-permute-done.6.refs_5_), channel_id=1, source_target_pairs={{8,0},{16,8},{24,16},{28,24},{20,28},{12,20},{4,12},{0,4},{9,1},{1... | collective-permute-start | bytes 786440 | tf_op jit(solution)/shard_map/ppermute | solution.py:349
  55.9 3.0 %collective-permute-done.8.refs_7_ = bf16[256,512]{1,0:T(8,128)(2,1)S(1)} collective-permute-done((bf16[256,512]{1,0:T(8,128)(2,1)S(1)}, bf16[256,512]{1,0:T(8,128)(2,1)S(1)}, u32[]{:S(2)}, u32[]{:S(2)}) %collective-permute-start.8) | collective-permute-done | bytes 262176 | tf_op jit(solution)/shard_map/ppermute | solution.py:349
  58.9 1.9 %collective-permute-start.12 = (bf16[256,512]{1,0:T(8,128)(2,1)S(1)}, bf16[256,512]{1,0:T(8,128)(2,1)S(1)}, u32[]{:S(2)}, u32[]{:S(2)}) collective-permute-start(bf16[256,512]{1,0:T(8,128)(2,1)S(1)} %collective-permute-done.8.refs_7_), channel_id=1, source_target_pairs={{8,0},{16,8},{24,16},{28,24},{20,28},{12,20},{4,12},{0,4},{9,1},{1... | collective-permute-start | bytes 786440 | tf_op jit(solution)/shard_map/ppermute | solution.py:349
  61.8 2.7 %collective-permute-done.10.refs_9_ = bf16[256,512]{1,0:T(8,128)(2,1)S(1)} collective-permute-done((bf16[256,512]{1,0:T(8,128)(2,1)S(1)}, bf16[256,512]{1,0:T(8,128)(2,1)S(1)}, u32[]{:S(2)}, u32[]{:S(2)}) %collective-permute-start.10) | collective-permute-done | bytes 262176 | tf_op jit(solution)/shard_map/ppermute | solution.py:349
  64.6 1.9 %collective-permute-start.14 = (bf16[256,512]{1,0:T(8,128)(2,1)S(1)}, bf16[256,512]{1,0:T(8,128)(2,1)S(1)}, u32[]{:S(2)}, u32[]{:S(2)}) collective-permute-start(bf16[256,512]{1,0:T(8,128)(2,1)S(1)} %collective-permute-done.10.refs_9_), channel_id=1, source_target_pairs={{8,0},{16,8},{24,16},{28,24},{20,28},{12,20},{4,12},{0,4},{9,1},{1... | collective-permute-start | bytes 786440 | tf_op jit(solution)/shard_map/ppermute | solution.py:349
  66.5 3.6 %collective-permute-done.12.refs_11_ = bf16[256,512]{1,0:T(8,128)(2,1)S(1)} collective-permute-done((bf16[256,512]{1,0:T(8,128)(2,1)S(1)}, bf16[256,512]{1,0:T(8,128)(2,1)S(1)}, u32[]{:S(2)}, u32[]{:S(2)}) %collective-permute-start.12) | collective-permute-done | bytes 262176 | tf_op jit(solution)/shard_map/ppermute | solution.py:349
  70.8 2.1 %collective-permute-done.15.refs_14_ = bf16[256,512]{1,0:T(8,128)(2,1)S(1)} collective-permute-done((bf16[256,512]{1,0:T(8,128)(2,1)S(1)}, bf16[256,512]{1,0:T(8,128)(2,1)S(1)}, u32[]{:S(2)}, u32[]{:S(2)}) %collective-permute-start.15) | collective-permute-done | bytes 262176 | tf_op jit(solution)/shard_map/ppermute | solution.py:349
  73.1 2.7 %collective-permute-done.14.refs_13_ = bf16[256,512]{1,0:T(8,128)(2,1)S(1)} collective-permute-done((bf16[256,512]{1,0:T(8,128)(2,1)S(1)}, bf16[256,512]{1,0:T(8,128)(2,1)S(1)}, u32[]{:S(2)}, u32[]{:S(2)}) %collective-permute-start.14) | collective-permute-done | bytes 262176 | tf_op jit(solution)/shard_map/ppermute | solution.py:349
  75.8 3.0 %collective-permute-done.16.refs_15_ = bf16[256,512]{1,0:T(8,128)(2,1)S(1)} collective-permute-done((bf16[256,512]{1,0:T(8,128)(2,1)S(1)}, bf16[256,512]{1,0:T(8,128)(2,1)S(1)}, u32[]{:S(2)}, u32[]{:S(2)}) %collective-permute-start.16) | collective-permute-done | bytes 262176 | tf_op jit(solution)/shard_map/ppermute | solution.py:349
  84.8 5.9 %collective-permute-done.20 = bf16[4,256,256]{2,1,0:T(8,128)(2,1)} collective-permute-done((bf16[4,256,256]{2,1,0:T(8,128)(2,1)}, bf16[4,256,256]{2,1,0:T(8,128)(2,1)}, u32[]{:S(2)}, u32[]{:S(2)}) %collective-permute-start.20) | collective-permute-done | bytes 524320 | tf_op jit(solution)/shard_map/ppermute | solution.py:321
  90.8 1.9 %broadcast_select_fusion.5.refs_17_ = bf16[4,256,256]{2,1,0:T(8,128)(2,1)} fusion(bf16[4,256,256]{2,1,0:T(8,128)(2,1)} %collective-permute-done.20, pred[]{:T(512)S(6)} %eq.34, bf16[4,256,256]{2,1,0:T(8,128)(2,1)S(1)} %collective-permute-done.19, bf16[1,256,256]{2,1,0:T(8,128)(2,1)S(1)} %dynamic-slice_bitcast_fusion, ...), kind=kLoop, calls=%fused_computation.7 | loop fusion | flops 1310720 | bytes 2097154 | tf_op jit(solution)/shard_map/jit(_where)/select_n | solution.py:321
  93.7 5.6 %collective-permute-done.22 = bf16[5,256,256]{2,1,0:T(8,128)(2,1)} collective-permute-done((bf16[5,256,256]{2,1,0:T(8,128)(2,1)S(1)}, bf16[5,256,256]{2,1,0:T(8,128)(2,1)}, u32[]{:S(2)}, u32[]{:S(2)}) %collective-permute-start.22) | collective-permute-done | bytes 655392 | tf_op jit(solution)/shard_map/ppermute | solution.py:321
  99.3 2.0 %broadcast_select_fusion.3.refs_18_ = bf16[5,256,256]{2,1,0:T(8,128)(2,1)} fusion(bf16[5,256,256]{2,1,0:T(8,128)(2,1)S(1)} %broadcast_select_fusion.2, bf16[5,256,256]{2,1,0:T(8,128)(2,1)} %collective-permute-done.22, pred[]{:T(512)S(6)} %eq.34), kind=kLoop, calls=%fused_computation.3 | loop fusion | flops 327680 | bytes 1966081 | tf_op jit(solution)/shard_map/jit(_where)/select_n | solution.py:321
  101.3 35.8 %correlate.1 = f32[512,256,128]{2,1,0:T(8,128)} custom-call(bf16[256,512]{1,0:T(8,128)(2,1)} %get-tuple-element.30.refs_0_, bf16[256,512]{1,0:T(8,128)(2,1)} %copy-done, bf16[256,512]{1,0:T(8,128)(2,1)} %copy-done.3, bf16[256,512]{1,0:T(8,128)(2,1)} %copy-done.5, bf16[256,512]{1,0:T(8,128)(2,1)} %copy-done.6, bf16[256,512]{1,0:T(8,128)(2,1)} %copy-done.7, ...), custom_call_target="tpu_custom_call" | custom-call | flops 25769803776 | bytes 67108864 | tf_op jit(solution)/shard_map/correlate/pallas_call | solution.py:272
  (86 shorter events, 21.6 us)
Async XLA Ops:
  4.3 11.3 %collective-permute-start.1 = (bf16[512,128]{1,0:T(8,128)(2,1)S(1)}, bf16[512,128]{1,0:T(8,128)(2,1)S(1)}, u32[]{:S(2)}, u32[]{:S(2)}) collective-permute-start(bf16[512,128]{1,0:T(8,128)(2,1)S(1)} %get-tuple-element.31), channel_id=1, source_target_pairs={{4,0},{8,4},{12,8},{16,12},{20,16},{24,20},{28,24},{5,1},{9,5},{13... | collective-permute-start | bytes 393224 | tf_op jit(solution)/shard_map/ppermute | solution.py:334
  5.6 10.0 %collective-permute-start = (bf16[512,128]{1,0:T(8,128)(2,1)S(1)}, bf16[512,128]{1,0:T(8,128)(2,1)S(1)}, u32[]{:S(2)}, u32[]{:S(2)}) collective-permute-start(bf16[512,128]{1,0:T(8,128)(2,1)S(1)} %get-tuple-element.32), channel_id=1, source_target_pairs={{0,4},{4,8},{8,12},{12,16},{16,20},{20,24},{24,28},{1,5},{5,9},{9,... | collective-permute-start | bytes 393224 | tf_op jit(solution)/shard_map/ppermute | solution.py:333
  20.2 15.2 %collective-permute-start.2 = (f32[256,512]{1,0:T(8,128)}, f32[256,512]{1,0:T(8,128)S(1)}, u32[]{:S(2)}, u32[]{:S(2)}) collective-permute-start(f32[256,512]{1,0:T(8,128)} %get-tuple-element.27), channel_id=1, source_target_pairs={{4,0},{8,4},{12,8},{16,12},{20,16},{24,20},{28,24},{5,1},{9,5},{13... | collective-permute-start | bytes 1572872 | tf_op jit(solution)/shard_map/ppermute | solution.py:338
  21.4 20.5 %collective-permute-start.3 = (bf16[256,512]{1,0:T(8,128)(2,1)}, bf16[256,512]{1,0:T(8,128)(2,1)S(1)}, u32[]{:S(2)}, u32[]{:S(2)}) collective-permute-start(bf16[256,512]{1,0:T(8,128)(2,1)} %get-tuple-element.30.refs_0_), channel_id=1, source_target_pairs={{8,0},{16,8},{24,16},{28,24},{20,28},{12,20},{4,12},{0,4},{9,1},{1... | collective-permute-start | bytes 786440 | tf_op jit(solution)/shard_map/ppermute | solution.py:349
  36.6 36.5 %copy-start = (bf16[256,512]{1,0:T(8,128)(2,1)}, bf16[256,512]{1,0:T(8,128)(2,1)S(1)}, u32[]{:S(2)}) copy-start(bf16[256,512]{1,0:T(8,128)(2,1)S(1)} %add_convert_fusion.refs_1_) | copy-start | bytes 786436
  36.6 14.6 %collective-permute-start.7 = (bf16[256,512]{1,0:T(8,128)(2,1)S(1)}, bf16[256,512]{1,0:T(8,128)(2,1)S(1)}, u32[]{:S(2)}, u32[]{:S(2)}) collective-permute-start(bf16[256,512]{1,0:T(8,128)(2,1)S(1)} %add_convert_fusion.refs_1_), channel_id=1, source_target_pairs={{0,8},{8,16},{16,24},{24,28},{28,20},{20,12},{12,4},{4,0},{1,9},{9... | collective-permute-start | bytes 786440 | tf_op jit(solution)/shard_map/ppermute | solution.py:349
  42.0 5.7 %collective-permute-start.4 = (bf16[256,512]{1,0:T(8,128)(2,1)S(1)}, bf16[256,512]{1,0:T(8,128)(2,1)S(1)}, u32[]{:S(2)}, u32[]{:S(2)}) collective-permute-start(bf16[256,512]{1,0:T(8,128)(2,1)S(1)} %collective-permute-done.3.refs_2_), channel_id=1, source_target_pairs={{8,0},{16,8},{24,16},{28,24},{20,28},{12,20},{4,12},{0,4},{9,1},{1... | collective-permute-start | bytes 786440 | tf_op jit(solution)/shard_map/ppermute | solution.py:349
  43.1 8.1 %collective-permute-start.5 = (bf16[256,512]{1,0:T(8,128)(2,1)}, bf16[256,512]{1,0:T(8,128)(2,1)S(1)}, u32[]{:S(2)}, u32[]{:S(2)}) collective-permute-start(bf16[256,512]{1,0:T(8,128)(2,1)} %get-tuple-element.30.refs_0_), channel_id=1, source_target_pairs={{0,8},{8,16},{16,24},{24,28},{28,20},{20,12},{12,4},{4,0},{1,9},{9... | collective-permute-start | bytes 786440 | tf_op jit(solution)/shard_map/ppermute | solution.py:349
  44.4 8.9 %collective-permute-start.6 = (bf16[256,512]{1,0:T(8,128)(2,1)S(1)}, bf16[256,512]{1,0:T(8,128)(2,1)S(1)}, u32[]{:S(2)}, u32[]{:S(2)}) collective-permute-start(bf16[256,512]{1,0:T(8,128)(2,1)S(1)} %add_convert_fusion.refs_1_), channel_id=1, source_target_pairs={{8,0},{16,8},{24,16},{28,24},{20,28},{12,20},{4,12},{0,4},{9,1},{1... | collective-permute-start | bytes 786440 | tf_op jit(solution)/shard_map/ppermute | solution.py:349
  47.7 11.2 %collective-permute-start.8 = (bf16[256,512]{1,0:T(8,128)(2,1)S(1)}, bf16[256,512]{1,0:T(8,128)(2,1)S(1)}, u32[]{:S(2)}, u32[]{:S(2)}) collective-permute-start(bf16[256,512]{1,0:T(8,128)(2,1)S(1)} %collective-permute-done.4.refs_3_), channel_id=1, source_target_pairs={{8,0},{16,8},{24,16},{28,24},{20,28},{12,20},{4,12},{0,4},{9,1},{1... | collective-permute-start | bytes 786440 | tf_op jit(solution)/shard_map/ppermute | solution.py:349
  51.1 9.6 %collective-permute-start.9 = (bf16[256,512]{1,0:T(8,128)(2,1)S(1)}, bf16[256,512]{1,0:T(8,128)(2,1)S(1)}, u32[]{:S(2)}, u32[]{:S(2)}) collective-permute-start(bf16[256,512]{1,0:T(8,128)(2,1)S(1)} %collective-permute-done.5.refs_4_), channel_id=1, source_target_pairs={{0,8},{8,16},{16,24},{24,28},{28,20},{20,12},{12,4},{4,0},{1,9},{9... | collective-permute-start | bytes 786440 | tf_op jit(solution)/shard_map/ppermute | solution.py:349
  51.2 10.6 %collective-permute-start.11 = (bf16[256,512]{1,0:T(8,128)(2,1)S(1)}, bf16[256,512]{1,0:T(8,128)(2,1)S(1)}, u32[]{:S(2)}, u32[]{:S(2)}) collective-permute-start(bf16[256,512]{1,0:T(8,128)(2,1)S(1)} %collective-permute-done.7.refs_6_), channel_id=1, source_target_pairs={{0,8},{8,16},{16,24},{24,28},{28,20},{20,12},{12,4},{4,0},{1,9},{9... | collective-permute-start | bytes 786440 | tf_op jit(solution)/shard_map/ppermute | solution.py:349
  53.3 26.3 %collective-permute-start.17 = (bf16[7,256,256]{2,1,0:T(8,128)(2,1)S(1)}, bf16[7,256,256]{2,1,0:T(8,128)(2,1)S(1)}, u32[]{:S(2)}, u32[]{:S(2)}) collective-permute-start(bf16[7,256,256]{2,1,0:T(8,128)(2,1)S(1)} %bitcast_dynamic-update-slice_fusion.5), channel_id=1, source_target_pairs={{0,2},{4,6},{9,11},{13,15},{18,16},{22,20},{27,25},{31,29}} | collective-permute-start | bytes 2752520 | tf_op jit(solution)/shard_map/ppermute | solution.py:321
  54.1 10.5 %collective-permute-start.10 = (bf16[256,512]{1,0:T(8,128)(2,1)S(1)}, bf16[256,512]{1,0:T(8,128)(2,1)S(1)}, u32[]{:S(2)}, u32[]{:S(2)}) collective-permute-start(bf16[256,512]{1,0:T(8,128)(2,1)S(1)} %collective-permute-done.6.refs_5_), channel_id=1, source_target_pairs={{8,0},{16,8},{24,16},{28,24},{20,28},{12,20},{4,12},{0,4},{9,1},{1... | collective-permute-start | bytes 786440 | tf_op jit(solution)/shard_map/ppermute | solution.py:349
  58.9 11.2 %collective-permute-start.12 = (bf16[256,512]{1,0:T(8,128)(2,1)S(1)}, bf16[256,512]{1,0:T(8,128)(2,1)S(1)}, u32[]{:S(2)}, u32[]{:S(2)}) collective-permute-start(bf16[256,512]{1,0:T(8,128)(2,1)S(1)} %collective-permute-done.8.refs_7_), channel_id=1, source_target_pairs={{8,0},{16,8},{24,16},{28,24},{20,28},{12,20},{4,12},{0,4},{9,1},{1... | collective-permute-start | bytes 786440 | tf_op jit(solution)/shard_map/ppermute | solution.py:349
  60.8 12.2 %collective-permute-start.13 = (bf16[256,512]{1,0:T(8,128)(2,1)S(1)}, bf16[256,512]{1,0:T(8,128)(2,1)S(1)}, u32[]{:S(2)}, u32[]{:S(2)}) collective-permute-start(bf16[256,512]{1,0:T(8,128)(2,1)S(1)} %collective-permute-done.9.refs_8_), channel_id=1, source_target_pairs={{0,8},{8,16},{16,24},{24,28},{28,20},{20,12},{12,4},{4,0},{1,9},{9... | collective-permute-start | bytes 786440 | tf_op jit(solution)/shard_map/ppermute | solution.py:349
  61.7 11.2 %collective-permute-start.15 = (bf16[256,512]{1,0:T(8,128)(2,1)S(1)}, bf16[256,512]{1,0:T(8,128)(2,1)S(1)}, u32[]{:S(2)}, u32[]{:S(2)}) collective-permute-start(bf16[256,512]{1,0:T(8,128)(2,1)S(1)} %collective-permute-done.11.refs_10_), channel_id=1, source_target_pairs={{0,8},{8,16},{16,24},{24,28},{28,20},{20,12},{12,4},{4,0},{1,9},{9... | collective-permute-start | bytes 786440 | tf_op jit(solution)/shard_map/ppermute | solution.py:349
  64.6 11.2 %collective-permute-start.14 = (bf16[256,512]{1,0:T(8,128)(2,1)S(1)}, bf16[256,512]{1,0:T(8,128)(2,1)S(1)}, u32[]{:S(2)}, u32[]{:S(2)}) collective-permute-start(bf16[256,512]{1,0:T(8,128)(2,1)S(1)} %collective-permute-done.10.refs_9_), channel_id=1, source_target_pairs={{8,0},{16,8},{24,16},{28,24},{20,28},{12,20},{4,12},{0,4},{9,1},{1... | collective-permute-start | bytes 786440 | tf_op jit(solution)/shard_map/ppermute | solution.py:349
  70.1 10.9 %collective-permute-start.19 = (bf16[4,256,256]{2,1,0:T(8,128)(2,1)S(1)}, bf16[4,256,256]{2,1,0:T(8,128)(2,1)S(1)}, u32[]{:S(2)}, u32[]{:S(2)}) collective-permute-start(bf16[4,256,256]{2,1,0:T(8,128)(2,1)S(1)} %pad_maximum_fusion), channel_id=1, source_target_pairs={{0,2},{4,6},{9,11},{13,15},{18,16},{22,20},{27,25},{31,29}} | collective-permute-start | bytes 1572872 | tf_op jit(solution)/shard_map/ppermute | solution.py:321
  72.9 5.9 %collective-permute-start.16 = (bf16[256,512]{1,0:T(8,128)(2,1)S(1)}, bf16[256,512]{1,0:T(8,128)(2,1)S(1)}, u32[]{:S(2)}, u32[]{:S(2)}) collective-permute-start(bf16[256,512]{1,0:T(8,128)(2,1)S(1)} %collective-permute-done.15.refs_14_), channel_id=1, source_target_pairs={{0,8},{8,16},{16,24},{24,28},{28,20},{20,12},{12,4},{4,0},{1,9},{9... | collective-permute-start | bytes 786440 | tf_op jit(solution)/shard_map/ppermute | solution.py:349
  78.9 4.4 %collective-permute-start.21 = (bf16[5,256,256]{2,1,0:T(8,128)(2,1)S(1)}, bf16[5,256,256]{2,1,0:T(8,128)(2,1)S(1)}, u32[]{:S(2)}, u32[]{:S(2)}) collective-permute-start(bf16[5,256,256]{2,1,0:T(8,128)(2,1)S(1)} %bitcast_dynamic-update-slice_fusion), channel_id=1, source_target_pairs={{0,2},{4,6},{9,11},{13,15},{18,16},{22,20},{27,25},{31,29}} | collective-permute-start | bytes 1966088 | tf_op jit(solution)/shard_map/ppermute | solution.py:321
  79.8 12.9 %collective-permute-start.18 = (bf16[7,256,256]{2,1,0:T(8,128)(2,1)S(1)}, bf16[7,256,256]{2,1,0:T(8,128)(2,1)S(1)}, u32[]{:S(2)}, u32[]{:S(2)}) collective-permute-start(bf16[7,256,256]{2,1,0:T(8,128)(2,1)S(1)} %broadcast_select_fusion), channel_id=1, source_target_pairs={{0,1},{2,3},{4,5},{6,7},{9,8},{11,10},{13,12},{15,14},{18,19},{16,... | collective-permute-start | bytes 2752520 | tf_op jit(solution)/shard_map/ppermute | solution.py:321
  81.9 8.8 %collective-permute-start.20 = (bf16[4,256,256]{2,1,0:T(8,128)(2,1)}, bf16[4,256,256]{2,1,0:T(8,128)(2,1)}, u32[]{:S(2)}, u32[]{:S(2)}) collective-permute-start(bf16[4,256,256]{2,1,0:T(8,128)(2,1)} %broadcast_select_fusion.4), channel_id=1, source_target_pairs={{0,1},{2,3},{4,5},{6,7},{9,8},{11,10},{13,12},{15,14},{18,19},{16,... | collective-permute-start | bytes 1572872 | tf_op jit(solution)/shard_map/ppermute | solution.py:321
  83.3 16.0 %collective-permute-start.22 = (bf16[5,256,256]{2,1,0:T(8,128)(2,1)S(1)}, bf16[5,256,256]{2,1,0:T(8,128)(2,1)}, u32[]{:S(2)}, u32[]{:S(2)}) collective-permute-start(bf16[5,256,256]{2,1,0:T(8,128)(2,1)S(1)} %broadcast_select_fusion.2), channel_id=1, source_target_pairs={{0,1},{2,3},{4,5},{6,7},{9,8},{11,10},{13,12},{15,14},{18,19},{16,... | collective-permute-start | bytes 1966088 | tf_op jit(solution)/shard_map/ppermute | solution.py:321
  (16 other events, 190.7 us)
